TPU v7x, 32 devices: a whole 2x2x4 slice. The times are simulated.
32 devices in a mesh: dp: 4 (over y, x), tensor: 2 (over core), expert: 4 (over z).
Axes of the slice: x: 2, y: 2, z: 4, core: 2. Of those that a mesh axis runs over, the one named last changes fastest.
Arguments:
- tokens: bfloat16 [2048, 2304], P(('dp', 'tensor', 'expert')), may hold values from -6 to 6
- routes: int32 [2048, 2], P(('dp', 'tensor', 'expert')), may hold values from 0 to 7, all different within a row; in each aligned block of 64 rows (0 to 63, 64 to 127, ...) at most 24 rows name the same one
- gates: float32 [2048, 2], P(('dp', 'tensor', 'expert')), may hold values from 0.2 to 1
- segments: int32 [2048], P(('dp', 'tensor', 'expert')), may hold values from 0 to 7, never falling along the last dimension, each value on 1 to 512 neighbouring positions
- w_gate: bfloat16 [8, 2304, 7680], P('expert', None, ('dp', 'tensor')), may hold values from -0.125 to 0.125
- w_up: bfloat16 [8, 2304, 7680], P('expert', None, ('dp', 'tensor')), may hold values from -0.125 to 0.125
- w_down: bfloat16 [8, 7680, 2304], P('expert', ('dp', 'tensor')), may hold values from -0.0625 to 0.0625
Outputs:
- embedded: bfloat16 [2048, 2304], P(('dp', 'tensor', 'expert'))
- pooled: float32 [8, 2304], replicated
Inputs may be any that keep to these rules, and one draw needn't show every extreme that they name: `routes`: each residue names two different experts. Within the rows of one device no expert is named more than 24 times, and in every draw some expert is named exactly 24 times by the rows of some device. `segments`: sequence numbers never fall along the residues; each sequence has 1 to 512 residues and one has exactly 512.
All inputs are finite; a program needn't handle non-finite values.
Results may differ from a plain program's by a relative error of at most 0.0085.
Values may be sent and summed in bfloat16 or wider, within the bound.
No kernel may reach another device: no remote copies, remote signals or barrier semaphores. Data moves between devices by JAX's collectives and lax.ppermute only.
A program may use at most 128 MiB of HBM per device.

v0:
```python
import jax
import jax.numpy as jnp
from jax import lax
from jax.sharding import PartitionSpec as P

EXPERTS = 8
TOP = 2
CAP = 24


epsilon = 1e-06


def norm_tokens(tokens):
    values = tokens.astype(jnp.float32)
    scale = lax.rsqrt(jnp.mean(values * values, axis=1, keepdims=True) + epsilon)
    return (values, (values * scale).astype(jnp.bfloat16))


def slot_numbers(routes):
    flat_routes = routes.reshape(-1)
    onehot = (flat_routes[:, None] == jnp.arange(EXPERTS, dtype=jnp.int32)[None, :]).astype(
        jnp.int32
    )
    before = jnp.cumsum(onehot, axis=0) - onehot
    slot_rank = jnp.sum(before * onehot, axis=1)
    return flat_routes * CAP + slot_rank


def placement_matrix(slot_index, tok_count):
    hits = (jnp.arange(EXPERTS * CAP, dtype=jnp.int32)[:, None] == slot_index[None, :]).astype(
        jnp.int32
    )
    return jnp.sum(hits.reshape(EXPERTS * CAP, tok_count, TOP), axis=2).astype(jnp.bfloat16)


def fan_out(slot_rows, replicas):
    leading = slot_rows.shape[:-2]
    features = slot_rows.shape[-1]
    shaped = slot_rows.reshape(leading + (EXPERTS, CAP, features))
    if replicas > 1:
        shaped = jnp.repeat(shaped, replicas, axis=len(leading))
    return shaped.reshape(leading + (EXPERTS * replicas * CAP, features))


def expert_hidden(row_block, w_gate, w_up):
    gate_proj = jnp.einsum("nacd,adf->nacf", row_block, w_gate, preferred_element_type=jnp.float32)
    up_proj = jnp.einsum("nacd,adf->nacf", row_block, w_up, preferred_element_type=jnp.float32)
    return (jax.nn.silu(gate_proj) * up_proj).astype(jnp.bfloat16)


def shards(tokens, routes, gates, segments, w_gate, w_up, w_down):
    tok_count = tokens.shape[0]
    width = tokens.shape[1]
    experts_axis = lax.axis_size("expert")
    per_device = w_gate.shape[0]
    replicas = max(1, experts_axis // EXPERTS)
    plane = lax.axis_size("dp") * lax.axis_size("tensor")
    values, normed = norm_tokens(tokens)
    slot_index = slot_numbers(routes)
    placing = placement_matrix(slot_index, tok_count)
    slot_rows = jnp.dot(placing, normed, preferred_element_type=jnp.float32).astype(jnp.bfloat16)
    send_rows = fan_out(slot_rows, replicas)
    received = lax.all_to_all(send_rows, "expert", split_axis=0, concat_axis=0, tiled=True)
    local_rows = received.reshape(experts_axis, per_device, CAP, width)
    hidden = expert_hidden(
        lax.all_gather(local_rows, ("dp", "tensor"), axis=0, tiled=True), w_gate, w_up
    )
    summed = lax.psum_scatter(
        jnp.einsum("nacf,afd->nacd", hidden, w_down, preferred_element_type=jnp.float32).astype(
            jnp.bfloat16
        ),
        ("dp", "tensor"),
        scatter_dimension=0,
        tiled=True,
    )
    returned = lax.all_to_all(summed, "expert", split_axis=0, concat_axis=0, tiled=True).astype(
        jnp.float32
    )
    if replicas > 1:
        expert_out = jnp.sum(returned.reshape(EXPERTS, replicas, CAP, width), axis=1)
    else:
        expert_out = returned.reshape(EXPERTS, CAP, width)
    picked = jnp.take(expert_out.reshape(EXPERTS * CAP, width), slot_index, axis=0).reshape(
        tok_count, TOP, width
    )
    mixed = values + jnp.sum(gates[:, :, None] * picked, axis=1)
    embedded = mixed.astype(jnp.bfloat16)
    devices_all = plane * experts_axis
    seq_total = tok_count * devices_all // 256
    seq_hot = (jnp.arange(seq_total, dtype=jnp.int32)[:, None] == segments[None, :]).astype(
        jnp.bfloat16
    )
    seq_sums = jnp.dot(seq_hot, embedded, preferred_element_type=jnp.float32)
    seq_counts = jnp.sum(seq_hot.astype(jnp.float32), axis=1)
    total_sums, total_counts = lax.psum((seq_sums, seq_counts), ("dp", "tensor", "expert"))
    pooled = total_sums / total_counts[:, None]
    return (embedded, pooled)


def solution(mesh):
    placed = (
        P(("dp", "tensor", "expert"), None),
        P(("dp", "tensor", "expert"), None),
        P(("dp", "tensor", "expert"), None),
        P(("dp", "tensor", "expert")),
        P("expert", None, ("dp", "tensor")),
        P("expert", None, ("dp", "tensor")),
        P("expert", ("dp", "tensor"), None),
    )
    return jax.shard_map(
        shards,
        mesh=mesh,
        in_specs=placed,
        out_specs=(P(("dp", "tensor", "expert"), None), P()),
        check_vma=False,
    )
```

profile of v0, /device:TPU:0, one launch (start us, length us, event | category | flops | bytes accessed | tf_op | source)
XLA Modules:
  0.0 399.8 jit_solution(3369024853161112235)
XLA Ops:
  7.2 0.8 copy.29
  8.8 0.7 compare_and_fusion
  9.6 1.1 fusion.14
  10.7 1.4 convolution_convert_fusion
  12.1 28.3 %all_to_all.14 = bf16[4,48,2304]{2,1,0:T(8,128)(2,1)S(1)} all-to-all(bf16[4,48,2304]{2,1,0:T(8,128)(2,1)S(1)} %bitcast.60), channel_id=1, replica_groups=mesh['dp'=4,'tensor'=2,'expert'=4] {'expert'}, dimensions={0} | all-to-all | bytes 1769472 | tf_op jit(solution)/shard_map/all_to_all | solution.py:64
  40.5 1.0 copy.32
  41.5 48.1 %all-gather.2.cloned.1.call-done = bf16[32,2,24,2304]{3,2,0,1:T(8,128)(2,1)} async-done(((bf16[4,2,24,2304]{3,2,0,1:T(8,128)(2,1)}), bf16[32,2,24,2304]{3,2,0,1:T(8,128)(2,1)}) %all-gather.2.cloned.1.call-update) | async-done | bytes 7077904 | tf_op jit(solution)/shard_map/all_gather | solution.py:67
  89.6 11.1 %fusion.2 = f32[2,32,24,960]{3,2,1,0:T(8,128)S(1)} fusion(bf16[32,2,24,2304]{3,2,0,1:T(8,128)(2,1)} %all-gather.2.cloned.1.call-done, bf16[2,2304,960]{1,2,0:T(8,128)(2,1)} %param.12), kind=kOutput, calls=%fused_computation.3 | convolution fusion | flops 6794772480 | bytes 21823488 | tf_op jit(solution)/shard_map/nacd,adf->nacf/dot_general | solution.py:48
  100.6 13.1 %fusion.8 = bf16[32,2,24,960]{3,2,0,1:T(8,128)(2,1)S(1)} fusion(f32[2,32,24,960]{3,2,1,0:T(8,128)S(1)} %fusion.2, bf16[32,2,24,2304]{3,2,0,1:T(8,128)(2,1)} %all-gather.2.cloned.1.call-done, bf16[2,2304,960]{1,2,0:T(8,128)(2,1)} %param.11), kind=kOutput, calls=%fused_computation.9 | convolution fusion | flops 6803619840 | bytes 24772608 | tf_op jit(solution)/shard_map/nacd,adf->nacf/dot_general | solution.py:47
  113.7 12.9 %convert_bitcast_fusion = bf16[32,2,24,2304]{3,2,0,1:T(8,128)(2,1)} fusion(bf16[32,2,24,960]{3,2,0,1:T(8,128)(2,1)S(1)} %fusion.8, bf16[2,960,2304]{2,1,0:T(8,128)(2,1)} %param.13), kind=kOutput, calls=%fused_computation.7 | convolution fusion | flops 6798311424 | bytes 18874368 | tf_op jit(solution)/shard_map/nacf,afd->nacd/dot_general | solution.py:70
  126.6 0.6 copy-done.5
  127.2 0.6 dynamic-slice
  128.5 111.2 %all-reduce.6.cloned.1.call-done = bf16[32,2,24,2304]{3,2,0,1:T(8,128)(2,1)} async-done(((bf16[32,2,24,2304]{3,2,0,1:T(8,128)(2,1)}), bf16[32,2,24,2304]{3,2,0,1:T(8,128)(2,1)}) %all-reduce.6.cloned.1.call-update) | async-done | bytes 7077904
  239.6 1.2 constant_dynamic-slice_fusion
  240.9 1.0 copy.33
  241.8 4.6 %all-to-all-start.1 = ((bf16[4,2,24,2304]{3,2,1,0:T(8,128)(2,1)}), bf16[4,2,24,2304]{3,2,1,0:T(8,128)(2,1)S(1)}, u32[]{:S(2)}, u32[]{:S(2)}) async-start(bf16[4,2,24,2304]{3,2,1,0:T(8,128)(2,1)} %copy.33), calls=%async_computation.1 | async-start | bytes 1769472 | tf_op jit(solution)/shard_map/all_to_all | solution.py:77
  246.9 21.6 %all-to-all-done.1 = bf16[4,2,24,2304]{3,2,1,0:T(8,128)(2,1)S(1)} async-done(((bf16[4,2,24,2304]{3,2,1,0:T(8,128)(2,1)}), bf16[4,2,24,2304]{3,2,1,0:T(8,128)(2,1)S(1)}, u32[]{:S(2)}, u32[]{:S(2)}) %all-to-all-start.1) | async-done | bytes 884768 | tf_op jit(solution)/shard_map/all_to_all | solution.py:77
  268.7 1.1 gather_fusion
  269.8 0.7 gather.7
  270.5 3.2 multiply_reduce_fusion
  273.8 0.8 fusion.22
  274.7 37.3 %psum.15 = f32[8]{0:T(128)S(1)} all-reduce(f32[8]{0:T(128)S(1)} %convert_reduce_fusion.1), channel_id=1, replica_groups=mesh['dp'=4,'tensor'=2,'expert'=4] {'dp','tensor','expert'}, use_global_device_ids=true, to_apply=%region_8.9 | all-reduce | flops 8 | bytes 64 | tf_op jit(solution)/shard_map/psum | solution.py:96
  312.0 79.6 %all-reduce.4.cloned.1.call-done = f32[8,2304]{1,0:T(8,128)} async-done(((f32[8,2304]{1,0:T(8,128)}), f32[8,2304]{1,0:T(8,128)}) %all-reduce.4.cloned.1.call-update) | async-done | bytes 73744 | tf_op jit(solution)/shard_map/psum | solution.py:96
  391.7 1.6 broadcast_divide_fusion
  (35 shorter events, 1.8 us)
Async XLA Ops:
  7.2 82.4 %all-gather.2.cloned.1.call-start = ((), (), s32[]{:S(2)}) async-start(), calls=%async_computation.2 | async-start | bytes 7962624 | tf_op jit(solution)/shard_map/all_gather | solution.py:67
  41.5 198.2 %all-reduce.6.cloned.1.call-start = ((), (), s32[]{:S(2)}) async-start(), calls=%async_computation.4 | async-start | bytes 14155776
  126.6 0.7 copy-start.5
  126.6 119.9 %copy-start.2 = (s32[64,2]{0,1:T(2,128)S(1)}, s32[64,2]{0,1:T(2,128)}, u32[]{:S(2)}) copy-start(s32[64,2]{0,1:T(2,128)} %param.8) | copy-start | bytes 1540
  126.6 120.2 %copy-start.3 = (f32[64,2]{0,1:T(2,128)S(1)}, f32[64,2]{0,1:T(2,128)}, u32[]{:S(2)}) copy-start(f32[64,2]{0,1:T(2,128)} %param.9) | copy-start | bytes 1540
  241.8 26.7 %all-to-all-start.1 = ((bf16[4,2,24,2304]{3,2,1,0:T(8,128)(2,1)}), bf16[4,2,24,2304]{3,2,1,0:T(8,128)(2,1)S(1)}, u32[]{:S(2)}, u32[]{:S(2)}) async-start(bf16[4,2,24,2304]{3,2,1,0:T(8,128)(2,1)} %copy.33), calls=%async_computation.1 | async-start | bytes 1769472 | tf_op jit(solution)/shard_map/all_to_all | solution.py:77
  246.4 145.2 %all-reduce.4.cloned.1.call-start = ((), (), s32[]{:S(2)}) async-start(), calls=%async_computation.3 | async-start | bytes 147456 | tf_op jit(solution)/shard_map/psum | solution.py:96
  268.7 5.0 %copy-start = (bf16[64,2304]{1,0:T(8,128)(2,1)S(1)}, bf16[64,2304]{1,0:T(8,128)(2,1)}, u32[]{:S(2)}) copy-start(bf16[64,2304]{1,0:T(8,128)(2,1)} %param.7) | copy-start | bytes 884740
  268.7 5.1 %copy-start.4 = (s32[64]{0:T(128)S(1)}, s32[64]{0:T(128)}, u32[]{:S(2)}) copy-start(s32[64]{0:T(128)} %param.10) | copy-start | bytes 772
  273.8 119.5 %copy-start.1 = (bf16[64,2304]{1,0:T(8,128)(2,1)}, bf16[64,2304]{1,0:T(8,128)(2,1)S(1)}, u32[]{:S(2)}) copy-start(bf16[64,2304]{1,0:T(8,128)(2,1)S(1)} %fusion.16) | copy-start | bytes 884740
Sparse Core Ops, SparseCore 0:
  41.6 47.9 all-gather.1
  126.7 112.8 all-reduce.5
  274.7 116.8 all-reduce.3
where the time goes:
time: 402 us; the launch traced here: 400 us
  waiting for transfers between devices  261 us (65%)
  blocking collectives  65.6 us (16%)
  matrix products  39.2 us (10%)
  between operations  14.6 us (4%)
  local copies, waits for them, and re-layouts  7.73 us (2%)
  other arithmetic  7.49 us (2%)
  starting transfers between devices  4.68 us (1%)
    unnamed x4, waiting for transfers between devices  111 us
    psum x1, waiting for transfers between devices, shards(): lax.psum((seq_sums, seq_counts), ('dp', 'tensor', 'expert'))  79.6 us
    all_gather x1, waiting for transfers between devices, shards(): lax.all_gather(local_rows, ('dp', 'tensor'), axis=0, tiled=True)  48.1 us
    psum x1, blocking collectives, shards(): lax.psum((seq_sums, seq_counts), ('dp', 'tensor', 'expert'))  37.3 us
    all_to_all x1, blocking collectives, shards(): lax.all_to_all(send_rows, 'expert', split_axis=0, concat_axis=0, tiled=True)  28.3 us
    all_to_all x1, waiting for transfers between devices, shards(): lax.all_to_all(summed, 'expert', split_axis=0, concat_axis=0, tiled=True)  21.6 us
    dot_general x1, matrix products, expert_hidden(): jnp.einsum('nacd,adf->nacf', row_block, w_gate, preferred_element_type=jn...  13.1 us
    dot_general x1, matrix products, shards(): jnp.einsum('nacf,afd->nacd', hidden, w_down, preferred_element_type=jnp.f...  12.9 us
  transfers between devices with their start and end apart: 4, of which 4 were waited for; matrix products, arithmetic and copies ran while one was open for 0% of the time, Pallas kernels for 0%

commit v1 on v0

v1 whole, which is shorter than its diff:
```python
import functools

import jax
import jax.numpy as jnp
from jax import lax
from jax.experimental import pallas as pl
from jax.experimental.pallas import tpu as pltpu
from jax.sharding import PartitionSpec as P

EXPERTS = 8
TOP = 2
CAP = 24
LANES = 128
AXES = ("dp", "tensor", "expert")


epsilon = 1e-06


def xor_steps(size):
    return size & (size - 1) == 0


def swap(x, d=0, t=0, z=0, turned=None):
    sizes = [lax.axis_size(name) for name in AXES]
    pairs = []
    for i in range(sizes[0]):
        for j in range(sizes[1]):
            for k in range(sizes[2]):
                flip = d if turned is None or j % 2 == 0 else turned
                here = (i * sizes[1] + j) * sizes[2] + k
                there = ((i ^ flip) * sizes[1] + (j ^ t)) * sizes[2] + (k ^ z)
                pairs.append((here, there))
    return lax.ppermute(x, AXES, pairs)


def prep_kernel(seqs, planes, pos, tokens, routes, gates, seg_row, seg_col, own, other, weights, sums):
    tok_count, width = tokens.shape
    slots = 2 * planes * CAP
    t, z = pos[0], pos[1]
    raw = tokens[...]
    values = raw.astype(jnp.float32)
    scale = lax.rsqrt(jnp.mean(values * values, axis=1, keepdims=True) + epsilon)
    normed = (values * scale).astype(jnp.bfloat16)

    expert = lax.broadcasted_iota(jnp.int32, (EXPERTS, tok_count), 0)
    hot = [expert == routes[k : k + 1, :] for k in range(TOP)]
    named = (hot[0] | hot[1]).astype(jnp.bfloat16)
    earlier = (
        lax.broadcasted_iota(jnp.int32, (tok_count, tok_count), 0)
        < lax.broadcasted_iota(jnp.int32, (tok_count, tok_count), 1)
    ).astype(jnp.bfloat16)
    before = jnp.dot(named, earlier, preferred_element_type=jnp.float32)

    row = lax.broadcasted_iota(jnp.int32, (slots, tok_count), 0)
    group = row // CAP
    rank = row - group * CAP
    row_expert = 2 * (z ^ (group % planes)) + (t ^ (group // planes))
    place = jnp.zeros((slots, tok_count), jnp.float32)
    weight = jnp.zeros((slots, tok_count), jnp.float32)
    for k in range(TOP):
        own_rank = jnp.sum(jnp.where(hot[k], before, 0.0), axis=0, keepdims=True).astype(jnp.int32)
        hit = (row_expert == routes[k : k + 1, :]) & (rank == own_rank)
        place = place + jnp.where(hit, 1.0, 0.0)
        weight = weight + jnp.where(hit, gates[k : k + 1, :], 0.0)
    weights[...] = weight

    rows = jnp.dot(place.astype(jnp.bfloat16), normed, preferred_element_type=jnp.float32).astype(jnp.bfloat16)
    high = weight.astype(jnp.bfloat16)
    low = (weight - high.astype(jnp.float32)).astype(jnp.bfloat16)
    lane = lax.broadcasted_iota(jnp.int32, (tok_count, LANES), 1)
    member = (lane == seg_col[...]).astype(jnp.bfloat16)
    member_low = (lane == seg_col[...] + seqs).astype(jnp.bfloat16)
    marks = (
        jnp.dot(high, member, preferred_element_type=jnp.float32)
        + jnp.dot(low, member_low, preferred_element_type=jnp.float32)
    ).astype(jnp.bfloat16)
    half = planes * CAP
    own[:, :width] = rows[:half]
    own[:, width:] = marks[:half]
    other[:, :width] = rows[half:]
    other[:, width:] = marks[half:]

    seq_hot = lax.broadcasted_iota(jnp.int32, (seqs, tok_count), 0) == seg_row[...]
    sums[:, :width] = jnp.dot(seq_hot.astype(jnp.bfloat16), raw, preferred_element_type=jnp.float32)
    counts = jnp.sum(seq_hot.astype(jnp.float32), axis=1, keepdims=True)
    sums[:, width:] = jnp.broadcast_to(counts, (seqs, LANES))


def prep(pos, tokens, routes, gates, segments, seqs, planes):
    tok_count, width = tokens.shape
    half = planes * CAP
    vmem = pl.BlockSpec(memory_space=pltpu.VMEM)
    return pl.pallas_call(
        functools.partial(prep_kernel, seqs, planes),
        out_shape=(
            jax.ShapeDtypeStruct((half, width + LANES), jnp.bfloat16),
            jax.ShapeDtypeStruct((half, width + LANES), jnp.bfloat16),
            jax.ShapeDtypeStruct((2 * half, tok_count), jnp.float32),
            jax.ShapeDtypeStruct((seqs, width + LANES), jnp.float32),
        ),
        in_specs=[pl.BlockSpec(memory_space=pltpu.SMEM)] + [vmem] * 5,
        out_specs=(vmem,) * 4,
        name="prep",
    )(pos, tokens, routes.T, gates.T, segments[None, :], segments[:, None])


def ffn_kernel(pieces, tile, cols, pos, *refs):
    parts = refs[:pieces]
    gate_own, up_own, down_own, gate_far, up_far, down_far = refs[pieces : pieces + 6]
    outs = refs[pieces + 6 : 2 * pieces + 6]
    rows_buf, gate_buf, up_buf, down_buf, hidden, row_sem, in_sem, out_sem = refs[2 * pieces + 6 :]
    t = pos[0]
    size, width = parts[0].shape
    units = down_far.shape[0]
    row_copies = [
        pltpu.make_async_copy(parts[i], rows_buf.at[pl.ds(i * size, size)], row_sem.at[i]) for i in range(pieces)
    ]
    for copy in row_copies:
        copy.start()
    sources = [(gate_own.at[t], up_own.at[t], down_own.at[t]), (gate_far, up_far, down_far)]
    spans = [(start, min(tile, units - start)) for start in range(0, units, tile)]
    in_copies = []
    for h in range(2):
        for j, (start, length) in enumerate(spans):
            here = pl.ds(start, length)
            pair = [
                pltpu.make_async_copy(sources[h][m].at[here], buf.at[h, here], in_sem.at[m, h * len(spans) + j])
                for m, buf in enumerate((gate_buf, up_buf))
            ]
            for copy in pair:
                copy.start()
            in_copies.append(pair)
    down_copies = []
    for h in range(2):
        copy = pltpu.make_async_copy(sources[h][2], down_buf.at[pl.ds(h * units, units)], out_sem.at[h])
        copy.start()
        down_copies.append(copy)
    for copy in row_copies:
        copy.wait()
    x = rows_buf[...]
    nt = (((1,), (1,)), ((), ()))
    for h in range(2):
        for j, (start, length) in enumerate(spans):
            for copy in in_copies[h * len(spans) + j]:
                copy.wait()
            here = pl.ds(start, length)
            g = lax.dot_general(x, gate_buf[h, here], nt, preferred_element_type=jnp.float32)
            u = lax.dot_general(x, up_buf[h, here], nt, preferred_element_type=jnp.float32)
            value = g / (1.0 + jnp.exp(-g)) * u
            hidden[:, h * units + start : h * units + start + length] = value.astype(jnp.bfloat16)
    for copy in down_copies:
        copy.wait()
    for start in range(0, width, cols):
        length = min(cols, width - start)
        y = jnp.dot(hidden[...], down_buf[:, start : start + length], preferred_element_type=jnp.float32)
        for i in range(pieces):
            outs[i][:, start : start + length] = y[i * size : (i + 1) * size].astype(jnp.bfloat16)


def ffn(pos, parts, weights):
    pieces = len(parts)
    size, width = parts[0].shape
    units = weights[5].shape[0]
    tile, cols = 320, 768
    tiles = 2 * -(-units // tile)
    anywhere = pl.BlockSpec(memory_space=pl.ANY)
    vmem = pl.BlockSpec(memory_space=pltpu.VMEM)
    return pl.pallas_call(
        functools.partial(ffn_kernel, pieces, tile, cols),
        out_shape=(jax.ShapeDtypeStruct((size, width), jnp.bfloat16),) * pieces,
        in_specs=[pl.BlockSpec(memory_space=pltpu.SMEM)] + [anywhere] * (pieces + 6),
        out_specs=(vmem,) * pieces,
        scratch_shapes=[
            pltpu.VMEM((pieces * size, width), jnp.bfloat16),
            pltpu.VMEM((2, units, width), jnp.bfloat16),
            pltpu.VMEM((2, units, width), jnp.bfloat16),
            pltpu.VMEM((2 * units, width), jnp.bfloat16),
            pltpu.VMEM((pieces * size, 2 * units), jnp.bfloat16),
            pltpu.SemaphoreType.DMA((pieces,)),
            pltpu.SemaphoreType.DMA((2, tiles)),
            pltpu.SemaphoreType.DMA((2,)),
        ],
        compiler_params=pltpu.CompilerParams(vmem_limit_bytes=44 << 20),
        cost_estimate=pl.CostEstimate(
            flops=12 * pieces * size * width * units, transcendentals=2 * pieces * size * units,
            bytes_accessed=12 * units * width,
        ),
        name="ffn",
    )(pos, *parts, *weights)


def combine_kernel(tokens, first, second, weights, out):
    weight = weights[...].T
    high = weight.astype(jnp.bfloat16)
    low = (weight - high.astype(jnp.float32)).astype(jnp.bfloat16)
    half = first.shape[0]
    total = tokens[...].astype(jnp.float32)
    mixed = jnp.zeros_like(total)
    for part in (low, high):
        mixed = mixed + jnp.dot(part[:, :half], first[...], preferred_element_type=jnp.float32)
        mixed = mixed + jnp.dot(part[:, half:], second[...], preferred_element_type=jnp.float32)
    out[...] = (total + mixed).astype(jnp.bfloat16)


def combine(tokens, first, second, weights):
    vmem = pl.BlockSpec(memory_space=pltpu.VMEM)
    return pl.pallas_call(
        combine_kernel,
        out_shape=jax.ShapeDtypeStruct(tokens.shape, jnp.bfloat16),
        in_specs=[vmem] * 4,
        out_specs=vmem,
        name="combine",
    )(tokens, first, second, weights)


def added(*arrays):
    total = arrays[0].astype(jnp.float32)
    for array in arrays[1:]:
        total = total + array.astype(jnp.float32)
    return total.astype(jnp.bfloat16)


def core_shards(tokens, routes, gates, segments, w_gate, w_up, w_down):
    tok_count, width = tokens.shape
    planes = lax.axis_size("expert")
    devices_all = lax.axis_size("dp") * lax.axis_size("tensor") * planes
    seqs = tok_count * devices_all // 256
    t, z = lax.axis_index("tensor"), lax.axis_index("expert")
    pos = jnp.stack([t, z]).astype(jnp.int32)

    own, other, weights, sums = prep(pos, tokens, routes, gates, segments, seqs, planes)
    sibling = swap(other, t=1)

    stored = (jnp.swapaxes(w_gate, 1, 2), jnp.swapaxes(w_up, 1, 2), w_down)
    far = tuple(swap(lax.dynamic_index_in_dim(w, 1 - t, 0, keepdims=False), t=1) for w in stored)

    chunks = []
    for source in (own, sibling):
        blocks = [source[c * CAP : (c + 1) * CAP] for c in range(planes)]
        arrived = [blocks[0]] + [swap(blocks[c], z=c) for c in range(1, planes)]
        whole = jnp.concatenate(arrived, axis=0)
        rows, marks = whole[:, :width], whole[:, width:]
        near = swap(rows, d=1, turned=2)
        side = swap(rows, d=2, turned=1)
        across = swap(near, d=2, turned=1)
        chunks.append((marks, (rows, near, side, across)))

    returned = []
    pool = sums
    for marks, parts in chunks:
        mine, to_near, to_side, to_across = ffn(pos, parts, stored + far)
        passed = added(to_near, swap(to_across, d=2, turned=1))
        done = added(mine, swap(to_side, d=2, turned=1), swap(passed, d=1, turned=2))
        shares = lax.dot_general(
            marks[:, : 2 * seqs], done, (((0,), (0,)), ((), ())), preferred_element_type=jnp.float32
        )
        shares = shares[:seqs] + shares[seqs:]
        pool = pool + jnp.pad(shares, ((0, 0), (0, LANES)))
        blocks = [done[c * CAP : (c + 1) * CAP] for c in range(planes)]
        back = [blocks[0]] + [swap(blocks[c], z=c) for c in range(1, planes)]
        returned.append(jnp.concatenate(back, axis=0))

    second = swap(returned[1], t=1)
    embedded = combine(tokens, returned[0], second, weights)

    pool = pool + swap(pool, t=1)
    for axis in ("d", "z"):
        step = 1
        while step < lax.axis_size({"d": "dp", "z": "expert"}[axis]):
            pool = pool + swap(pool, **{axis: step})
            step *= 2
    pooled = pool[:, :width] / pool[:, width : width + 1]
    return (embedded, pooled)


def slot_numbers(routes):
    flat_routes = routes.reshape(-1)
    pairs = flat_routes.shape[0]
    same = flat_routes[:, None] == flat_routes[None, :]
    earlier = jnp.arange(pairs)[None, :] < jnp.arange(pairs)[:, None]
    slot_rank = jnp.sum((same & earlier).astype(jnp.int32), axis=1)
    return flat_routes * CAP + slot_rank


def shards(tokens, routes, gates, segments, w_gate, w_up, w_down):
    tok_count, width = tokens.shape
    experts_axis = lax.axis_size("expert")
    per_device = w_gate.shape[0]
    replicas = max(1, experts_axis // EXPERTS)
    plane = lax.axis_size("dp") * lax.axis_size("tensor")
    values = tokens.astype(jnp.float32)
    scale = lax.rsqrt(jnp.mean(values * values, axis=1, keepdims=True) + epsilon)
    normed = (values * scale).astype(jnp.bfloat16)
    slot_index = slot_numbers(routes)
    hits = jnp.arange(EXPERTS * CAP, dtype=jnp.int32)[:, None] == slot_index[None, :]
    placing = jnp.sum(hits.astype(jnp.int32).reshape(EXPERTS * CAP, tok_count, TOP), axis=2)
    slot_rows = jnp.dot(placing.astype(jnp.bfloat16), normed, preferred_element_type=jnp.float32)
    shaped = slot_rows.astype(jnp.bfloat16).reshape(EXPERTS, CAP, width)
    if replicas > 1:
        shaped = jnp.repeat(shaped, replicas, axis=0)
    send_rows = shaped.reshape(EXPERTS * replicas * CAP, width)
    received = lax.all_to_all(send_rows, "expert", split_axis=0, concat_axis=0, tiled=True)
    local_rows = received.reshape(experts_axis, per_device, CAP, width)
    block = lax.all_gather(local_rows, ("dp", "tensor"), axis=0, tiled=True)
    gate_proj = jnp.einsum("nacd,adf->nacf", block, w_gate, preferred_element_type=jnp.float32)
    up_proj = jnp.einsum("nacd,adf->nacf", block, w_up, preferred_element_type=jnp.float32)
    hidden = (jax.nn.silu(gate_proj) * up_proj).astype(jnp.bfloat16)
    summed = lax.psum_scatter(
        jnp.einsum("nacf,afd->nacd", hidden, w_down, preferred_element_type=jnp.float32).astype(jnp.bfloat16),
        ("dp", "tensor"),
        scatter_dimension=0,
        tiled=True,
    )
    returned = lax.all_to_all(summed, "expert", split_axis=0, concat_axis=0, tiled=True).astype(jnp.float32)
    expert_out = jnp.sum(returned.reshape(EXPERTS, replicas, CAP, width), axis=1)
    picked = jnp.take(expert_out.reshape(EXPERTS * CAP, width), slot_index, axis=0).reshape(tok_count, TOP, width)
    embedded = (values + jnp.sum(gates[:, :, None] * picked, axis=1)).astype(jnp.bfloat16)
    seq_total = tok_count * plane * experts_axis // 256
    seq_hot = jnp.arange(seq_total, dtype=jnp.int32)[:, None] == segments[None, :]
    seq_sums = jnp.dot(seq_hot.astype(jnp.bfloat16), embedded, preferred_element_type=jnp.float32)
    seq_counts = jnp.sum(seq_hot.astype(jnp.float32), axis=1)
    total_sums, total_counts = lax.psum((seq_sums, seq_counts), AXES)
    return (embedded, total_sums / total_counts[:, None])


def solution(mesh):
    placed = (
        P(AXES, None),
        P(AXES, None),
        P(AXES, None),
        P(AXES),
        P("expert", None, ("dp", "tensor")),
        P("expert", None, ("dp", "tensor")),
        P("expert", ("dp", "tensor"), None),
    )
    dp, tensor, planes = (mesh.shape[name] for name in AXES)
    paired = dp == 4 and tensor == 2 and EXPERTS == tensor * planes and xor_steps(planes)
    return jax.shard_map(
        core_shards if paired else shards,
        mesh=mesh,
        in_specs=placed,
        out_specs=(P(AXES, None), P()),
        check_vma=False,
    )
```

time: 402 us -> 172 us (0.43)
  waiting for transfers between devices: 261 us -> 61.1 us
  blocking collectives: 65.6 us -> 0 us
  Pallas kernels: 0 us -> 46.3 us
  starting transfers between devices: 4.68 us -> 44.5 us
  matrix products: 39.2 us -> 0.43 us
  between operations: 14.6 us -> 0.86 us
  local copies, waits for them, and re-layouts: 7.73 us -> 15.1 us
  other arithmetic: 7.49 us -> 2.88 us
    unnamed x4 -> x0, waiting for transfers between devices: 111 us -> none
    psum x1 -> x0, waiting for transfers between devices: 79.6 us -> none  [shards(): lax.psum((seq_sums, seq_counts), ('dp', 'tensor', 'expert'))]
    ppermute x0 -> x34, waiting for transfers between devices: none -> 61.1 us  [swap(): return lax.ppermute(x, AXES, pairs)]
    all_gather x1 -> x0, waiting for transfers between devices: 48.1 us -> none  [shards(): lax.all_gather(local_rows, ('dp', 'tensor'), axis=0, tiled=True)]
    pallas_call x0 -> x4, Pallas kernels: none -> 46.3 us  [the longest x2 41.2 us: ffn(): pl.pallas_call(functools.partial(ffn_kernel, pieces, tile, cols), out_sha...]
    ppermute x0 -> x34, starting transfers between devices: none -> 44.5 us  [swap(): return lax.ppermute(x, AXES, pairs)]
    dot_general x5 -> x2, matrix products: 39.2 us -> 0.43 us  [core_shards(): lax.dot_general(marks[:, :2 * seqs], done, (((0,), (0,)), ((), ())), pref...]
    psum x1 -> x0, blocking collectives: 37.3 us -> none  [shards(): lax.psum((seq_sums, seq_counts), ('dp', 'tensor', 'expert'))]
  transfers between devices with their start and end apart: 4 -> 34, of which waited for: 4 -> 16; matrix products, arithmetic and copies ran while one was open for 0% -> 6% of each run, Pallas kernels for 0% -> 26%
where the time goes in v1:
time: 172 us; the launch traced here: 171 us
  waiting for transfers between devices  61.1 us (36%)
  Pallas kernels  46.3 us (27%)
  starting transfers between devices  44.5 us (26%)
  local copies, waits for them, and re-layouts  15.1 us (9%)
  other arithmetic  2.88 us (2%)
    ppermute x34, waiting for transfers between devices, swap(): return lax.ppermute(x, AXES, pairs)  61.1 us
    ppermute x34, starting transfers between devices, swap(): return lax.ppermute(x, AXES, pairs)  44.5 us
    pallas_call x2, Pallas kernels, ffn(): pl.pallas_call(functools.partial(ffn_kernel, pieces, tile, cols), out_sha...  41.2 us
    squeeze x3, local copies, waits for them, and re-layouts, core_shards(): lax.dynamic_index_in_dim(w, 1 - t, 0, keepdims=False)  9.87 us
  transfers between devices with their start and end apart: 34, of which 16 were waited for; matrix products, arithmetic and copies ran while one was open for 6% of the time, Pallas kernels for 26%

profile of v1, /device:TPU:0, one launch (start us, length us, event | category | flops | bytes accessed | tf_op | source)
XLA Modules:
  0.0 171.3 jit_solution(11571099235302921626)
XLA Ops:
  0.6 4.9 %dynamic-slice_bitcast_fusion.2 = bf16[960,2304]{1,0:T(8,128)(2,1)} fusion(bf16[2,2304,960]{1,2,0:T(8,128)(2,1)} %param.11, s32[]{:T(128)S(6)} %select_n.6), kind=kLoop, calls=%fused_computation.2 | loop fusion | bytes 8847364 | tf_op jit(solution)/shard_map/jit(dynamic_index_in_dim)/squeeze | solution.py:236
  7.1 2.5 %dynamic-slice_bitcast_fusion.1 = bf16[960,2304]{1,0:T(8,128)(2,1)} fusion(bf16[2,2304,960]{1,2,0:T(8,128)(2,1)S(1)} %copy-done.1, s32[]{:T(128)S(6)} %select_n.6), kind=kLoop, calls=%fused_computation.1 | loop fusion | bytes 8847364 | tf_op jit(solution)/shard_map/jit(dynamic_index_in_dim)/squeeze | solution.py:236
  11.4 2.4 %dynamic-slice_bitcast_fusion = bf16[960,2304]{1,0:T(8,128)(2,1)} fusion(bf16[2,960,2304]{2,1,0:T(8,128)(2,1)S(1)} %copy-done.2, s32[]{:T(128)S(6)} %select_n.6), kind=kLoop, calls=%fused_computation | loop fusion | bytes 8847364 | tf_op jit(solution)/shard_map/jit(dynamic_index_in_dim)/squeeze | solution.py:236
  15.6 2.5 %prep.1 = (bf16[96,2432]{1,0:T(8,128)(2,1)}, bf16[96,2432]{1,0:T(8,128)(2,1)}, f32[192,64]{1,0:T(8,128)}, f32[8,2432]{1,0:T(8,128)}) custom-call(s32[2]{0:T(128)} %pad_add_fusion.1.pos, bf16[64,2304]{1,0:T(8,128)(2,1)} %tokens.3, s32[2,64]{1,0:T(2,128)} %bitcast.26, f32[2,64]{1,0:T(2,128)} %bitcast.27, s32[1,64]{1,0:T(1,128)} %bitcast.24, s32[64,1]{1,0:T(8,128)} %copy.10.seg_col), custom_call_target="tpu_custom_call" | custom-call | tf_op jit(solution)/shard_map/prep/pallas_call | solution.py:94
  19.3 3.1 %collective-permute-start = (bf16[24,2432]{1,0:T(8,128)(2,1)S(1)}, bf16[24,2432]{1,0:T(8,128)(2,1)S(1)}, u32[]{:S(2)}, u32[]{:S(2)}) collective-permute-start(bf16[24,2432]{1,0:T(8,128)(2,1)S(1)} %get-tuple-element.33), channel_id=1, source_target_pairs={{0,1},{1,0},{2,3},{3,2},{4,5},{5,4},{6,7},{7,6},{8,9},{9,8},{10,11... | collective-permute-start | bytes 350216 | tf_op jit(solution)/shard_map/ppermute | solution.py:34
  22.4 2.6 %collective-permute-start.1 = (bf16[24,2432]{1,0:T(8,128)(2,1)S(1)}, bf16[24,2432]{1,0:T(8,128)(2,1)S(1)}, u32[]{:S(2)}, u32[]{:S(2)}) collective-permute-start(bf16[24,2432]{1,0:T(8,128)(2,1)S(1)} %get-tuple-element.32), channel_id=1, source_target_pairs={{0,2},{1,3},{2,0},{3,1},{4,6},{5,7},{6,4},{7,5},{8,10},{9,11},{10,... | collective-permute-start | bytes 350216 | tf_op jit(solution)/shard_map/ppermute | solution.py:34
  25.8 3.8 %collective-permute-start.2 = (bf16[24,2432]{1,0:T(8,128)(2,1)S(1)}, bf16[24,2432]{1,0:T(8,128)(2,1)S(1)}, u32[]{:S(2)}, u32[]{:S(2)}) collective-permute-start(bf16[24,2432]{1,0:T(8,128)(2,1)S(1)} %get-tuple-element.31), channel_id=1, source_target_pairs={{0,3},{1,2},{2,1},{3,0},{4,7},{5,6},{6,5},{7,4},{8,11},{9,10},{10,... | collective-permute-start | bytes 350216 | tf_op jit(solution)/shard_map/ppermute | solution.py:34
  29.5 4.5 %collective-permute-done.1 = bf16[24,2432]{1,0:T(8,128)(2,1)S(1)} collective-permute-done((bf16[24,2432]{1,0:T(8,128)(2,1)S(1)}, bf16[24,2432]{1,0:T(8,128)(2,1)S(1)}, u32[]{:S(2)}, u32[]{:S(2)}) %collective-permute-start.1) | collective-permute-done | bytes 116768 | tf_op jit(solution)/shard_map/ppermute | solution.py:34
  34.3 4.3 %collective-permute-start.17 = (bf16[24,2432]{1,0:T(8,128)(2,1)S(1)}, bf16[24,2432]{1,0:T(8,128)(2,1)S(1)}, u32[]{:S(2)}, u32[]{:S(2)}) collective-permute-start(bf16[24,2432]{1,0:T(8,128)(2,1)S(1)} %get-tuple-element.28), channel_id=1, source_target_pairs={{0,2},{1,3},{2,0},{3,1},{4,6},{5,7},{6,4},{7,5},{8,10},{9,11},{10,... | collective-permute-start | bytes 350216 | tf_op jit(solution)/shard_map/ppermute | solution.py:34
  38.9 5.8 %collective-permute-start.18 = (bf16[24,2432]{1,0:T(8,128)(2,1)S(1)}, bf16[24,2432]{1,0:T(8,128)(2,1)S(1)}, u32[]{:S(2)}, u32[]{:S(2)}) collective-permute-start(bf16[24,2432]{1,0:T(8,128)(2,1)S(1)} %get-tuple-element.27), channel_id=1, source_target_pairs={{0,3},{1,2},{2,1},{3,0},{4,7},{5,6},{6,5},{7,4},{8,11},{9,10},{10,... | collective-permute-start | bytes 350216 | tf_op jit(solution)/shard_map/ppermute | solution.py:34
  49.1 5.4 %collective-permute-done.3.refs_1_ = bf16[96,2304]{1,0:T(8,128)(2,1)S(1)} collective-permute-done((bf16[96,2304]{1,0:T(8,128)(2,1)S(1)}, bf16[96,2304]{1,0:T(8,128)(2,1)S(1)}, u32[]{:S(2)}, u32[]{:S(2)}) %collective-permute-start.3) | collective-permute-done | bytes 442400 | tf_op jit(solution)/shard_map/ppermute | solution.py:34
  56.1 8.0 %collective-permute-done.19.refs_1_ = bf16[96,2304]{1,0:T(8,128)(2,1)S(1)} collective-permute-done((bf16[96,2304]{1,0:T(8,128)(2,1)S(1)}, bf16[96,2304]{1,0:T(8,128)(2,1)S(1)}, u32[]{:S(2)}, u32[]{:S(2)}) %collective-permute-start.19) | collective-permute-done | bytes 442400 | tf_op jit(solution)/shard_map/ppermute | solution.py:34
  66.1 6.3 %collective-permute-done.21.refs_3_ = bf16[96,2304]{1,0:T(8,128)(2,1)S(1)} collective-permute-done((bf16[96,2304]{1,0:T(8,128)(2,1)S(1)}, bf16[96,2304]{1,0:T(8,128)(2,1)S(1)}, u32[]{:S(2)}, u32[]{:S(2)}) %collective-permute-start.21) | collective-permute-done | bytes 442400 | tf_op jit(solution)/shard_map/ppermute | solution.py:34
  73.9 20.6 %ffn.3 = (bf16[96,2304]{1,0:T(8,128)(2,1)S(1)}, bf16[96,2304]{1,0:T(8,128)(2,1)S(1)}, bf16[96,2304]{1,0:T(8,128)(2,1)S(1)}, bf16[96,2304]{1,0:T(8,128)(2,1)S(1)}) custom-call(s32[2]{0:T(128)S(1)} %copy-done, bf16[96,2304]{1,0:T(8,128)(2,1)S(1)} %slice.117.refs_0_, bf16[96,2304]{1,0:T(8,128)(2,1)S(1)} %collective-permute-done.19.refs_1_, ...), custom_call_target="tpu_custom_call" | custom-call | flops 10192158720 | bytes 26542080 | tf_op jit(solution)/shard_map/ffn/pallas_call | solution.py:169
  96.6 20.6 %ffn.2 = (bf16[96,2304]{1,0:T(8,128)(2,1)S(1)}, bf16[96,2304]{1,0:T(8,128)(2,1)S(1)}, bf16[96,2304]{1,0:T(8,128)(2,1)S(1)}, bf16[96,2304]{1,0:T(8,128)(2,1)S(1)}) custom-call(s32[2]{0:T(128)S(1)} %copy-done, bf16[96,2304]{1,0:T(8,128)(2,1)S(1)} %slice.108.refs_0_, bf16[96,2304]{1,0:T(8,128)(2,1)S(1)} %collective-permute-done.3.refs_1_, ...), custom_call_target="tpu_custom_call" | custom-call | flops 10192158720 | bytes 26542080 | tf_op jit(solution)/shard_map/ffn/pallas_call | solution.py:169
  121.0 9.3 %collective-permute-done.10 = bf16[96,2304]{1,0:T(8,128)(2,1)S(1)} collective-permute-done((bf16[96,2304]{1,0:T(8,128)(2,1)S(1)}, bf16[96,2304]{1,0:T(8,128)(2,1)S(1)}, u32[]{:S(2)}, u32[]{:S(2)}) %collective-permute-start.10) | collective-permute-done | bytes 442400 | tf_op jit(solution)/shard_map/ppermute | solution.py:34
  131.5 4.6 %collective-permute-done.9 = bf16[96,2304]{1,0:T(8,128)(2,1)S(1)} collective-permute-done((bf16[96,2304]{1,0:T(8,128)(2,1)S(1)}, bf16[96,2304]{1,0:T(8,128)(2,1)S(1)}, u32[]{:S(2)}, u32[]{:S(2)}) %collective-permute-start.9) | collective-permute-done | bytes 442400 | tf_op jit(solution)/shard_map/ppermute | solution.py:34
  136.1 2.6 %collective-permute-done.11 = bf16[96,2304]{1,0:T(8,128)(2,1)S(1)} collective-permute-done((bf16[96,2304]{1,0:T(8,128)(2,1)S(1)}, bf16[96,2304]{1,0:T(8,128)(2,1)S(1)}, u32[]{:S(2)}, u32[]{:S(2)}) %collective-permute-start.11) | collective-permute-done | bytes 442400 | tf_op jit(solution)/shard_map/ppermute | solution.py:34
  143.2 2.6 %collective-permute-start.27 = (bf16[24,2304]{1,0:T(8,128)(2,1)S(1)}, bf16[24,2304]{1,0:T(8,128)(2,1)S(1)}, u32[]{:S(2)}, u32[]{:S(2)}) collective-permute-start(bf16[24,2304]{1,0:T(8,128)(2,1)S(1)} %get-tuple-element.35), channel_id=1, source_target_pairs={{0,3},{1,2},{2,1},{3,0},{4,7},{5,6},{6,5},{7,4},{8,11},{9,10},{10,... | collective-permute-start | bytes 331784 | tf_op jit(solution)/shard_map/ppermute | solution.py:34
  147.4 2.8 %collective-permute-done.31 = f32[8,2432]{1,0:T(8,128)S(1)} collective-permute-done((f32[8,2432]{1,0:T(8,128)S(1)}, f32[8,2432]{1,0:T(8,128)S(1)}, u32[]{:S(2)}, u32[]{:S(2)}) %collective-permute-start.31) | collective-permute-done | bytes 77856 | tf_op jit(solution)/shard_map/ppermute | solution.py:34
  151.9 2.5 %collective-permute-done.26 = bf16[24,2304]{1,0:T(8,128)(2,1)S(1)} collective-permute-done((bf16[24,2304]{1,0:T(8,128)(2,1)S(1)}, bf16[24,2304]{1,0:T(8,128)(2,1)S(1)}, u32[]{:S(2)}, u32[]{:S(2)}) %collective-permute-start.26) | collective-permute-done | bytes 110624 | tf_op jit(solution)/shard_map/ppermute | solution.py:34
  154.5 6.0 %collective-permute-done.32 = f32[8,2432]{1,0:T(8,128)S(1)} collective-permute-done((f32[8,2432]{1,0:T(8,128)S(1)}, f32[8,2432]{1,0:T(8,128)S(1)}, u32[]{:S(2)}, u32[]{:S(2)}) %collective-permute-start.32) | collective-permute-done | bytes 77856 | tf_op jit(solution)/shard_map/ppermute | solution.py:34
  163.3 3.9 %collective-permute-done.33 = f32[8,2432]{1,0:T(8,128)S(1)} collective-permute-done((f32[8,2432]{1,0:T(8,128)S(1)}, f32[8,2432]{1,0:T(8,128)S(1)}, u32[]{:S(2)}, u32[]{:S(2)}) %collective-permute-start.33) | collective-permute-done | bytes 77856 | tf_op jit(solution)/shard_map/ppermute | solution.py:34
  168.8 2.6 %combine.1 = bf16[64,2304]{1,0:T(8,128)(2,1)} custom-call(bf16[64,2304]{1,0:T(8,128)(2,1)} %tokens.3, bf16[96,2304]{1,0:T(8,128)(2,1)} %pad_maximum_fusion.2.first, bf16[96,2304]{1,0:T(8,128)(2,1)} %copy-done.3, f32[192,64]{1,0:T(8,128)} %get-tuple-element.24.weights), custom_call_target="tpu_custom_call" | custom-call | tf_op jit(solution)/shard_map/combine/pallas_call | solution.py:208
  (91 shorter events, 36.3 us)
Async XLA Ops:
  5.6 68.2 %collective-permute-start.6 = (bf16[960,2304]{1,0:T(8,128)(2,1)}, bf16[960,2304]{1,0:T(8,128)(2,1)}, u32[]{:S(2)}, u32[]{:S(2)}) collective-permute-start(bf16[960,2304]{1,0:T(8,128)(2,1)} %dynamic-slice_bitcast_fusion.2), channel_id=1, source_target_pairs={{0,4},{1,5},{2,6},{3,7},{4,0},{5,1},{6,2},{7,3},{8,12},{9,13},{10,... | collective-permute-start | bytes 13271048 | tf_op jit(solution)/shard_map/ppermute | solution.py:34
  9.6 64.2 %collective-permute-start.7 = (bf16[960,2304]{1,0:T(8,128)(2,1)}, bf16[960,2304]{1,0:T(8,128)(2,1)}, u32[]{:S(2)}, u32[]{:S(2)}) collective-permute-start(bf16[960,2304]{1,0:T(8,128)(2,1)} %dynamic-slice_bitcast_fusion.1), channel_id=1, source_target_pairs={{0,4},{1,5},{2,6},{3,7},{4,0},{5,1},{6,2},{7,3},{8,12},{9,13},{10,... | collective-permute-start | bytes 13271048 | tf_op jit(solution)/shard_map/ppermute | solution.py:34
  13.8 60.0 %collective-permute-start.8 = (bf16[960,2304]{1,0:T(8,128)(2,1)}, bf16[960,2304]{1,0:T(8,128)(2,1)}, u32[]{:S(2)}, u32[]{:S(2)}) collective-permute-start(bf16[960,2304]{1,0:T(8,128)(2,1)} %dynamic-slice_bitcast_fusion), channel_id=1, source_target_pairs={{0,4},{1,5},{2,6},{3,7},{4,0},{5,1},{6,2},{7,3},{8,12},{9,13},{10,... | collective-permute-start | bytes 13271048 | tf_op jit(solution)/shard_map/ppermute | solution.py:34
  22.4 11.7 %collective-permute-start.1 = (bf16[24,2432]{1,0:T(8,128)(2,1)S(1)}, bf16[24,2432]{1,0:T(8,128)(2,1)S(1)}, u32[]{:S(2)}, u32[]{:S(2)}) collective-permute-start(bf16[24,2432]{1,0:T(8,128)(2,1)S(1)} %get-tuple-element.32), channel_id=1, source_target_pairs={{0,2},{1,3},{2,0},{3,1},{4,6},{5,7},{6,4},{7,5},{8,10},{9,11},{10,... | collective-permute-start | bytes 350216 | tf_op jit(solution)/shard_map/ppermute | solution.py:34
  25.8 8.5 %collective-permute-start.2 = (bf16[24,2432]{1,0:T(8,128)(2,1)S(1)}, bf16[24,2432]{1,0:T(8,128)(2,1)S(1)}, u32[]{:S(2)}, u32[]{:S(2)}) collective-permute-start(bf16[24,2432]{1,0:T(8,128)(2,1)S(1)} %get-tuple-element.31), channel_id=1, source_target_pairs={{0,3},{1,2},{2,1},{3,0},{4,7},{5,6},{6,5},{7,4},{8,11},{9,10},{10,... | collective-permute-start | bytes 350216 | tf_op jit(solution)/shard_map/ppermute | solution.py:34
  34.3 11.9 %collective-permute-start.17 = (bf16[24,2432]{1,0:T(8,128)(2,1)S(1)}, bf16[24,2432]{1,0:T(8,128)(2,1)S(1)}, u32[]{:S(2)}, u32[]{:S(2)}) collective-permute-start(bf16[24,2432]{1,0:T(8,128)(2,1)S(1)} %get-tuple-element.28), channel_id=1, source_target_pairs={{0,2},{1,3},{2,0},{3,1},{4,6},{5,7},{6,4},{7,5},{8,10},{9,11},{10,... | collective-permute-start | bytes 350216 | tf_op jit(solution)/shard_map/ppermute | solution.py:34
  38.9 8.8 %collective-permute-start.18 = (bf16[24,2432]{1,0:T(8,128)(2,1)S(1)}, bf16[24,2432]{1,0:T(8,128)(2,1)S(1)}, u32[]{:S(2)}, u32[]{:S(2)}) collective-permute-start(bf16[24,2432]{1,0:T(8,128)(2,1)S(1)} %get-tuple-element.27), channel_id=1, source_target_pairs={{0,3},{1,2},{2,1},{3,0},{4,7},{5,6},{6,5},{7,4},{8,11},{9,10},{10,... | collective-permute-start | bytes 350216 | tf_op jit(solution)/shard_map/ppermute | solution.py:34
  46.1 8.4 %collective-permute-start.3 = (bf16[96,2304]{1,0:T(8,128)(2,1)S(1)}, bf16[96,2304]{1,0:T(8,128)(2,1)S(1)}, u32[]{:S(2)}, u32[]{:S(2)}) collective-permute-start(bf16[96,2304]{1,0:T(8,128)(2,1)S(1)} %slice.108.refs_0_), channel_id=1, source_target_pairs={{0,8},{1,9},{2,10},{3,11},{4,20},{5,21},{6,22},{7,23},{8,0},{9,1},... | collective-permute-start | bytes 1327112 | tf_op jit(solution)/shard_map/ppermute | solution.py:34
  47.7 16.3 %collective-permute-start.19 = (bf16[96,2304]{1,0:T(8,128)(2,1)S(1)}, bf16[96,2304]{1,0:T(8,128)(2,1)S(1)}, u32[]{:S(2)}, u32[]{:S(2)}) collective-permute-start(bf16[96,2304]{1,0:T(8,128)(2,1)S(1)} %slice.117.refs_0_), channel_id=1, source_target_pairs={{0,8},{1,9},{2,10},{3,11},{4,20},{5,21},{6,22},{7,23},{8,0},{9,1},... | collective-permute-start | bytes 1327112 | tf_op jit(solution)/shard_map/ppermute | solution.py:34
  54.5 11.0 %collective-permute-start.20 = (bf16[96,2304]{1,0:T(8,128)(2,1)S(1)}, bf16[96,2304]{1,0:T(8,128)(2,1)S(1)}, u32[]{:S(2)}, u32[]{:S(2)}) collective-permute-start(bf16[96,2304]{1,0:T(8,128)(2,1)S(1)} %slice.117.refs_0_), channel_id=1, source_target_pairs={{0,16},{1,17},{2,18},{3,19},{4,12},{5,13},{6,14},{7,15},{8,24},{9,... | collective-permute-start | bytes 1327112 | tf_op jit(solution)/shard_map/ppermute | solution.py:34
  65.5 31.0 %collective-permute-start.4 = (bf16[96,2304]{1,0:T(8,128)(2,1)S(1)}, bf16[96,2304]{1,0:T(8,128)(2,1)S(1)}, u32[]{:S(2)}, u32[]{:S(2)}) collective-permute-start(bf16[96,2304]{1,0:T(8,128)(2,1)S(1)} %slice.108.refs_0_), channel_id=1, source_target_pairs={{0,16},{1,17},{2,18},{3,19},{4,12},{5,13},{6,14},{7,15},{8,24},{9,... | collective-permute-start | bytes 1327112 | tf_op jit(solution)/shard_map/ppermute | solution.py:34
  72.3 24.2 %collective-permute-start.5 = (bf16[96,2304]{1,0:T(8,128)(2,1)S(1)}, bf16[96,2304]{1,0:T(8,128)(2,1)S(1)}, u32[]{:S(2)}, u32[]{:S(2)}) collective-permute-start(bf16[96,2304]{1,0:T(8,128)(2,1)S(1)} %collective-permute-done.3.refs_1_), channel_id=1, source_target_pairs={{0,16},{1,17},{2,18},{3,19},{4,12},{5,13},{6,14},{7,15},{8,24},{9,... | collective-permute-start | bytes 1327112 | tf_op jit(solution)/shard_map/ppermute | solution.py:34
  94.5 24.8 %collective-permute-start.23 = (bf16[96,2304]{1,0:T(8,128)(2,1)S(1)}, bf16[96,2304]{1,0:T(8,128)(2,1)S(1)}, u32[]{:S(2)}, u32[]{:S(2)}) collective-permute-start(bf16[96,2304]{1,0:T(8,128)(2,1)S(1)} %get-tuple-element.23), channel_id=1, source_target_pairs={{0,16},{1,17},{2,18},{3,19},{4,12},{5,13},{6,14},{7,15},{8,24},{9,... | collective-permute-start | bytes 1327112 | tf_op jit(solution)/shard_map/ppermute | solution.py:34
  95.0 36.1 %collective-permute-start.22 = (bf16[96,2304]{1,0:T(8,128)(2,1)S(1)}, bf16[96,2304]{1,0:T(8,128)(2,1)S(1)}, u32[]{:S(2)}, u32[]{:S(2)}) collective-permute-start(bf16[96,2304]{1,0:T(8,128)(2,1)S(1)} %get-tuple-element.21), channel_id=1, source_target_pairs={{0,16},{1,17},{2,18},{3,19},{4,12},{5,13},{6,14},{7,15},{8,24},{9,... | collective-permute-start | bytes 1327112 | tf_op jit(solution)/shard_map/ppermute | solution.py:34
  117.2 13.0 %collective-permute-start.10 = (bf16[96,2304]{1,0:T(8,128)(2,1)S(1)}, bf16[96,2304]{1,0:T(8,128)(2,1)S(1)}, u32[]{:S(2)}, u32[]{:S(2)}) collective-permute-start(bf16[96,2304]{1,0:T(8,128)(2,1)S(1)} %get-tuple-element.18), channel_id=1, source_target_pairs={{0,16},{1,17},{2,18},{3,19},{4,12},{5,13},{6,14},{7,15},{8,24},{9,... | collective-permute-start | bytes 1327112 | tf_op jit(solution)/shard_map/ppermute | solution.py:34
  117.8 18.3 %collective-permute-start.9 = (bf16[96,2304]{1,0:T(8,128)(2,1)S(1)}, bf16[96,2304]{1,0:T(8,128)(2,1)S(1)}, u32[]{:S(2)}, u32[]{:S(2)}) collective-permute-start(bf16[96,2304]{1,0:T(8,128)(2,1)S(1)} %get-tuple-element.16), channel_id=1, source_target_pairs={{0,16},{1,17},{2,18},{3,19},{4,12},{5,13},{6,14},{7,15},{8,24},{9,... | collective-permute-start | bytes 1327112 | tf_op jit(solution)/shard_map/ppermute | solution.py:34
  119.4 11.7 %collective-permute-start.24 = (bf16[96,2304]{1,0:T(8,128)(2,1)S(1)}, bf16[96,2304]{1,0:T(8,128)(2,1)S(1)}, u32[]{:S(2)}, u32[]{:S(2)}) collective-permute-start(bf16[96,2304]{1,0:T(8,128)(2,1)S(1)} %add_convert_fusion.1), channel_id=1, source_target_pairs={{0,8},{1,9},{2,10},{3,11},{4,20},{5,21},{6,22},{7,23},{8,0},{9,1},... | collective-permute-start | bytes 1327112 | tf_op jit(solution)/shard_map/ppermute | solution.py:34
  141.3 9.0 %collective-permute-start.25 = (bf16[24,2304]{1,0:T(8,128)(2,1)S(1)}, bf16[24,2304]{1,0:T(8,128)(2,1)S(1)}, u32[]{:S(2)}, u32[]{:S(2)}) collective-permute-start(bf16[24,2304]{1,0:T(8,128)(2,1)S(1)} %get-tuple-element.37), channel_id=1, source_target_pairs={{0,1},{1,0},{2,3},{3,2},{4,5},{5,4},{6,7},{7,6},{8,9},{9,8},{10,11... | collective-permute-start | bytes 331784 | tf_op jit(solution)/shard_map/ppermute | solution.py:34
  141.4 13.0 %collective-permute-start.26 = (bf16[24,2304]{1,0:T(8,128)(2,1)S(1)}, bf16[24,2304]{1,0:T(8,128)(2,1)S(1)}, u32[]{:S(2)}, u32[]{:S(2)}) collective-permute-start(bf16[24,2304]{1,0:T(8,128)(2,1)S(1)} %get-tuple-element.36), channel_id=1, source_target_pairs={{0,2},{1,3},{2,0},{3,1},{4,6},{5,7},{6,4},{7,5},{8,10},{9,11},{10,... | collective-permute-start | bytes 331784 | tf_op jit(solution)/shard_map/ppermute | solution.py:34
  143.2 11.2 %collective-permute-start.27 = (bf16[24,2304]{1,0:T(8,128)(2,1)S(1)}, bf16[24,2304]{1,0:T(8,128)(2,1)S(1)}, u32[]{:S(2)}, u32[]{:S(2)}) collective-permute-start(bf16[24,2304]{1,0:T(8,128)(2,1)S(1)} %get-tuple-element.35), channel_id=1, source_target_pairs={{0,3},{1,2},{2,1},{3,0},{4,7},{5,6},{6,5},{7,4},{8,11},{9,10},{10,... | collective-permute-start | bytes 331784 | tf_op jit(solution)/shard_map/ppermute | solution.py:34
  147.3 13.5 %collective-permute-start.12 = (bf16[24,2304]{1,0:T(8,128)(2,1)S(1)}, bf16[24,2304]{1,0:T(8,128)(2,1)S(1)}, u32[]{:S(2)}, u32[]{:S(2)}) collective-permute-start(bf16[24,2304]{1,0:T(8,128)(2,1)S(1)} %get-tuple-element.41), channel_id=1, source_target_pairs={{0,1},{1,0},{2,3},{3,2},{4,5},{5,4},{6,7},{7,6},{8,9},{9,8},{10,11... | collective-permute-start | bytes 331784 | tf_op jit(solution)/shard_map/ppermute | solution.py:34
  150.2 12.3 %collective-permute-start.13 = (bf16[24,2304]{1,0:T(8,128)(2,1)S(1)}, bf16[24,2304]{1,0:T(8,128)(2,1)S(1)}, u32[]{:S(2)}, u32[]{:S(2)}) collective-permute-start(bf16[24,2304]{1,0:T(8,128)(2,1)S(1)} %get-tuple-element.40), channel_id=1, source_target_pairs={{0,2},{1,3},{2,0},{3,1},{4,6},{5,7},{6,4},{7,5},{8,10},{9,11},{10,... | collective-permute-start | bytes 331784 | tf_op jit(solution)/shard_map/ppermute | solution.py:34
  150.3 12.2 %collective-permute-start.14 = (bf16[24,2304]{1,0:T(8,128)(2,1)S(1)}, bf16[24,2304]{1,0:T(8,128)(2,1)S(1)}, u32[]{:S(2)}, u32[]{:S(2)}) collective-permute-start(bf16[24,2304]{1,0:T(8,128)(2,1)S(1)} %get-tuple-element.39), channel_id=1, source_target_pairs={{0,3},{1,2},{2,1},{3,0},{4,7},{5,6},{6,5},{7,4},{8,11},{9,10},{10,... | collective-permute-start | bytes 331784 | tf_op jit(solution)/shard_map/ppermute | solution.py:34
  154.4 13.6 %collective-permute-start.28 = (bf16[96,2304]{1,0:T(8,128)(2,1)S(1)}, bf16[96,2304]{1,0:T(8,128)(2,1)S(1)}, u32[]{:S(2)}, u32[]{:S(2)}) collective-permute-start(bf16[96,2304]{1,0:T(8,128)(2,1)S(1)} %pad_maximum_fusion.3), channel_id=1, source_target_pairs={{0,4},{1,5},{2,6},{3,7},{4,0},{5,1},{6,2},{7,3},{8,12},{9,13},{10,... | collective-permute-start | bytes 1327112 | tf_op jit(solution)/shard_map/ppermute | solution.py:34
  (16 other events, 153.9 us)

commit v2 on v1

v2 whole, which is shorter than its diff:
```python
import functools

import jax
import jax.numpy as jnp
from jax import lax
from jax.experimental import pallas as pl
from jax.experimental.pallas import tpu as pltpu
from jax.sharding import PartitionSpec as P

EXPERTS = 8
TOP = 2
CAP = 24
LANES = 128
VMEM_LIMIT = 48 << 20
AXES = ("dp", "tensor", "expert")


epsilon = 1e-06


def xor_steps(size):
    return size & (size - 1) == 0


def swap(x, d=0, t=0, z=0, turned=None):
    sizes = [lax.axis_size(name) for name in AXES]
    pairs = []
    for i in range(sizes[0]):
        for j in range(sizes[1]):
            for k in range(sizes[2]):
                flip = d if turned is None or j % 2 == 0 else turned
                here = (i * sizes[1] + j) * sizes[2] + k
                there = ((i ^ flip) * sizes[1] + (j ^ t)) * sizes[2] + (k ^ z)
                pairs.append((here, there))
    return lax.ppermute(x, AXES, pairs)


def prep_kernel(seqs, planes, tokens, routes, gates, seg_row, own, own_home, other, other_home, weights, sums):
    tok_count, width = tokens.shape
    slots = 2 * (planes + 1) * CAP
    t, z = lax.axis_index("tensor"), lax.axis_index("expert")
    raw = tokens[...]
    values = raw.astype(jnp.float32)
    scale = lax.rsqrt(jnp.mean(values * values, axis=1, keepdims=True) + epsilon)
    normed = (values * scale).astype(jnp.bfloat16)

    expert = lax.broadcasted_iota(jnp.int32, (EXPERTS, tok_count), 0)
    hot = [expert == routes[k : k + 1, :] for k in range(TOP)]
    named = (hot[0] | hot[1]).astype(jnp.bfloat16)
    earlier = (
        lax.broadcasted_iota(jnp.int32, (tok_count, tok_count), 0)
        < lax.broadcasted_iota(jnp.int32, (tok_count, tok_count), 1)
    ).astype(jnp.bfloat16)
    before = jnp.dot(named, earlier, preferred_element_type=jnp.float32)

    row = lax.broadcasted_iota(jnp.int32, (slots, tok_count), 0)
    group = row // CAP
    rank = row - group * CAP
    side = group // (planes + 1)
    plane = group - side * (planes + 1)
    row_expert = 2 * jnp.where(plane == planes, z, jnp.where(plane == z, EXPERTS, plane)) + (t ^ side)
    place = jnp.zeros((slots, tok_count), jnp.float32)
    weight = jnp.zeros((slots, tok_count), jnp.float32)
    for k in range(TOP):
        own_rank = jnp.sum(jnp.where(hot[k], before, 0.0), axis=0, keepdims=True).astype(jnp.int32)
        hit = (row_expert == routes[k : k + 1, :]) & (rank == own_rank)
        place = place + jnp.where(hit, 1.0, 0.0)
        weight = weight + jnp.where(hit, gates[k : k + 1, :], 0.0)
    weights[...] = weight

    rows = jnp.dot(place.astype(jnp.bfloat16), normed, preferred_element_type=jnp.float32).astype(jnp.bfloat16)
    high = weight.astype(jnp.bfloat16)
    low = (weight - high.astype(jnp.float32)).astype(jnp.bfloat16)
    lane = lax.broadcasted_iota(jnp.int32, (LANES, tok_count), 0)
    nt = (((1,), (1,)), ((), ()))
    marks = jnp.zeros((slots, LANES), jnp.float32)
    for part, first in ((high, 0), (low, seqs)):
        member = (lane == seg_row[...] + first).astype(jnp.bfloat16)
        marks = marks + lax.dot_general(part, member, nt, preferred_element_type=jnp.float32)
    marks = marks.astype(jnp.bfloat16)
    start = 0
    for out in (own, own_home, other, other_home):
        stop = start + out.shape[0]
        out[:, :width] = rows[start:stop]
        out[:, width:] = marks[start:stop]
        start = stop

    seq_hot = lax.broadcasted_iota(jnp.int32, (seqs, tok_count), 0) == seg_row[...]
    sums[:, :width] = jnp.dot(seq_hot.astype(jnp.bfloat16), raw, preferred_element_type=jnp.float32)
    counts = jnp.sum(seq_hot.astype(jnp.float32), axis=1, keepdims=True)
    sums[:, width:] = jnp.broadcast_to(counts, (seqs, LANES))


def prep(tokens, routes, gates, segments, seqs, planes):
    tok_count, width = tokens.shape
    vmem = pl.BlockSpec(memory_space=pltpu.VMEM)
    blocks = [
        jax.ShapeDtypeStruct((count * CAP, width + LANES), jnp.bfloat16) for count in (planes, 1, planes, 1)
    ]
    return pl.pallas_call(
        functools.partial(prep_kernel, seqs, planes),
        out_shape=(
            *blocks,
            jax.ShapeDtypeStruct((2 * (planes + 1) * CAP, tok_count), jnp.float32),
            jax.ShapeDtypeStruct((seqs, width + LANES), jnp.float32),
        ),
        in_specs=[vmem] * 4,
        out_specs=(vmem,) * 6,
        name="prep",
    )(tokens, routes.T, gates.T, segments[None, :])


def spans_of(total, tile):
    return [(start, min(tile, total - start)) for start in range(0, total, tile)]


def tie(value, *before):
    return lax.optimization_barrier((value,) + before)[0]


def ffn_kernel(pieces, tile, cols, depth, seqs, pool_in, *refs):
    parts, weights, outs = refs[:pieces], refs[pieces : pieces + 6], refs[pieces + 6 : 2 * pieces + 6]
    pool_out, rows_buf, gate_buf, up_buf, down_buf, hidden, row_sem, in_sem, down_sem = refs[2 * pieces + 6 :]
    t = lax.axis_index("tensor")
    halves = [[w.at[t] for w in weights[:3]], [w.at[t] for w in weights[3:]]]
    size = parts[0].shape[0]
    _, units, width = weights[0].shape
    row_copies = [
        pltpu.make_async_copy(parts[i], rows_buf.at[i, pl.ds(0, size)], row_sem.at[i]) for i in range(pieces)
    ]
    padded = rows_buf.shape[1]
    if padded > size:
        for i in range(pieces):
            rows_buf[i, size:] = jnp.zeros((padded - size, rows_buf.shape[2]), rows_buf.dtype)
    spans = spans_of(units, tile)
    col_spans = spans_of(width, cols)
    copies = []
    for h in range(2):
        for j, (start, length) in enumerate(spans):
            here = pl.ds(start, length)
            copies.append(
                [
                    pltpu.make_async_copy(halves[h][m].at[here], buf.at[h, here], in_sem.at[m, h * len(spans) + j])
                    for m, buf in enumerate((gate_buf, up_buf))
                ]
            )
    for j, (start, length) in enumerate(col_spans):
        here = pl.ds(start, length)
        copies.append(
            [
                pltpu.make_async_copy(
                    halves[h][2].at[:, here], down_buf.at[pl.ds(h * units, units), here], down_sem.at[h, j]
                )
                for h in range(2)
            ]
        )
    for copy in row_copies:
        copy.start()
    for group in copies[:depth]:
        for copy in group:
            copy.start()

    def arrive(i):
        for copy in copies[i]:
            copy.wait()
        for group in copies[i + depth : i + depth + 1]:
            for copy in group:
                copy.start()

    for copy in row_copies:
        copy.wait()
    x = rows_buf[:, :, :width].reshape(pieces * padded, width)
    marks = rows_buf[:, :, width:].reshape(pieces * padded, LANES).astype(jnp.float32).T[: 2 * seqs].astype(jnp.bfloat16)
    nt = (((1,), (1,)), ((), ()))
    for h in range(2):
        for j, (start, length) in enumerate(spans):
            arrive(h * len(spans) + j)
            here = slice(start, start + length)
            g = lax.dot_general(x, gate_buf[h, here], nt, preferred_element_type=jnp.float32)
            u = lax.dot_general(x, up_buf[h, here], nt, preferred_element_type=jnp.float32)
            value = g / (1.0 + jnp.exp(-g)) * u
            hidden[:, h * units + start : h * units + start + length] = value.astype(jnp.bfloat16)
    pool_out[:, width:] = pool_in[:, width:]
    for j, (start, length) in enumerate(col_spans):
        arrive(2 * len(spans) + j)
        here = slice(start, start + length)
        y = jnp.dot(hidden[...], down_buf[:, here], preferred_element_type=jnp.float32).astype(jnp.bfloat16)
        share = jnp.dot(marks, y, preferred_element_type=jnp.float32)
        pool_out[:, here] = pool_in[:, here] + share[:seqs] + share[seqs:]
        for i in range(pieces):
            outs[i][:, here] = y[i * padded : i * padded + size]


def ffn(parts, weights, pool):
    pieces = len(parts)
    size = parts[0].shape[0]
    _, units, width = weights[0].shape
    tile, cols, depth = 256, 768, 3
    padded = -(-size // 16) * 16
    rows = pieces * padded
    anywhere = pl.BlockSpec(memory_space=pl.ANY)
    vmem = pl.BlockSpec(memory_space=pltpu.VMEM)
    return pl.pallas_call(
        functools.partial(ffn_kernel, pieces, tile, cols, depth, pool.shape[0]),
        out_shape=(jax.ShapeDtypeStruct((size, width), jnp.bfloat16),) * pieces
        + (jax.ShapeDtypeStruct(pool.shape, pool.dtype),),
        in_specs=[vmem] + [anywhere] * (pieces + 6),
        out_specs=(vmem,) * (pieces + 1),
        scratch_shapes=[
            pltpu.VMEM((pieces, padded, width + LANES), jnp.bfloat16),
            pltpu.VMEM((2, units, width), jnp.bfloat16),
            pltpu.VMEM((2, units, width), jnp.bfloat16),
            pltpu.VMEM((2 * units, width), jnp.bfloat16),
            pltpu.VMEM((rows, 2 * units), jnp.bfloat16),
            pltpu.SemaphoreType.DMA((pieces,)),
            pltpu.SemaphoreType.DMA((2, 2 * len(spans_of(units, tile)))),
            pltpu.SemaphoreType.DMA((2, len(spans_of(width, cols)))),
        ],
        compiler_params=pltpu.CompilerParams(vmem_limit_bytes=VMEM_LIMIT),
        cost_estimate=pl.CostEstimate(
            flops=12 * rows * width * units, transcendentals=2 * rows * units, bytes_accessed=12 * units * width
        ),
        name="ffn",
    )(pool, *parts, *weights)


def settle_kernel(planes, *refs):
    parts, out = refs[:-1], refs[-1]
    z = lax.axis_index("expert")
    total = parts[0][...].astype(jnp.float32)
    for part in parts[1:]:
        total = total + part[...].astype(jnp.float32)
    for j in range(planes - 1):
        out[lax.rem(z + 1 + j, planes)] = total[j * CAP : (j + 1) * CAP].astype(jnp.bfloat16)
    out[z] = jnp.zeros(out.shape[1:], jnp.bfloat16)


def settle(parts, planes):
    vmem = pl.BlockSpec(memory_space=pltpu.VMEM)
    return pl.pallas_call(
        functools.partial(settle_kernel, planes),
        out_shape=jax.ShapeDtypeStruct((planes, CAP, parts[0].shape[1]), jnp.bfloat16),
        in_specs=[vmem] * len(parts),
        out_specs=vmem,
        name="settle",
    )(*parts)


def combine_kernel(tokens, weights, *refs):
    parts, out = refs[:-1], refs[-1]
    mixed = jnp.zeros(tokens.shape, jnp.float32)
    start = 0
    for part in parts:
        stop = start + part.shape[0]
        weight = weights[start:stop].T
        high = weight.astype(jnp.bfloat16)
        low = (weight - high.astype(jnp.float32)).astype(jnp.bfloat16)
        for factor in (low, high):
            mixed = mixed + jnp.dot(factor, part[...], preferred_element_type=jnp.float32)
        start = stop
    out[...] = (tokens[...].astype(jnp.float32) + mixed).astype(jnp.bfloat16)


def combine(tokens, weights, parts):
    vmem = pl.BlockSpec(memory_space=pltpu.VMEM)
    return pl.pallas_call(
        combine_kernel,
        out_shape=jax.ShapeDtypeStruct(tokens.shape, jnp.bfloat16),
        in_specs=[vmem] * (2 + len(parts)),
        out_specs=vmem,
        name="combine",
    )(tokens, weights, *parts)


def added(*arrays):
    total = arrays[0].astype(jnp.float32)
    for array in arrays[1:]:
        total = total + array.astype(jnp.float32)
    return total.astype(jnp.bfloat16)


def core_shards(tokens, routes, gates, segments, w_gate, w_up, w_down):
    tok_count, width = tokens.shape
    chips, cores, planes = (lax.axis_size(name) for name in AXES)
    seqs = tok_count * chips * cores * planes // 256

    own, own_home, other, other_home, weights, pool = prep(tokens, routes, gates, segments, seqs, planes)
    sibling, sibling_home = swap(other, t=1), swap(other_home, t=1)
    stored = (jnp.swapaxes(w_gate, 1, 2), jnp.swapaxes(w_up, 1, 2), w_down)

    tied = lax.optimization_barrier(stored + (sibling,))
    far = tuple(pltpu.with_memory_space_constraint(swap(array, t=1), pltpu.HBM) for array in tied[:3])

    z = lax.axis_index("expert")
    others = (planes - 1) * CAP

    def exchange(rows):
        return lax.all_to_all(rows, "expert", split_axis=0, concat_axis=0, tiled=True)

    def outward(rows):
        return lax.dynamic_slice_in_dim(jnp.concatenate([rows, rows]), (z + 1) * CAP, others)

    def sent_on(arrays):
        return [swap(array, d=step, turned=turned) for array, (step, turned) in zip(arrays, ((1, 2), (2, 1), (3, 3)))]

    def together(arrays, *before):
        return list(lax.optimization_barrier(tuple(arrays) + before))[: len(arrays)]

    home = jnp.concatenate([own_home, sibling_home])
    arrived = exchange(own)
    home_near, home_side = swap(home, d=1, turned=2), swap(home, d=2, turned=1)
    arrived, home_near = together([arrived], home_near)[0], home_near
    early = outward(arrived)
    near, side = swap(early, d=1, turned=2), swap(early, d=2, turned=1)
    late = outward(exchange(tie(sibling, early)))
    first = [early, near, side, swap(near, d=2, turned=1)]
    home = [home, home_near, home_side, swap(home_near, d=2, turned=1)]
    second = [late] + sent_on([late] * 3)

    def back(parts):
        return [parts[0]] + sent_on(parts[1:])

    *partial, pool = ffn(first, stored + far, pool)
    early = back(partial)
    *partial, pool = ffn(second, stored + far, pool)
    early = settle(together(early, pool), planes)
    late = [partial[0]] + sent_on(together(partial[1:], early))
    home[0] = tie(home[0], early)
    early = exchange(early).reshape(planes * CAP, width)
    *partial, pool = ffn(home, stored + far, pool)
    early, *late = together([early] + late, pool)
    late = settle(late, planes)
    partial = together(partial, early, late)
    late = exchange(late).reshape(planes * CAP, width)
    home = added(*back(partial))
    pool = tie(pool, early)
    for axis in ("z", "t", "d"):
        size = lax.axis_size({"t": "tensor", "z": "expert", "d": "dp"}[axis])
        pool = sum([swap(pool, **{axis: step}) for step in range(1, size)], pool)
    parts = (early, home[:CAP], swap(late, t=1), swap(home[CAP:], t=1))
    embedded = combine(tokens, weights, parts)

    pooled = pool[:, :width] / pool[:, width : width + 1]
    return (embedded, pooled)


def slot_numbers(routes):
    flat_routes = routes.reshape(-1)
    pairs = flat_routes.shape[0]
    same = flat_routes[:, None] == flat_routes[None, :]
    earlier = jnp.arange(pairs)[None, :] < jnp.arange(pairs)[:, None]
    slot_rank = jnp.sum((same & earlier).astype(jnp.int32), axis=1)
    return flat_routes * CAP + slot_rank


def shards(tokens, routes, gates, segments, w_gate, w_up, w_down):
    tok_count, width = tokens.shape
    experts_axis = lax.axis_size("expert")
    per_device = w_gate.shape[0]
    replicas = max(1, experts_axis // EXPERTS)
    plane = lax.axis_size("dp") * lax.axis_size("tensor")
    values = tokens.astype(jnp.float32)
    scale = lax.rsqrt(jnp.mean(values * values, axis=1, keepdims=True) + epsilon)
    normed = (values * scale).astype(jnp.bfloat16)
    slot_index = slot_numbers(routes)
    hits = jnp.arange(EXPERTS * CAP, dtype=jnp.int32)[:, None] == slot_index[None, :]
    placing = jnp.sum(hits.astype(jnp.int32).reshape(EXPERTS * CAP, tok_count, TOP), axis=2)
    slot_rows = jnp.dot(placing.astype(jnp.bfloat16), normed, preferred_element_type=jnp.float32)
    shaped = slot_rows.astype(jnp.bfloat16).reshape(EXPERTS, CAP, width)
    if replicas > 1:
        shaped = jnp.repeat(shaped, replicas, axis=0)
    send_rows = shaped.reshape(EXPERTS * replicas * CAP, width)
    received = lax.all_to_all(send_rows, "expert", split_axis=0, concat_axis=0, tiled=True)
    local_rows = received.reshape(experts_axis, per_device, CAP, width)
    block = lax.all_gather(local_rows, ("dp", "tensor"), axis=0, tiled=True)
    gate_proj = jnp.einsum("nacd,adf->nacf", block, w_gate, preferred_element_type=jnp.float32)
    up_proj = jnp.einsum("nacd,adf->nacf", block, w_up, preferred_element_type=jnp.float32)
    hidden = (jax.nn.silu(gate_proj) * up_proj).astype(jnp.bfloat16)
    summed = lax.psum_scatter(
        jnp.einsum("nacf,afd->nacd", hidden, w_down, preferred_element_type=jnp.float32).astype(jnp.bfloat16),
        ("dp", "tensor"),
        scatter_dimension=0,
        tiled=True,
    )
    returned = lax.all_to_all(summed, "expert", split_axis=0, concat_axis=0, tiled=True).astype(jnp.float32)
    expert_out = jnp.sum(returned.reshape(EXPERTS, replicas, CAP, width), axis=1)
    picked = jnp.take(expert_out.reshape(EXPERTS * CAP, width), slot_index, axis=0).reshape(tok_count, TOP, width)
    embedded = (values + jnp.sum(gates[:, :, None] * picked, axis=1)).astype(jnp.bfloat16)
    seq_total = tok_count * plane * experts_axis // 256
    seq_hot = jnp.arange(seq_total, dtype=jnp.int32)[:, None] == segments[None, :]
    seq_sums = jnp.dot(seq_hot.astype(jnp.bfloat16), embedded, preferred_element_type=jnp.float32)
    seq_counts = jnp.sum(seq_hot.astype(jnp.float32), axis=1)
    total_sums, total_counts = lax.psum((seq_sums, seq_counts), AXES)
    return (embedded, total_sums / total_counts[:, None])


def solution(mesh):
    placed = (
        P(AXES, None),
        P(AXES, None),
        P(AXES, None),
        P(AXES),
        P("expert", None, ("dp", "tensor")),
        P("expert", None, ("dp", "tensor")),
        P("expert", ("dp", "tensor"), None),
    )
    dp, tensor, planes = (mesh.shape[name] for name in AXES)
    paired = dp == 4 and tensor == 2 and EXPERTS == tensor * planes and xor_steps(planes)
    return jax.shard_map(
        core_shards if paired else shards,
        mesh=mesh,
        in_specs=placed,
        out_specs=(P(AXES, None), P()),
        check_vma=False,
    )
```

time: 172 us -> 156 us (0.907)
  waiting for transfers between devices: 61.1 us -> 36.3 us
  starting transfers between devices: 44.5 us -> 54.1 us
  Pallas kernels: 46.3 us -> 55.1 us
  local copies, waits for them, and re-layouts: 15.1 us -> 7.76 us
    ppermute x34 -> x32, waiting for transfers between devices: 61.1 us -> 28.9 us  [swap(): return lax.ppermute(x, AXES, pairs)]
    all_to_all x0 -> x4, starting transfers between devices: none -> 21.9 us  [exchange(): lax.all_to_all(rows, 'expert', split_axis=0, concat_axis=0, tiled=True)]
    ppermute x34 -> x32, starting transfers between devices: 44.5 us -> 32.2 us  [swap(): return lax.ppermute(x, AXES, pairs)]
    squeeze x3 -> x0, local copies, waits for them, and re-layouts: 9.87 us -> none  [core_shards(): lax.dynamic_index_in_dim(w, 1 - t, 0, keepdims=False)]
    pallas_call x3 -> x6, Pallas kernels: 43.8 us -> 52.2 us  [the longest x3 45 us: ffn(): pl.pallas_call(functools.partial(ffn_kernel, pieces, tile, cols, depth, p...]
    all_to_all x0 -> x4, waiting for transfers between devices: none -> 7.4 us  [exchange(): lax.all_to_all(rows, 'expert', split_axis=0, concat_axis=0, tiled=True)]
    unnamed x12 -> x23, local copies, waits for them, and re-layouts: 3.18 us -> 6.97 us
  transfers between devices with their start and end apart: 34 -> 36, of which waited for: 16 -> 11; matrix products, arithmetic and copies ran while one was open for 6% -> 2% of each run, Pallas kernels for 26% -> 32%
where the time goes in v2:
time: 156 us; the launch traced here: 155 us
  Pallas kernels  55.1 us (35%)
  starting transfers between devices  54.1 us (35%)
  waiting for transfers between devices  36.3 us (23%)
  local copies, waits for them, and re-layouts  7.76 us (5%)
    pallas_call x3, Pallas kernels, ffn(): pl.pallas_call(functools.partial(ffn_kernel, pieces, tile, cols, depth, p...  45 us
    ppermute x32, starting transfers between devices, swap(): return lax.ppermute(x, AXES, pairs)  32.2 us
    ppermute x32, waiting for transfers between devices, swap(): return lax.ppermute(x, AXES, pairs)  28.9 us
    all_to_all x4, starting transfers between devices, exchange(): lax.all_to_all(rows, 'expert', split_axis=0, concat_axis=0, tiled=True)  21.9 us
    all_to_all x4, waiting for transfers between devices, exchange(): lax.all_to_all(rows, 'expert', split_axis=0, concat_axis=0, tiled=True)  7.4 us
    unnamed x23, local copies, waits for them, and re-layouts  6.97 us
    pallas_call x2, Pallas kernels, settle(): pl.pallas_call(functools.partial(settle_kernel, planes), out_shape=jax.Sh...  4.42 us
  transfers between devices with their start and end apart: 36, of which 11 were waited for; matrix products, arithmetic and copies ran while one was open for 2% of the time, Pallas kernels for 32%

profile of v2, /device:TPU:0, one launch (start us, length us, event | category | flops | bytes accessed | tf_op | source)
XLA Modules:
  0.0 155.3 jit_solution(4262559527240610441)
XLA Ops:
  0.6 2.8 %prep.1 = (bf16[96,2432]{1,0:T(8,128)(2,1)}, bf16[24,2432]{1,0:T(8,128)(2,1)}, bf16[96,2432]{1,0:T(8,128)(2,1)}, bf16[24,2432]{1,0:T(8,128)(2,1)}, f32[240,64]{1,0:T(8,128)}, /*index=5*/f32[8,2432]{1,0:T(8,128)}) custom-call(bf16[64,2304]{1,0:T(8,128)(2,1)} %tokens.3, s32[2,64]{1,0:T(2,128)} %bitcast.24, f32[2,64]{1,0:T(2,128)} %bitcast.25, s32[1,64]{1,0:T(1,128)} %bitcast.26), custom_call_target="tpu_custom_call" | custom-call | tf_op jit(solution)/shard_map/prep/pallas_call | solution.py:100
  6.5 6.0 %all-to-all-start = ((bf16[4,24,2432]{2,1,0:T(8,128)(2,1)}), bf16[4,24,2432]{2,1,0:T(8,128)(2,1)S(1)}, u32[]{:S(2)}, u32[]{:S(2)}) async-start(bf16[4,24,2432]{2,1,0:T(8,128)(2,1)} %bitcast.22), calls=%async_computation | async-start | bytes 933888 | tf_op jit(solution)/shard_map/all_to_all | solution.py:298
  13.5 6.5 %collective-permute-done = bf16[24,2432]{1,0:T(8,128)(2,1)S(1)} collective-permute-done((bf16[24,2432]{1,0:T(8,128)(2,1)}, bf16[24,2432]{1,0:T(8,128)(2,1)S(1)}, u32[]{:S(2)}, u32[]{:S(2)}) %collective-permute-start) | collective-permute-done | bytes 116768 | tf_op jit(solution)/shard_map/ppermute | solution.py:35
  20.0 2.9 %collective-permute-start.1 = (bf16[48,2432]{1,0:T(8,128)(2,1)S(1)}, bf16[48,2432]{1,0:T(8,128)(2,1)S(1)}, u32[]{:S(2)}, u32[]{:S(2)}) collective-permute-start(bf16[48,2432]{1,0:T(8,128)(2,1)S(1)} %constant_dynamic-update-slice_fusion.refs_0_), channel_id=1, source_target_pairs={{0,8},{1,9},{2,10},{3,11},{4,20},{5,21},{6,22},{7,23},{8,0},{9,1},... | collective-permute-start | bytes 700424 | tf_op jit(solution)/shard_map/ppermute | solution.py:35
  22.9 4.0 %collective-permute-done.1.refs_1_ = bf16[48,2432]{1,0:T(8,128)(2,1)S(1)} collective-permute-done((bf16[48,2432]{1,0:T(8,128)(2,1)S(1)}, bf16[48,2432]{1,0:T(8,128)(2,1)S(1)}, u32[]{:S(2)}, u32[]{:S(2)}) %collective-permute-start.1) | collective-permute-done | bytes 233504 | tf_op jit(solution)/shard_map/ppermute | solution.py:35
  27.1 5.4 %all-to-all-start.1 = ((bf16[4,24,2432]{2,1,0:T(8,128)(2,1)}), bf16[4,24,2432]{2,1,0:T(8,128)(2,1)S(1)}, u32[]{:S(2)}, u32[]{:S(2)}) async-start(bf16[4,24,2432]{2,1,0:T(8,128)(2,1)} %bitcast.7), calls=%async_computation.1 | async-start | bytes 933888 | tf_op jit(solution)/shard_map/all_to_all | solution.py:298
  35.6 8.0 %collective-permute-done.2.refs_1_ = bf16[72,2432]{1,0:T(8,128)(2,1)S(1)} collective-permute-done((bf16[72,2432]{1,0:T(8,128)(2,1)S(1)}, bf16[72,2432]{1,0:T(8,128)(2,1)S(1)}, u32[]{:S(2)}, u32[]{:S(2)}) %collective-permute-start.2) | collective-permute-done | bytes 350240 | tf_op jit(solution)/shard_map/ppermute | solution.py:35
  47.0 4.4 %collective-permute-done.4.refs_3_ = bf16[72,2432]{1,0:T(8,128)(2,1)S(1)} collective-permute-done((bf16[72,2432]{1,0:T(8,128)(2,1)S(1)}, bf16[72,2432]{1,0:T(8,128)(2,1)S(1)}, u32[]{:S(2)}, u32[]{:S(2)}) %collective-permute-start.4) | collective-permute-done | bytes 350240 | tf_op jit(solution)/shard_map/ppermute | solution.py:35
  51.5 2.4 %collective-permute-start.12 = (bf16[72,2432]{1,0:T(8,128)(2,1)S(1)}, bf16[72,2432]{1,0:T(8,128)(2,1)S(1)}, u32[]{:S(2)}, u32[]{:S(2)}) collective-permute-start(bf16[72,2432]{1,0:T(8,128)(2,1)S(1)} %fusion.refs_0_), channel_id=1, source_target_pairs={{0,8},{1,9},{2,10},{3,11},{4,20},{5,21},{6,22},{7,23},{8,0},{9,1},... | collective-permute-start | bytes 1050632 | tf_op jit(solution)/shard_map/ppermute | solution.py:35
  53.9 2.0 %collective-permute-start.13 = (bf16[72,2432]{1,0:T(8,128)(2,1)S(1)}, bf16[72,2432]{1,0:T(8,128)(2,1)S(1)}, u32[]{:S(2)}, u32[]{:S(2)}) collective-permute-start(bf16[72,2432]{1,0:T(8,128)(2,1)S(1)} %fusion.refs_0_), channel_id=1, source_target_pairs={{0,16},{1,17},{2,18},{3,19},{4,12},{5,13},{6,14},{7,15},{8,24},{9,... | collective-permute-start | bytes 1050632 | tf_op jit(solution)/shard_map/ppermute | solution.py:35
  56.8 15.6 %ffn.3 = (bf16[72,2304]{1,0:T(8,128)(2,1)S(1)}, bf16[72,2304]{1,0:T(8,128)(2,1)S(1)}, bf16[72,2304]{1,0:T(8,128)(2,1)S(1)}, bf16[72,2304]{1,0:T(8,128)(2,1)S(1)}, f32[8,2432]{1,0:T(8,128)S(1)}) custom-call(f32[8,2432]{1,0:T(8,128)S(1)} %copy-done.2, bf16[72,2432]{1,0:T(8,128)(2,1)S(1)} %fusion.1.refs_0_, ...), custom_call_target="tpu_custom_call" | custom-call | flops 8493465600 | bytes 26542080 | tf_op jit(solution)/shard_map/ffn/pallas_call | solution.py:203
  74.7 2.0 %collective-permute-start.10 = (bf16[72,2304]{1,0:T(8,128)(2,1)S(1)}, bf16[72,2304]{1,0:T(8,128)(2,1)S(1)}, u32[]{:S(2)}, u32[]{:S(2)}) collective-permute-start(bf16[72,2304]{1,0:T(8,128)(2,1)S(1)} %get-tuple-element.58), channel_id=1, source_target_pairs={{0,16},{1,17},{2,18},{3,19},{4,12},{5,13},{6,14},{7,15},{8,24},{9,... | collective-permute-start | bytes 995336 | tf_op jit(solution)/shard_map/ppermute | solution.py:35
  76.6 15.8 %ffn.4 = (bf16[72,2304]{1,0:T(8,128)(2,1)S(1)}, bf16[72,2304]{1,0:T(8,128)(2,1)S(1)}, bf16[72,2304]{1,0:T(8,128)(2,1)S(1)}, bf16[72,2304]{1,0:T(8,128)(2,1)S(1)}, f32[8,2432]{1,0:T(8,128)S(1)}) custom-call(f32[8,2432]{1,0:T(8,128)S(1)} %get-tuple-element.60.pool_in, bf16[72,2432]{1,0:T(8,128)(2,1)S(1)} %fusion.refs_0_, ...), custom_call_target="tpu_custom_call" | custom-call | flops 8493465600 | bytes 26542080 | tf_op jit(solution)/shard_map/ffn/pallas_call | solution.py:203
  94.7 2.2 %settle.2 = bf16[4,24,2304]{2,1,0:T(8,128)(2,1)} custom-call(bf16[72,2304]{1,0:T(8,128)(2,1)} %copy-done.1, bf16[72,2304]{1,0:T(8,128)(2,1)} %copy-done.7, bf16[72,2304]{1,0:T(8,128)(2,1)} %copy-done.8, bf16[72,2304]{1,0:T(8,128)(2,1)} %copy-done.9), custom_call_target="tpu_custom_call" | custom-call | tf_op jit(solution)/shard_map/settle/pallas_call | solution.py:240
  96.9 5.5 %all-to-all-start.2 = ((bf16[4,24,2304]{2,1,0:T(8,128)(2,1)}), bf16[4,24,2304]{2,1,0:T(8,128)(2,1)S(1)}, u32[]{:S(2)}, u32[]{:S(2)}) async-start(bf16[4,24,2304]{2,1,0:T(8,128)(2,1)} %settle.2), calls=%async_computation.2 | async-start | bytes 884736 | tf_op jit(solution)/shard_map/all_to_all | solution.py:298
  103.9 2.0 %collective-permute-start.16 = (bf16[72,2304]{1,0:T(8,128)(2,1)S(1)}, bf16[72,2304]{1,0:T(8,128)(2,1)S(1)}, u32[]{:S(2)}, u32[]{:S(2)}) collective-permute-start(bf16[72,2304]{1,0:T(8,128)(2,1)S(1)} %get-tuple-element.72), channel_id=1, source_target_pairs={{0,16},{1,17},{2,18},{3,19},{4,12},{5,13},{6,14},{7,15},{8,24},{9,... | collective-permute-start | bytes 995336 | tf_op jit(solution)/shard_map/ppermute | solution.py:35
  105.9 13.7 %ffn.5 = (bf16[48,2304]{1,0:T(8,128)(2,1)S(1)}, bf16[48,2304]{1,0:T(8,128)(2,1)S(1)}, bf16[48,2304]{1,0:T(8,128)(2,1)S(1)}, bf16[48,2304]{1,0:T(8,128)(2,1)S(1)}, f32[8,2432]{1,0:T(8,128)S(1)}) custom-call(f32[8,2432]{1,0:T(8,128)S(1)} %get-tuple-element.62.pool_in, bf16[48,2432]{1,0:T(8,128)(2,1)S(1)} %constant_dynamic-update-slice_fusion.refs_0_, ...), custom_call_target="tpu_custom_call" | custom-call | flops 5096079360 | bytes 26542080 | tf_op jit(solution)/shard_map/ffn/pallas_call | solution.py:203
  121.1 3.9 %collective-permute-start.27 = (f32[8,2432]{1,0:T(8,128)S(1)}, f32[8,2432]{1,0:T(8,128)S(1)}, u32[]{:S(2)}, u32[]{:S(2)}) collective-permute-start(f32[8,2432]{1,0:T(8,128)S(1)} %get-tuple-element.89), channel_id=1, source_target_pairs={{0,3},{1,2},{2,1},{3,0},{4,7},{5,6},{6,5},{7,4},{8,11},{9,10},{10,... | collective-permute-start | bytes 233480 | tf_op jit(solution)/shard_map/ppermute | solution.py:35
  125.6 2.2 %settle.3 = bf16[4,24,2304]{2,1,0:T(8,128)(2,1)} custom-call(bf16[72,2304]{1,0:T(8,128)(2,1)} %copy-done, bf16[72,2304]{1,0:T(8,128)(2,1)} %copy-done.5, bf16[72,2304]{1,0:T(8,128)(2,1)} %copy-done.6, bf16[72,2304]{1,0:T(8,128)(2,1)} %collective-permute-done.17.refs_3_), custom_call_target="tpu_custom_call" | custom-call | tf_op jit(solution)/shard_map/settle/pallas_call | solution.py:240
  127.8 2.9 %collective-permute-start.22 = (bf16[48,2304]{1,0:T(8,128)(2,1)S(1)}, bf16[48,2304]{1,0:T(8,128)(2,1)S(1)}, u32[]{:S(2)}, u32[]{:S(2)}) collective-permute-start(bf16[48,2304]{1,0:T(8,128)(2,1)S(1)} %get-tuple-element.88), channel_id=1, source_target_pairs={{0,24},{1,25},{2,26},{3,27},{4,28},{5,29},{6,30},{7,31},{8,16},{9,... | collective-permute-start | bytes 663560 | tf_op jit(solution)/shard_map/ppermute | solution.py:35
  131.4 5.0 %all-to-all-start.3 = ((bf16[4,24,2304]{2,1,0:T(8,128)(2,1)}), bf16[4,24,2304]{2,1,0:T(8,128)(2,1)S(1)}, u32[]{:S(2)}, u32[]{:S(2)}) async-start(bf16[4,24,2304]{2,1,0:T(8,128)(2,1)} %settle.3), calls=%async_computation.3 | async-start | bytes 884736 | tf_op jit(solution)/shard_map/all_to_all | solution.py:298
  136.4 2.9 %collective-permute-start.31 = (f32[8,2432]{1,0:T(8,128)S(1)}, f32[8,2432]{1,0:T(8,128)S(1)}, u32[]{:S(2)}, u32[]{:S(2)}) collective-permute-start(f32[8,2432]{1,0:T(8,128)S(1)} %add.46), channel_id=1, source_target_pairs={{0,24},{1,25},{2,26},{3,27},{4,28},{5,29},{6,30},{7,31},{8,16},{9,... | collective-permute-start | bytes 233480 | tf_op jit(solution)/shard_map/ppermute | solution.py:35
  144.0 5.8 %all-to-all-done.3 = bf16[4,24,2304]{2,1,0:T(8,128)(2,1)S(1)} async-done(((bf16[4,24,2304]{2,1,0:T(8,128)(2,1)}), bf16[4,24,2304]{2,1,0:T(8,128)(2,1)S(1)}, u32[]{:S(2)}, u32[]{:S(2)}) %all-to-all-start.3) | async-done | bytes 442400 | tf_op jit(solution)/shard_map/all_to_all | solution.py:298
  152.4 2.9 %combine.1 = bf16[64,2304]{1,0:T(8,128)(2,1)} custom-call(bf16[64,2304]{1,0:T(8,128)(2,1)} %tokens.3, f32[240,64]{1,0:T(8,128)} %get-tuple-element.46.weights, bf16[96,2304]{1,0:T(8,128)(2,1)} %bitcast.21, bf16[24,2304]{1,0:T(8,128)(2,1)} %get-tuple-element.91.refs_1_, bf16[96,2304]{1,0:T(8,128)(2,1)} %copy-done.4, bf16[24,2304]{1,0:T(8,128)(2,1)} %copy-done.10), custom_call_target="tpu_custom_call" | custom-call | tf_op jit(solution)/shard_map/combine/pallas_call | solution.py:266
  (88 shorter events, 27.6 us)
Async XLA Ops:
  5.6 45.8 %collective-permute-start.6 = (bf16[2,960,2304]{2,1,0:T(8,128)(2,1)}, bf16[2,960,2304]{2,1,0:T(8,128)(2,1)}, u32[]{:S(2)}, u32[]{:S(2)}) collective-permute-start(bf16[2,960,2304]{2,1,0:T(8,128)(2,1)} %bitcast.11), channel_id=1, source_target_pairs={{0,4},{1,5},{2,6},{3,7},{4,0},{5,1},{6,2},{7,3},{8,12},{9,13},{10,... | collective-permute-start | bytes 26542088 | tf_op jit(solution)/shard_map/ppermute | solution.py:35
  6.0 47.9 %collective-permute-start.7 = (bf16[2,960,2304]{2,1,0:T(8,128)(2,1)}, bf16[2,960,2304]{2,1,0:T(8,128)(2,1)}, u32[]{:S(2)}, u32[]{:S(2)}) collective-permute-start(bf16[2,960,2304]{2,1,0:T(8,128)(2,1)} %bitcast.15), channel_id=1, source_target_pairs={{0,4},{1,5},{2,6},{3,7},{4,0},{5,1},{6,2},{7,3},{8,12},{9,13},{10,... | collective-permute-start | bytes 26542088 | tf_op jit(solution)/shard_map/ppermute | solution.py:35
  6.2 49.8 %collective-permute-start.8 = (bf16[2,960,2304]{2,1,0:T(8,128)(2,1)}, bf16[2,960,2304]{2,1,0:T(8,128)(2,1)}, u32[]{:S(2)}, u32[]{:S(2)}) collective-permute-start(bf16[2,960,2304]{2,1,0:T(8,128)(2,1)} %refs_6_.5), channel_id=1, source_target_pairs={{0,4},{1,5},{2,6},{3,7},{4,0},{5,1},{6,2},{7,3},{8,12},{9,13},{10,... | collective-permute-start | bytes 26542088 | tf_op jit(solution)/shard_map/ppermute | solution.py:35
  6.5 20.5 %all-to-all-start = ((bf16[4,24,2432]{2,1,0:T(8,128)(2,1)}), bf16[4,24,2432]{2,1,0:T(8,128)(2,1)S(1)}, u32[]{:S(2)}, u32[]{:S(2)}) async-start(bf16[4,24,2432]{2,1,0:T(8,128)(2,1)} %bitcast.22), calls=%async_computation | async-start | bytes 933888 | tf_op jit(solution)/shard_map/all_to_all | solution.py:298
  27.1 18.1 %all-to-all-start.1 = ((bf16[4,24,2432]{2,1,0:T(8,128)(2,1)}), bf16[4,24,2432]{2,1,0:T(8,128)(2,1)S(1)}, u32[]{:S(2)}, u32[]{:S(2)}) async-start(bf16[4,24,2432]{2,1,0:T(8,128)(2,1)} %bitcast.7), calls=%async_computation.1 | async-start | bytes 933888 | tf_op jit(solution)/shard_map/all_to_all | solution.py:298
  32.5 11.0 %collective-permute-start.2 = (bf16[72,2432]{1,0:T(8,128)(2,1)S(1)}, bf16[72,2432]{1,0:T(8,128)(2,1)S(1)}, u32[]{:S(2)}, u32[]{:S(2)}) collective-permute-start(bf16[72,2432]{1,0:T(8,128)(2,1)S(1)} %fusion.1.refs_0_), channel_id=1, source_target_pairs={{0,8},{1,9},{2,10},{3,11},{4,20},{5,21},{6,22},{7,23},{8,0},{9,1},... | collective-permute-start | bytes 1050632 | tf_op jit(solution)/shard_map/ppermute | solution.py:35
  34.0 11.4 %collective-permute-start.3 = (bf16[72,2432]{1,0:T(8,128)(2,1)S(1)}, bf16[72,2432]{1,0:T(8,128)(2,1)S(1)}, u32[]{:S(2)}, u32[]{:S(2)}) collective-permute-start(bf16[72,2432]{1,0:T(8,128)(2,1)S(1)} %fusion.1.refs_0_), channel_id=1, source_target_pairs={{0,16},{1,17},{2,18},{3,19},{4,12},{5,13},{6,14},{7,15},{8,24},{9,... | collective-permute-start | bytes 1050632 | tf_op jit(solution)/shard_map/ppermute | solution.py:35
  45.4 60.5 %collective-permute-start.18 = (bf16[48,2432]{1,0:T(8,128)(2,1)S(1)}, bf16[48,2432]{1,0:T(8,128)(2,1)S(1)}, u32[]{:S(2)}, u32[]{:S(2)}) collective-permute-start(bf16[48,2432]{1,0:T(8,128)(2,1)S(1)} %constant_dynamic-update-slice_fusion.refs_0_), channel_id=1, source_target_pairs={{0,16},{1,17},{2,18},{3,19},{4,12},{5,13},{6,14},{7,15},{8,24},{9,... | collective-permute-start | bytes 700424 | tf_op jit(solution)/shard_map/ppermute | solution.py:35
  51.4 54.4 %collective-permute-start.19 = (bf16[48,2432]{1,0:T(8,128)(2,1)S(1)}, bf16[48,2432]{1,0:T(8,128)(2,1)S(1)}, u32[]{:S(2)}, u32[]{:S(2)}) collective-permute-start(bf16[48,2432]{1,0:T(8,128)(2,1)S(1)} %collective-permute-done.1.refs_1_), channel_id=1, source_target_pairs={{0,16},{1,17},{2,18},{3,19},{4,12},{5,13},{6,14},{7,15},{8,24},{9,... | collective-permute-start | bytes 700424 | tf_op jit(solution)/shard_map/ppermute | solution.py:35
  51.5 21.7 %collective-permute-start.12 = (bf16[72,2432]{1,0:T(8,128)(2,1)S(1)}, bf16[72,2432]{1,0:T(8,128)(2,1)S(1)}, u32[]{:S(2)}, u32[]{:S(2)}) collective-permute-start(bf16[72,2432]{1,0:T(8,128)(2,1)S(1)} %fusion.refs_0_), channel_id=1, source_target_pairs={{0,8},{1,9},{2,10},{3,11},{4,20},{5,21},{6,22},{7,23},{8,0},{9,1},... | collective-permute-start | bytes 1050632 | tf_op jit(solution)/shard_map/ppermute | solution.py:35
  53.9 20.8 %collective-permute-start.13 = (bf16[72,2432]{1,0:T(8,128)(2,1)S(1)}, bf16[72,2432]{1,0:T(8,128)(2,1)S(1)}, u32[]{:S(2)}, u32[]{:S(2)}) collective-permute-start(bf16[72,2432]{1,0:T(8,128)(2,1)S(1)} %fusion.refs_0_), channel_id=1, source_target_pairs={{0,16},{1,17},{2,18},{3,19},{4,12},{5,13},{6,14},{7,15},{8,24},{9,... | collective-permute-start | bytes 1050632 | tf_op jit(solution)/shard_map/ppermute | solution.py:35
  55.9 20.7 %collective-permute-start.14 = (bf16[72,2432]{1,0:T(8,128)(2,1)S(1)}, bf16[72,2432]{1,0:T(8,128)(2,1)S(1)}, u32[]{:S(2)}, u32[]{:S(2)}) collective-permute-start(bf16[72,2432]{1,0:T(8,128)(2,1)S(1)} %fusion.refs_0_), channel_id=1, source_target_pairs={{0,24},{1,25},{2,26},{3,27},{4,28},{5,29},{6,30},{7,31},{8,16},{9,... | collective-permute-start | bytes 1050632 | tf_op jit(solution)/shard_map/ppermute | solution.py:35
  73.1 20.0 %collective-permute-start.9 = (bf16[72,2304]{1,0:T(8,128)(2,1)S(1)}, bf16[72,2304]{1,0:T(8,128)(2,1)S(1)}, u32[]{:S(2)}, u32[]{:S(2)}) collective-permute-start(bf16[72,2304]{1,0:T(8,128)(2,1)S(1)} %get-tuple-element.57), channel_id=1, source_target_pairs={{0,8},{1,9},{2,10},{3,11},{4,20},{5,21},{6,22},{7,23},{8,0},{9,1},... | collective-permute-start | bytes 995336 | tf_op jit(solution)/shard_map/ppermute | solution.py:35
  74.7 18.5 %collective-permute-start.10 = (bf16[72,2304]{1,0:T(8,128)(2,1)S(1)}, bf16[72,2304]{1,0:T(8,128)(2,1)S(1)}, u32[]{:S(2)}, u32[]{:S(2)}) collective-permute-start(bf16[72,2304]{1,0:T(8,128)(2,1)S(1)} %get-tuple-element.58), channel_id=1, source_target_pairs={{0,16},{1,17},{2,18},{3,19},{4,12},{5,13},{6,14},{7,15},{8,24},{9,... | collective-permute-start | bytes 995336 | tf_op jit(solution)/shard_map/ppermute | solution.py:35
  76.6 16.5 %collective-permute-start.11 = (bf16[72,2304]{1,0:T(8,128)(2,1)S(1)}, bf16[72,2304]{1,0:T(8,128)(2,1)S(1)}, u32[]{:S(2)}, u32[]{:S(2)}) collective-permute-start(bf16[72,2304]{1,0:T(8,128)(2,1)S(1)} %get-tuple-element.59), channel_id=1, source_target_pairs={{0,24},{1,25},{2,26},{3,27},{4,28},{5,29},{6,30},{7,31},{8,16},{9,... | collective-permute-start | bytes 995336 | tf_op jit(solution)/shard_map/ppermute | solution.py:35
  96.9 24.1 %all-to-all-start.2 = ((bf16[4,24,2304]{2,1,0:T(8,128)(2,1)}), bf16[4,24,2304]{2,1,0:T(8,128)(2,1)S(1)}, u32[]{:S(2)}, u32[]{:S(2)}) async-start(bf16[4,24,2304]{2,1,0:T(8,128)(2,1)} %settle.2), calls=%async_computation.2 | async-start | bytes 884736 | tf_op jit(solution)/shard_map/all_to_all | solution.py:298
  102.4 17.2 %collective-permute-start.15 = (bf16[72,2304]{1,0:T(8,128)(2,1)S(1)}, bf16[72,2304]{1,0:T(8,128)(2,1)S(1)}, u32[]{:S(2)}, u32[]{:S(2)}) collective-permute-start(bf16[72,2304]{1,0:T(8,128)(2,1)S(1)} %get-tuple-element.71), channel_id=1, source_target_pairs={{0,8},{1,9},{2,10},{3,11},{4,20},{5,21},{6,22},{7,23},{8,0},{9,1},... | collective-permute-start | bytes 995336 | tf_op jit(solution)/shard_map/ppermute | solution.py:35
  103.9 15.7 %collective-permute-start.16 = (bf16[72,2304]{1,0:T(8,128)(2,1)S(1)}, bf16[72,2304]{1,0:T(8,128)(2,1)S(1)}, u32[]{:S(2)}, u32[]{:S(2)}) collective-permute-start(bf16[72,2304]{1,0:T(8,128)(2,1)S(1)} %get-tuple-element.72), channel_id=1, source_target_pairs={{0,16},{1,17},{2,18},{3,19},{4,12},{5,13},{6,14},{7,15},{8,24},{9,... | collective-permute-start | bytes 995336 | tf_op jit(solution)/shard_map/ppermute | solution.py:35
  105.9 15.2 %collective-permute-start.17 = (bf16[72,2304]{1,0:T(8,128)(2,1)S(1)}, bf16[72,2304]{1,0:T(8,128)(2,1)}, u32[]{:S(2)}, u32[]{:S(2)}) collective-permute-start(bf16[72,2304]{1,0:T(8,128)(2,1)S(1)} %get-tuple-element.73), channel_id=1, source_target_pairs={{0,24},{1,25},{2,26},{3,27},{4,28},{5,29},{6,30},{7,31},{8,16},{9,... | collective-permute-start | bytes 995336 | tf_op jit(solution)/shard_map/ppermute | solution.py:35
  121.1 9.7 %collective-permute-start.27 = (f32[8,2432]{1,0:T(8,128)S(1)}, f32[8,2432]{1,0:T(8,128)S(1)}, u32[]{:S(2)}, u32[]{:S(2)}) collective-permute-start(f32[8,2432]{1,0:T(8,128)S(1)} %get-tuple-element.89), channel_id=1, source_target_pairs={{0,3},{1,2},{2,1},{3,0},{4,7},{5,6},{6,5},{7,4},{8,11},{9,10},{10,... | collective-permute-start | bytes 233480 | tf_op jit(solution)/shard_map/ppermute | solution.py:35
  127.8 11.7 %collective-permute-start.22 = (bf16[48,2304]{1,0:T(8,128)(2,1)S(1)}, bf16[48,2304]{1,0:T(8,128)(2,1)S(1)}, u32[]{:S(2)}, u32[]{:S(2)}) collective-permute-start(bf16[48,2304]{1,0:T(8,128)(2,1)S(1)} %get-tuple-element.88), channel_id=1, source_target_pairs={{0,24},{1,25},{2,26},{3,27},{4,28},{5,29},{6,30},{7,31},{8,16},{9,... | collective-permute-start | bytes 663560 | tf_op jit(solution)/shard_map/ppermute | solution.py:35
  130.7 9.4 %collective-permute-start.21 = (bf16[48,2304]{1,0:T(8,128)(2,1)S(1)}, bf16[48,2304]{1,0:T(8,128)(2,1)S(1)}, u32[]{:S(2)}, u32[]{:S(2)}) collective-permute-start(bf16[48,2304]{1,0:T(8,128)(2,1)S(1)} %get-tuple-element.87), channel_id=1, source_target_pairs={{0,16},{1,17},{2,18},{3,19},{4,12},{5,13},{6,14},{7,15},{8,24},{9,... | collective-permute-start | bytes 663560 | tf_op jit(solution)/shard_map/ppermute | solution.py:35
  131.4 18.4 %all-to-all-start.3 = ((bf16[4,24,2304]{2,1,0:T(8,128)(2,1)}), bf16[4,24,2304]{2,1,0:T(8,128)(2,1)S(1)}, u32[]{:S(2)}, u32[]{:S(2)}) async-start(bf16[4,24,2304]{2,1,0:T(8,128)(2,1)} %settle.3), calls=%async_computation.3 | async-start | bytes 884736 | tf_op jit(solution)/shard_map/all_to_all | solution.py:298
  140.8 9.7 %collective-permute-start.24 = (bf16[24,2304]{1,0:T(8,128)(2,1)S(1)}, bf16[24,2304]{1,0:T(8,128)(2,1)S(1)}, u32[]{:S(2)}, u32[]{:S(2)}) collective-permute-start(bf16[24,2304]{1,0:T(8,128)(2,1)S(1)} %get-tuple-element.90), channel_id=1, source_target_pairs={{0,4},{1,5},{2,6},{3,7},{4,0},{5,1},{6,2},{7,3},{8,12},{9,13},{10,... | collective-permute-start | bytes 331784 | tf_op jit(solution)/shard_map/ppermute | solution.py:35
  (23 other events, 107.2 us)

commit v3 on v2

--- a/solution.py
+++ b/solution.py
@@ -246,30 +246,33 @@
     )(*parts)
 
 
-def combine_kernel(tokens, weights, *refs):
-    parts, out = refs[:-1], refs[-1]
+def combine_kernel(planes, tokens, weights, early, home, sibling_home, *refs):
+    late, out = refs[:-1], refs[-1]
+    z = lax.axis_index("expert")
     mixed = jnp.zeros(tokens.shape, jnp.float32)
-    start = 0
-    for part in parts:
-        stop = start + part.shape[0]
-        weight = weights[start:stop].T
+    half = (planes + 1) * CAP
+    parts = [(early, 0), (home, planes * CAP), (sibling_home, half + planes * CAP)]
+    for j, part in enumerate(late):
+        plane = lax.rem(z + planes - 1 - j, planes)
+        parts.append((part, pl.multiple_of(half + plane * CAP, 8)))
+    for part, start in parts:
+        weight = weights[pl.ds(start, part.shape[0])].T
         high = weight.astype(jnp.bfloat16)
         low = (weight - high.astype(jnp.float32)).astype(jnp.bfloat16)
         for factor in (low, high):
             mixed = mixed + jnp.dot(factor, part[...], preferred_element_type=jnp.float32)
-        start = stop
     out[...] = (tokens[...].astype(jnp.float32) + mixed).astype(jnp.bfloat16)
 
 
-def combine(tokens, weights, parts):
+def combine(tokens, weights, early, home, sibling_home, late):
     vmem = pl.BlockSpec(memory_space=pltpu.VMEM)
     return pl.pallas_call(
-        combine_kernel,
+        functools.partial(combine_kernel, len(late) + 1),
         out_shape=jax.ShapeDtypeStruct(tokens.shape, jnp.bfloat16),
-        in_specs=[vmem] * (2 + len(parts)),
+        in_specs=[vmem] * (5 + len(late)),
         out_specs=vmem,
         name="combine",
-    )(tokens, weights, *parts)
+    )(tokens, weights, early, home, sibling_home, *late)
 
 
 def added(*arrays):
@@ -288,7 +291,7 @@
     sibling, sibling_home = swap(other, t=1), swap(other_home, t=1)
     stored = (jnp.swapaxes(w_gate, 1, 2), jnp.swapaxes(w_up, 1, 2), w_down)
 
-    tied = lax.optimization_barrier(stored + (sibling,))
+    tied = lax.optimization_barrier(stored + (sibling, sibling_home))
     far = tuple(pltpu.with_memory_space_constraint(swap(array, t=1), pltpu.HBM) for array in tied[:3])
 
     z = lax.axis_index("expert")
@@ -296,6 +299,9 @@
 
     def exchange(rows):
         return lax.all_to_all(rows, "expert", split_axis=0, concat_axis=0, tiled=True)
+
+    def turn(block, step):
+        return lax.ppermute(block, "expert", [(i, (i + step) % planes) for i in range(planes)])
 
     def outward(rows):
         return lax.dynamic_slice_in_dim(jnp.concatenate([rows, rows]), (z + 1) * CAP, others)
@@ -329,16 +335,16 @@
     early = exchange(early).reshape(planes * CAP, width)
     *partial, pool = ffn(home, stored + far, pool)
     early, *late = together([early] + late, pool)
-    late = settle(late, planes)
+    late = added(*late)
     partial = together(partial, early, late)
-    late = exchange(late).reshape(planes * CAP, width)
     home = added(*back(partial))
+    late = [turn(late[(j - 1) * CAP : j * CAP], j) for j in range(1, planes)]
     pool = tie(pool, early)
     for axis in ("z", "t", "d"):
         size = lax.axis_size({"t": "tensor", "z": "expert", "d": "dp"}[axis])
         pool = sum([swap(pool, **{axis: step}) for step in range(1, size)], pool)
-    parts = (early, home[:CAP], swap(late, t=1), swap(home[CAP:], t=1))
-    embedded = combine(tokens, weights, parts)
+    late = [swap(block, t=1) for block in late]
+    embedded = combine(tokens, weights, early, home[:CAP], swap(home[CAP:], t=1), late)
 
     pooled = pool[:, :width] / pool[:, width : width + 1]
     return (embedded, pooled)

time: 156 us -> 146 us (0.936)
  waiting for transfers between devices: 36.3 us -> 29.7 us
  Pallas kernels: 55.1 us -> 53.2 us
  local copies, waits for them, and re-layouts: 7.76 us -> 6.13 us
    ppermute x32 -> x34, waiting for transfers between devices: 28.9 us -> 20.4 us  [swap(): return lax.ppermute(x, AXES, pairs)]
    all_to_all x4 -> x3, starting transfers between devices: 21.9 us -> 14.9 us  [exchange(): lax.all_to_all(rows, 'expert', split_axis=0, concat_axis=0, tiled=True)]
    ppermute x0 -> x3, starting transfers between devices: none -> 6.91 us  [turn(): lax.ppermute(block, 'expert', [(i, (i + step) % planes) for i in range(pl...]
    pallas_call x2 -> x1, Pallas kernels: 4.42 us -> 2.2 us  [settle(): pl.pallas_call(functools.partial(settle_kernel, planes), out_shape=jax.Sh...]
    unnamed x23, local copies, waits for them, and re-layouts: 6.97 us -> 5.31 us
    all_to_all x4 -> x3, waiting for transfers between devices: 7.4 us -> 8.45 us  [exchange(): lax.all_to_all(rows, 'expert', split_axis=0, concat_axis=0, tiled=True)]
    ppermute x32 -> x34, starting transfers between devices: 32.2 us -> 31.6 us  [swap(): return lax.ppermute(x, AXES, pairs)]
  transfers between devices with their start and end apart: 36 -> 40, of which waited for: 11 -> 12; matrix products, arithmetic and copies ran while one was open for 2% -> 3% of each run, Pallas kernels for 32% -> 32%
where the time goes in v3:
time: 146 us
  starting transfers between devices  53.4 us (37%)
  Pallas kernels  53.2 us (36%)
  waiting for transfers between devices  29.7 us (20%)
  local copies, waits for them, and re-layouts  6.13 us (4%)
  other arithmetic  2.51 us (2%)
    pallas_call x3, Pallas kernels, ffn(): pl.pallas_call(functools.partial(ffn_kernel, pieces, tile, cols, depth, p...  45 us
    ppermute x34, starting transfers between devices, swap(): return lax.ppermute(x, AXES, pairs)  31.6 us
    ppermute x34, waiting for transfers between devices, swap(): return lax.ppermute(x, AXES, pairs)  20.4 us
    all_to_all x3, starting transfers between devices, exchange(): lax.all_to_all(rows, 'expert', split_axis=0, concat_axis=0, tiled=True)  14.9 us
    all_to_all x3, waiting for transfers between devices, exchange(): lax.all_to_all(rows, 'expert', split_axis=0, concat_axis=0, tiled=True)  8.45 us
    ppermute x3, starting transfers between devices, turn(): lax.ppermute(block, 'expert', [(i, (i + step) % planes) for i in range(pl...  6.91 us
    unnamed x23, local copies, waits for them, and re-layouts  5.31 us
    pallas_call x1, Pallas kernels, combine(): pl.pallas_call(functools.partial(combine_kernel, len(late) + 1), out_shap...  3.19 us
  transfers between devices with their start and end apart: 40, of which 12 were waited for; matrix products, arithmetic and copies ran while one was open for 3% of the time, Pallas kernels for 32%

profile of v3, /device:TPU:0, one launch (start us, length us, event | category | flops | bytes accessed | tf_op | source)
XLA Modules:
  0.0 145.9 jit_solution(14885004109728844224)
XLA Ops:
  0.6 2.8 %prep.1 = (bf16[96,2432]{1,0:T(8,128)(2,1)}, bf16[24,2432]{1,0:T(8,128)(2,1)}, bf16[96,2432]{1,0:T(8,128)(2,1)}, bf16[24,2432]{1,0:T(8,128)(2,1)}, f32[240,64]{1,0:T(8,128)}, /*index=5*/f32[8,2432]{1,0:T(8,128)}) custom-call(bf16[64,2304]{1,0:T(8,128)(2,1)} %tokens.3, s32[2,64]{1,0:T(2,128)} %bitcast.21, f32[2,64]{1,0:T(2,128)} %bitcast.22, s32[1,64]{1,0:T(1,128)} %bitcast.23), custom_call_target="tpu_custom_call" | custom-call | tf_op jit(solution)/shard_map/prep/pallas_call | solution.py:100
  3.9 1.8 %collective-permute-done = bf16[24,2432]{1,0:T(8,128)(2,1)S(1)} collective-permute-done((bf16[24,2432]{1,0:T(8,128)(2,1)}, bf16[24,2432]{1,0:T(8,128)(2,1)S(1)}, u32[]{:S(2)}, u32[]{:S(2)}) %collective-permute-start) | collective-permute-done | bytes 116768 | tf_op jit(solution)/shard_map/ppermute | solution.py:35
  6.6 6.1 %all-to-all-start = ((bf16[4,24,2432]{2,1,0:T(8,128)(2,1)}), bf16[4,24,2432]{2,1,0:T(8,128)(2,1)S(1)}, u32[]{:S(2)}, u32[]{:S(2)}) async-start(bf16[4,24,2432]{2,1,0:T(8,128)(2,1)} %bitcast.20), calls=%async_computation | async-start | bytes 933888 | tf_op jit(solution)/shard_map/all_to_all | solution.py:301
  15.2 4.6 %collective-permute-done.1.refs_1_ = bf16[48,2432]{1,0:T(8,128)(2,1)S(1)} collective-permute-done((bf16[48,2432]{1,0:T(8,128)(2,1)S(1)}, bf16[48,2432]{1,0:T(8,128)(2,1)S(1)}, u32[]{:S(2)}, u32[]{:S(2)}) %collective-permute-start.1) | collective-permute-done | bytes 233504 | tf_op jit(solution)/shard_map/ppermute | solution.py:35
  19.8 6.7 %all-to-all-done = bf16[4,24,2432]{2,1,0:T(8,128)(2,1)S(1)} async-done(((bf16[4,24,2432]{2,1,0:T(8,128)(2,1)}), bf16[4,24,2432]{2,1,0:T(8,128)(2,1)S(1)}, u32[]{:S(2)}, u32[]{:S(2)}) %all-to-all-start) | async-done | bytes 466976 | tf_op jit(solution)/shard_map/all_to_all | solution.py:301
  26.7 3.5 %all-to-all-start.1 = ((bf16[4,24,2432]{2,1,0:T(8,128)(2,1)}), bf16[4,24,2432]{2,1,0:T(8,128)(2,1)S(1)}, u32[]{:S(2)}, u32[]{:S(2)}) async-start(bf16[4,24,2432]{2,1,0:T(8,128)(2,1)} %bitcast.7), calls=%async_computation.1 | async-start | bytes 933888 | tf_op jit(solution)/shard_map/all_to_all | solution.py:301
  33.2 8.0 %collective-permute-done.2.refs_1_ = bf16[72,2432]{1,0:T(8,128)(2,1)S(1)} collective-permute-done((bf16[72,2432]{1,0:T(8,128)(2,1)S(1)}, bf16[72,2432]{1,0:T(8,128)(2,1)S(1)}, u32[]{:S(2)}, u32[]{:S(2)}) %collective-permute-start.2) | collective-permute-done | bytes 350240 | tf_op jit(solution)/shard_map/ppermute | solution.py:35
  41.3 1.7 %all-to-all-done.1 = bf16[4,24,2432]{2,1,0:T(8,128)(2,1)S(1)} async-done(((bf16[4,24,2432]{2,1,0:T(8,128)(2,1)}), bf16[4,24,2432]{2,1,0:T(8,128)(2,1)S(1)}, u32[]{:S(2)}, u32[]{:S(2)}) %all-to-all-start.1) | async-done | bytes 466976 | tf_op jit(solution)/shard_map/all_to_all | solution.py:301
  44.8 4.0 %collective-permute-done.4.refs_3_ = bf16[72,2432]{1,0:T(8,128)(2,1)S(1)} collective-permute-done((bf16[72,2432]{1,0:T(8,128)(2,1)S(1)}, bf16[72,2432]{1,0:T(8,128)(2,1)S(1)}, u32[]{:S(2)}, u32[]{:S(2)}) %collective-permute-start.4) | collective-permute-done | bytes 350240 | tf_op jit(solution)/shard_map/ppermute | solution.py:35
  48.8 2.5 %collective-permute-start.12 = (bf16[72,2432]{1,0:T(8,128)(2,1)S(1)}, bf16[72,2432]{1,0:T(8,128)(2,1)S(1)}, u32[]{:S(2)}, u32[]{:S(2)}) collective-permute-start(bf16[72,2432]{1,0:T(8,128)(2,1)S(1)} %fusion.refs_0_), channel_id=1, source_target_pairs={{0,8},{1,9},{2,10},{3,11},{4,20},{5,21},{6,22},{7,23},{8,0},{9,1},... | collective-permute-start | bytes 1050632 | tf_op jit(solution)/shard_map/ppermute | solution.py:35
  51.3 2.0 %collective-permute-start.13 = (bf16[72,2432]{1,0:T(8,128)(2,1)S(1)}, bf16[72,2432]{1,0:T(8,128)(2,1)S(1)}, u32[]{:S(2)}, u32[]{:S(2)}) collective-permute-start(bf16[72,2432]{1,0:T(8,128)(2,1)S(1)} %fusion.refs_0_), channel_id=1, source_target_pairs={{0,16},{1,17},{2,18},{3,19},{4,12},{5,13},{6,14},{7,15},{8,24},{9,... | collective-permute-start | bytes 1050632 | tf_op jit(solution)/shard_map/ppermute | solution.py:35
  54.2 15.6 %ffn.3 = (bf16[72,2304]{1,0:T(8,128)(2,1)S(1)}, bf16[72,2304]{1,0:T(8,128)(2,1)S(1)}, bf16[72,2304]{1,0:T(8,128)(2,1)S(1)}, bf16[72,2304]{1,0:T(8,128)(2,1)S(1)}, f32[8,2432]{1,0:T(8,128)S(1)}) custom-call(f32[8,2432]{1,0:T(8,128)S(1)} %copy-done.1, bf16[72,2432]{1,0:T(8,128)(2,1)S(1)} %fusion.1.refs_0_, ...), custom_call_target="tpu_custom_call" | custom-call | flops 8493465600 | bytes 26542080 | tf_op jit(solution)/shard_map/ffn/pallas_call | solution.py:203
  71.4 2.0 %collective-permute-start.10 = (bf16[72,2304]{1,0:T(8,128)(2,1)S(1)}, bf16[72,2304]{1,0:T(8,128)(2,1)S(1)}, u32[]{:S(2)}, u32[]{:S(2)}) collective-permute-start(bf16[72,2304]{1,0:T(8,128)(2,1)S(1)} %get-tuple-element.58), channel_id=1, source_target_pairs={{0,16},{1,17},{2,18},{3,19},{4,12},{5,13},{6,14},{7,15},{8,24},{9,... | collective-permute-start | bytes 995336 | tf_op jit(solution)/shard_map/ppermute | solution.py:35
  73.4 15.8 %ffn.4 = (bf16[72,2304]{1,0:T(8,128)(2,1)S(1)}, bf16[72,2304]{1,0:T(8,128)(2,1)S(1)}, bf16[72,2304]{1,0:T(8,128)(2,1)S(1)}, bf16[72,2304]{1,0:T(8,128)(2,1)S(1)}, f32[8,2432]{1,0:T(8,128)S(1)}) custom-call(f32[8,2432]{1,0:T(8,128)S(1)} %get-tuple-element.60.pool_in, bf16[72,2432]{1,0:T(8,128)(2,1)S(1)} %fusion.refs_0_, ...), custom_call_target="tpu_custom_call" | custom-call | flops 8493465600 | bytes 26542080 | tf_op jit(solution)/shard_map/ffn/pallas_call | solution.py:203
  90.6 2.2 %settle.1 = bf16[4,24,2304]{2,1,0:T(8,128)(2,1)} custom-call(bf16[72,2304]{1,0:T(8,128)(2,1)} %copy-done, bf16[72,2304]{1,0:T(8,128)(2,1)} %copy-done.4, bf16[72,2304]{1,0:T(8,128)(2,1)} %copy-done.5, bf16[72,2304]{1,0:T(8,128)(2,1)} %copy-done.6), custom_call_target="tpu_custom_call" | custom-call | tf_op jit(solution)/shard_map/settle/pallas_call | solution.py:240
  92.8 5.4 %all-to-all-start.2 = ((bf16[4,24,2304]{2,1,0:T(8,128)(2,1)}), bf16[4,24,2304]{2,1,0:T(8,128)(2,1)}, u32[]{:S(2)}, u32[]{:S(2)}) async-start(bf16[4,24,2304]{2,1,0:T(8,128)(2,1)} %settle.1), calls=%async_computation.2 | async-start | bytes 884736 | tf_op jit(solution)/shard_map/all_to_all | solution.py:301
  99.7 2.0 %collective-permute-start.16 = (bf16[72,2304]{1,0:T(8,128)(2,1)S(1)}, bf16[72,2304]{1,0:T(8,128)(2,1)S(1)}, u32[]{:S(2)}, u32[]{:S(2)}) collective-permute-start(bf16[72,2304]{1,0:T(8,128)(2,1)S(1)} %get-tuple-element.72), channel_id=1, source_target_pairs={{0,16},{1,17},{2,18},{3,19},{4,12},{5,13},{6,14},{7,15},{8,24},{9,... | collective-permute-start | bytes 995336 | tf_op jit(solution)/shard_map/ppermute | solution.py:35
  101.7 13.7 %ffn.5 = (bf16[48,2304]{1,0:T(8,128)(2,1)S(1)}, bf16[48,2304]{1,0:T(8,128)(2,1)S(1)}, bf16[48,2304]{1,0:T(8,128)(2,1)S(1)}, bf16[48,2304]{1,0:T(8,128)(2,1)S(1)}, f32[8,2432]{1,0:T(8,128)S(1)}) custom-call(f32[8,2432]{1,0:T(8,128)S(1)} %get-tuple-element.62.pool_in, bf16[48,2432]{1,0:T(8,128)(2,1)S(1)} %constant_dynamic-update-slice_fusion.refs_0_, ...), custom_call_target="tpu_custom_call" | custom-call | flops 5096079360 | bytes 26542080 | tf_op jit(solution)/shard_map/ffn/pallas_call | solution.py:203
  116.9 3.8 %collective-permute-start.32 = (f32[8,2432]{1,0:T(8,128)S(1)}, f32[8,2432]{1,0:T(8,128)S(1)}, u32[]{:S(2)}, u32[]{:S(2)}) collective-permute-start(f32[8,2432]{1,0:T(8,128)S(1)} %get-tuple-element.89), channel_id=1, source_target_pairs={{0,3},{1,2},{2,1},{3,0},{4,7},{5,6},{6,5},{7,4},{8,11},{9,10},{10,... | collective-permute-start | bytes 233480 | tf_op jit(solution)/shard_map/ppermute | solution.py:35
  122.7 3.0 %collective-permute-start.22 = (bf16[48,2304]{1,0:T(8,128)(2,1)S(1)}, bf16[48,2304]{1,0:T(8,128)(2,1)S(1)}, u32[]{:S(2)}, u32[]{:S(2)}) collective-permute-start(bf16[48,2304]{1,0:T(8,128)(2,1)S(1)} %get-tuple-element.88), channel_id=1, source_target_pairs={{0,24},{1,25},{2,26},{3,27},{4,28},{5,29},{6,30},{7,31},{8,16},{9,... | collective-permute-start | bytes 663560 | tf_op jit(solution)/shard_map/ppermute | solution.py:35
  127.9 2.9 %collective-permute-start.26 = (bf16[24,2304]{1,0:T(8,128)(2,1)S(1)}, bf16[24,2304]{1,0:T(8,128)(2,1)S(1)}, u32[]{:S(2)}, u32[]{:S(2)}) collective-permute-start(bf16[24,2304]{1,0:T(8,128)(2,1)S(1)} %get-tuple-element.91), channel_id=1, source_target_pairs={{0,2},{1,3},{2,0},{3,1},{4,6},{5,7},{6,4},{7,5},{8,10},{9,11},{10,... | collective-permute-start | bytes 331784 | tf_op jit(solution)/shard_map/ppermute | solution.py:304
  130.8 2.5 %collective-permute-start.28 = (bf16[24,2304]{1,0:T(8,128)(2,1)S(1)}, bf16[24,2304]{1,0:T(8,128)(2,1)S(1)}, u32[]{:S(2)}, u32[]{:S(2)}) collective-permute-start(bf16[24,2304]{1,0:T(8,128)(2,1)S(1)} %get-tuple-element.90), channel_id=1, source_target_pairs={{0,3},{1,0},{2,1},{3,2},{4,7},{5,4},{6,5},{7,6},{8,11},{9,8},{10,9... | collective-permute-start | bytes 331784 | tf_op jit(solution)/shard_map/ppermute | solution.py:304
  133.3 3.0 %collective-permute-start.36 = (f32[8,2432]{1,0:T(8,128)S(1)}, f32[8,2432]{1,0:T(8,128)S(1)}, u32[]{:S(2)}, u32[]{:S(2)}) collective-permute-start(f32[8,2432]{1,0:T(8,128)S(1)} %add.58), channel_id=1, source_target_pairs={{0,24},{1,25},{2,26},{3,27},{4,28},{5,29},{6,30},{7,31},{8,16},{9,... | collective-permute-start | bytes 233480 | tf_op jit(solution)/shard_map/ppermute | solution.py:35
  142.7 3.2 %combine.1 = bf16[64,2304]{1,0:T(8,128)(2,1)} custom-call(bf16[64,2304]{1,0:T(8,128)(2,1)} %tokens.3, f32[240,64]{1,0:T(8,128)} %get-tuple-element.46.weights, bf16[96,2304]{1,0:T(8,128)(2,1)} %bitcast.9.early, bf16[24,2304]{1,0:T(8,128)(2,1)} %get-tuple-element.94.home, bf16[24,2304]{1,0:T(8,128)(2,1)} %copy-done.10, bf16[24,2304]{1,0:T(8,128)(2,1)} %copy-done.7, ...), custom_call_target="tpu_custom_call" | custom-call | tf_op jit(solution)/shard_map/combine/pallas_call | solution.py:269
  (97 shorter events, 26.5 us)
Async XLA Ops:
  5.8 43.0 %collective-permute-start.6 = (bf16[2,960,2304]{2,1,0:T(8,128)(2,1)}, bf16[2,960,2304]{2,1,0:T(8,128)(2,1)}, u32[]{:S(2)}, u32[]{:S(2)}) collective-permute-start(bf16[2,960,2304]{2,1,0:T(8,128)(2,1)} %bitcast.10), channel_id=1, source_target_pairs={{0,4},{1,5},{2,6},{3,7},{4,0},{5,1},{6,2},{7,3},{8,12},{9,13},{10,... | collective-permute-start | bytes 26542088 | tf_op jit(solution)/shard_map/ppermute | solution.py:35
  6.1 45.1 %collective-permute-start.7 = (bf16[2,960,2304]{2,1,0:T(8,128)(2,1)}, bf16[2,960,2304]{2,1,0:T(8,128)(2,1)}, u32[]{:S(2)}, u32[]{:S(2)}) collective-permute-start(bf16[2,960,2304]{2,1,0:T(8,128)(2,1)} %bitcast.14), channel_id=1, source_target_pairs={{0,4},{1,5},{2,6},{3,7},{4,0},{5,1},{6,2},{7,3},{8,12},{9,13},{10,... | collective-permute-start | bytes 26542088 | tf_op jit(solution)/shard_map/ppermute | solution.py:35
  6.3 47.0 %collective-permute-start.8 = (bf16[2,960,2304]{2,1,0:T(8,128)(2,1)}, bf16[2,960,2304]{2,1,0:T(8,128)(2,1)}, u32[]{:S(2)}, u32[]{:S(2)}) collective-permute-start(bf16[2,960,2304]{2,1,0:T(8,128)(2,1)} %refs_6_.5), channel_id=1, source_target_pairs={{0,4},{1,5},{2,6},{3,7},{4,0},{5,1},{6,2},{7,3},{8,12},{9,13},{10,... | collective-permute-start | bytes 26542088 | tf_op jit(solution)/shard_map/ppermute | solution.py:35
  6.6 19.9 %all-to-all-start = ((bf16[4,24,2432]{2,1,0:T(8,128)(2,1)}), bf16[4,24,2432]{2,1,0:T(8,128)(2,1)S(1)}, u32[]{:S(2)}, u32[]{:S(2)}) async-start(bf16[4,24,2432]{2,1,0:T(8,128)(2,1)} %bitcast.20), calls=%async_computation | async-start | bytes 933888 | tf_op jit(solution)/shard_map/all_to_all | solution.py:301
  26.7 16.4 %all-to-all-start.1 = ((bf16[4,24,2432]{2,1,0:T(8,128)(2,1)}), bf16[4,24,2432]{2,1,0:T(8,128)(2,1)S(1)}, u32[]{:S(2)}, u32[]{:S(2)}) async-start(bf16[4,24,2432]{2,1,0:T(8,128)(2,1)} %bitcast.7), calls=%async_computation.1 | async-start | bytes 933888 | tf_op jit(solution)/shard_map/all_to_all | solution.py:301
  30.1 11.1 %collective-permute-start.2 = (bf16[72,2432]{1,0:T(8,128)(2,1)S(1)}, bf16[72,2432]{1,0:T(8,128)(2,1)S(1)}, u32[]{:S(2)}, u32[]{:S(2)}) collective-permute-start(bf16[72,2432]{1,0:T(8,128)(2,1)S(1)} %fusion.1.refs_0_), channel_id=1, source_target_pairs={{0,8},{1,9},{2,10},{3,11},{4,20},{5,21},{6,22},{7,23},{8,0},{9,1},... | collective-permute-start | bytes 1050632 | tf_op jit(solution)/shard_map/ppermute | solution.py:35
  31.7 11.5 %collective-permute-start.3 = (bf16[72,2432]{1,0:T(8,128)(2,1)S(1)}, bf16[72,2432]{1,0:T(8,128)(2,1)S(1)}, u32[]{:S(2)}, u32[]{:S(2)}) collective-permute-start(bf16[72,2432]{1,0:T(8,128)(2,1)S(1)} %fusion.1.refs_0_), channel_id=1, source_target_pairs={{0,16},{1,17},{2,18},{3,19},{4,12},{5,13},{6,14},{7,15},{8,24},{9,... | collective-permute-start | bytes 1050632 | tf_op jit(solution)/shard_map/ppermute | solution.py:35
  43.2 58.5 %collective-permute-start.18 = (bf16[48,2432]{1,0:T(8,128)(2,1)S(1)}, bf16[48,2432]{1,0:T(8,128)(2,1)S(1)}, u32[]{:S(2)}, u32[]{:S(2)}) collective-permute-start(bf16[48,2432]{1,0:T(8,128)(2,1)S(1)} %constant_dynamic-update-slice_fusion.refs_0_), channel_id=1, source_target_pairs={{0,16},{1,17},{2,18},{3,19},{4,12},{5,13},{6,14},{7,15},{8,24},{9,... | collective-permute-start | bytes 700424 | tf_op jit(solution)/shard_map/ppermute | solution.py:35
  48.8 52.9 %collective-permute-start.19 = (bf16[48,2432]{1,0:T(8,128)(2,1)S(1)}, bf16[48,2432]{1,0:T(8,128)(2,1)S(1)}, u32[]{:S(2)}, u32[]{:S(2)}) collective-permute-start(bf16[48,2432]{1,0:T(8,128)(2,1)S(1)} %collective-permute-done.1.refs_1_), channel_id=1, source_target_pairs={{0,16},{1,17},{2,18},{3,19},{4,12},{5,13},{6,14},{7,15},{8,24},{9,... | collective-permute-start | bytes 700424 | tf_op jit(solution)/shard_map/ppermute | solution.py:35
  48.8 21.0 %collective-permute-start.12 = (bf16[72,2432]{1,0:T(8,128)(2,1)S(1)}, bf16[72,2432]{1,0:T(8,128)(2,1)S(1)}, u32[]{:S(2)}, u32[]{:S(2)}) collective-permute-start(bf16[72,2432]{1,0:T(8,128)(2,1)S(1)} %fusion.refs_0_), channel_id=1, source_target_pairs={{0,8},{1,9},{2,10},{3,11},{4,20},{5,21},{6,22},{7,23},{8,0},{9,1},... | collective-permute-start | bytes 1050632 | tf_op jit(solution)/shard_map/ppermute | solution.py:35
  51.3 20.1 %collective-permute-start.13 = (bf16[72,2432]{1,0:T(8,128)(2,1)S(1)}, bf16[72,2432]{1,0:T(8,128)(2,1)S(1)}, u32[]{:S(2)}, u32[]{:S(2)}) collective-permute-start(bf16[72,2432]{1,0:T(8,128)(2,1)S(1)} %fusion.refs_0_), channel_id=1, source_target_pairs={{0,16},{1,17},{2,18},{3,19},{4,12},{5,13},{6,14},{7,15},{8,24},{9,... | collective-permute-start | bytes 1050632 | tf_op jit(solution)/shard_map/ppermute | solution.py:35
  53.3 20.1 %collective-permute-start.14 = (bf16[72,2432]{1,0:T(8,128)(2,1)S(1)}, bf16[72,2432]{1,0:T(8,128)(2,1)S(1)}, u32[]{:S(2)}, u32[]{:S(2)}) collective-permute-start(bf16[72,2432]{1,0:T(8,128)(2,1)S(1)} %fusion.refs_0_), channel_id=1, source_target_pairs={{0,24},{1,25},{2,26},{3,27},{4,28},{5,29},{6,30},{7,31},{8,16},{9,... | collective-permute-start | bytes 1050632 | tf_op jit(solution)/shard_map/ppermute | solution.py:35
  69.8 19.4 %collective-permute-start.9 = (bf16[72,2304]{1,0:T(8,128)(2,1)S(1)}, bf16[72,2304]{1,0:T(8,128)(2,1)S(1)}, u32[]{:S(2)}, u32[]{:S(2)}) collective-permute-start(bf16[72,2304]{1,0:T(8,128)(2,1)S(1)} %get-tuple-element.57), channel_id=1, source_target_pairs={{0,8},{1,9},{2,10},{3,11},{4,20},{5,21},{6,22},{7,23},{8,0},{9,1},... | collective-permute-start | bytes 995336 | tf_op jit(solution)/shard_map/ppermute | solution.py:35
  71.4 17.8 %collective-permute-start.10 = (bf16[72,2304]{1,0:T(8,128)(2,1)S(1)}, bf16[72,2304]{1,0:T(8,128)(2,1)S(1)}, u32[]{:S(2)}, u32[]{:S(2)}) collective-permute-start(bf16[72,2304]{1,0:T(8,128)(2,1)S(1)} %get-tuple-element.58), channel_id=1, source_target_pairs={{0,16},{1,17},{2,18},{3,19},{4,12},{5,13},{6,14},{7,15},{8,24},{9,... | collective-permute-start | bytes 995336 | tf_op jit(solution)/shard_map/ppermute | solution.py:35
  73.4 15.8 %collective-permute-start.11 = (bf16[72,2304]{1,0:T(8,128)(2,1)S(1)}, bf16[72,2304]{1,0:T(8,128)(2,1)S(1)}, u32[]{:S(2)}, u32[]{:S(2)}) collective-permute-start(bf16[72,2304]{1,0:T(8,128)(2,1)S(1)} %get-tuple-element.59), channel_id=1, source_target_pairs={{0,24},{1,25},{2,26},{3,27},{4,28},{5,29},{6,30},{7,31},{8,16},{9,... | collective-permute-start | bytes 995336 | tf_op jit(solution)/shard_map/ppermute | solution.py:35
  92.8 24.0 %all-to-all-start.2 = ((bf16[4,24,2304]{2,1,0:T(8,128)(2,1)}), bf16[4,24,2304]{2,1,0:T(8,128)(2,1)}, u32[]{:S(2)}, u32[]{:S(2)}) async-start(bf16[4,24,2304]{2,1,0:T(8,128)(2,1)} %settle.1), calls=%async_computation.2 | async-start | bytes 884736 | tf_op jit(solution)/shard_map/all_to_all | solution.py:301
  98.2 17.2 %collective-permute-start.15 = (bf16[72,2304]{1,0:T(8,128)(2,1)S(1)}, bf16[72,2304]{1,0:T(8,128)(2,1)S(1)}, u32[]{:S(2)}, u32[]{:S(2)}) collective-permute-start(bf16[72,2304]{1,0:T(8,128)(2,1)S(1)} %get-tuple-element.71), channel_id=1, source_target_pairs={{0,8},{1,9},{2,10},{3,11},{4,20},{5,21},{6,22},{7,23},{8,0},{9,1},... | collective-permute-start | bytes 995336 | tf_op jit(solution)/shard_map/ppermute | solution.py:35
  99.7 15.7 %collective-permute-start.16 = (bf16[72,2304]{1,0:T(8,128)(2,1)S(1)}, bf16[72,2304]{1,0:T(8,128)(2,1)S(1)}, u32[]{:S(2)}, u32[]{:S(2)}) collective-permute-start(bf16[72,2304]{1,0:T(8,128)(2,1)S(1)} %get-tuple-element.72), channel_id=1, source_target_pairs={{0,16},{1,17},{2,18},{3,19},{4,12},{5,13},{6,14},{7,15},{8,24},{9,... | collective-permute-start | bytes 995336 | tf_op jit(solution)/shard_map/ppermute | solution.py:35
  101.7 15.2 %collective-permute-start.17 = (bf16[72,2304]{1,0:T(8,128)(2,1)S(1)}, bf16[72,2304]{1,0:T(8,128)(2,1)}, u32[]{:S(2)}, u32[]{:S(2)}) collective-permute-start(bf16[72,2304]{1,0:T(8,128)(2,1)S(1)} %get-tuple-element.73), channel_id=1, source_target_pairs={{0,24},{1,25},{2,26},{3,27},{4,28},{5,29},{6,30},{7,31},{8,16},{9,... | collective-permute-start | bytes 995336 | tf_op jit(solution)/shard_map/ppermute | solution.py:35
  116.9 8.8 %collective-permute-start.32 = (f32[8,2432]{1,0:T(8,128)S(1)}, f32[8,2432]{1,0:T(8,128)S(1)}, u32[]{:S(2)}, u32[]{:S(2)}) collective-permute-start(f32[8,2432]{1,0:T(8,128)S(1)} %get-tuple-element.89), channel_id=1, source_target_pairs={{0,3},{1,2},{2,1},{3,0},{4,7},{5,6},{6,5},{7,4},{8,11},{9,10},{10,... | collective-permute-start | bytes 233480 | tf_op jit(solution)/shard_map/ppermute | solution.py:35
  122.7 8.1 %collective-permute-start.22 = (bf16[48,2304]{1,0:T(8,128)(2,1)S(1)}, bf16[48,2304]{1,0:T(8,128)(2,1)S(1)}, u32[]{:S(2)}, u32[]{:S(2)}) collective-permute-start(bf16[48,2304]{1,0:T(8,128)(2,1)S(1)} %get-tuple-element.88), channel_id=1, source_target_pairs={{0,24},{1,25},{2,26},{3,27},{4,28},{5,29},{6,30},{7,31},{8,16},{9,... | collective-permute-start | bytes 663560 | tf_op jit(solution)/shard_map/ppermute | solution.py:35
  125.7 10.6 %collective-permute-start.20 = (bf16[48,2304]{1,0:T(8,128)(2,1)S(1)}, bf16[48,2304]{1,0:T(8,128)(2,1)S(1)}, u32[]{:S(2)}, u32[]{:S(2)}) collective-permute-start(bf16[48,2304]{1,0:T(8,128)(2,1)S(1)} %get-tuple-element.86), channel_id=1, source_target_pairs={{0,8},{1,9},{2,10},{3,11},{4,20},{5,21},{6,22},{7,23},{8,0},{9,1},... | collective-permute-start | bytes 663560 | tf_op jit(solution)/shard_map/ppermute | solution.py:35
  126.4 10.1 %collective-permute-start.24 = (bf16[24,2304]{1,0:T(8,128)(2,1)S(1)}, bf16[24,2304]{1,0:T(8,128)(2,1)S(1)}, u32[]{:S(2)}, u32[]{:S(2)}) collective-permute-start(bf16[24,2304]{1,0:T(8,128)(2,1)S(1)} %get-tuple-element.92), channel_id=1, source_target_pairs={{0,1},{1,2},{2,3},{3,0},{4,5},{5,6},{6,7},{7,4},{8,9},{9,10},{10,1... | collective-permute-start | bytes 331784 | tf_op jit(solution)/shard_map/ppermute | solution.py:304
  127.9 10.8 %collective-permute-start.26 = (bf16[24,2304]{1,0:T(8,128)(2,1)S(1)}, bf16[24,2304]{1,0:T(8,128)(2,1)S(1)}, u32[]{:S(2)}, u32[]{:S(2)}) collective-permute-start(bf16[24,2304]{1,0:T(8,128)(2,1)S(1)} %get-tuple-element.91), channel_id=1, source_target_pairs={{0,2},{1,3},{2,0},{3,1},{4,6},{5,7},{6,4},{7,5},{8,10},{9,11},{10,... | collective-permute-start | bytes 331784 | tf_op jit(solution)/shard_map/ppermute | solution.py:304
  (27 other events, 98.0 us)

commit v4 on v3

--- a/solution.py
+++ b/solution.py
@@ -154,9 +154,12 @@
                 for h in range(2)
             ]
         )
+    for group in copies[:1]:
+        for copy in group:
+            copy.start()
     for copy in row_copies:
         copy.start()
-    for group in copies[:depth]:
+    for group in copies[1:depth]:
         for copy in group:
             copy.start()
 
@@ -195,7 +198,7 @@
     pieces = len(parts)
     size = parts[0].shape[0]
     _, units, width = weights[0].shape
-    tile, cols, depth = 256, 768, 3
+    tile, cols, depth = 256, 768, 4
     padded = -(-size // 16) * 16
     rows = pieces * padded
     anywhere = pl.BlockSpec(memory_space=pl.ANY)
@@ -336,7 +339,7 @@
     *partial, pool = ffn(home, stored + far, pool)
     early, *late = together([early] + late, pool)
     late = added(*late)
-    partial = together(partial, early, late)
+    partial = together(partial, early)
     home = added(*back(partial))
     late = [turn(late[(j - 1) * CAP : j * CAP], j) for j in range(1, planes)]
     pool = tie(pool, early)

time: 146 us -> 143 us (0.979)
  Pallas kernels: 53.2 us -> 51 us
    pallas_call x3, Pallas kernels: 45 us -> 42.9 us  [ffn(): pl.pallas_call(functools.partial(ffn_kernel, pieces, tile, cols, depth, p...]
    ppermute x34, waiting for transfers between devices: 20.4 us -> 18.5 us  [swap(): return lax.ppermute(x, AXES, pairs)]
  transfers between devices with their start and end apart: 40 -> 40, of which waited for: 12 -> 9; matrix products, arithmetic and copies ran while one was open for 3% -> 3% of each run, Pallas kernels for 32% -> 32%
where the time goes in v4:
time: 143 us
  starting transfers between devices  52.7 us (37%)
  Pallas kernels  51 us (36%)
  waiting for transfers between devices  29.3 us (20%)
  local copies, waits for them, and re-layouts  6.2 us (4%)
  other arithmetic  2.52 us (2%)
    pallas_call x3, Pallas kernels, ffn(): pl.pallas_call(functools.partial(ffn_kernel, pieces, tile, cols, depth, p...  42.9 us
    ppermute x34, starting transfers between devices, swap(): return lax.ppermute(x, AXES, pairs)  32.4 us
    ppermute x34, waiting for transfers between devices, swap(): return lax.ppermute(x, AXES, pairs)  18.5 us
    all_to_all x3, starting transfers between devices, exchange(): lax.all_to_all(rows, 'expert', split_axis=0, concat_axis=0, tiled=True)  14.8 us
    all_to_all x3, waiting for transfers between devices, exchange(): lax.all_to_all(rows, 'expert', split_axis=0, concat_axis=0, tiled=True)  8.45 us
    ppermute x3, starting transfers between devices, turn(): lax.ppermute(block, 'expert', [(i, (i + step) % planes) for i in range(pl...  5.58 us
    unnamed x23, local copies, waits for them, and re-layouts  5.38 us
    pallas_call x1, Pallas kernels, combine(): pl.pallas_call(functools.partial(combine_kernel, len(late) + 1), out_shap...  3.2 us
  transfers between devices with their start and end apart: 40, of which 9 were waited for; matrix products, arithmetic and copies ran while one was open for 3% of the time, Pallas kernels for 32%

profile of v4, /device:TPU:0, one launch (start us, length us, event | category | flops | bytes accessed | tf_op | source)
XLA Modules:
  0.0 142.7 jit_solution(14758883138327656124)
XLA Ops:
  0.6 2.8 %prep.1 = (bf16[96,2432]{1,0:T(8,128)(2,1)}, bf16[24,2432]{1,0:T(8,128)(2,1)}, bf16[96,2432]{1,0:T(8,128)(2,1)}, bf16[24,2432]{1,0:T(8,128)(2,1)}, f32[240,64]{1,0:T(8,128)}, /*index=5*/f32[8,2432]{1,0:T(8,128)}) custom-call(bf16[64,2304]{1,0:T(8,128)(2,1)} %tokens.3, s32[2,64]{1,0:T(2,128)} %bitcast.21, f32[2,64]{1,0:T(2,128)} %bitcast.22, s32[1,64]{1,0:T(1,128)} %bitcast.23), custom_call_target="tpu_custom_call" | custom-call | tf_op jit(solution)/shard_map/prep/pallas_call | solution.py:100
  3.9 1.8 %collective-permute-done = bf16[24,2432]{1,0:T(8,128)(2,1)S(1)} collective-permute-done((bf16[24,2432]{1,0:T(8,128)(2,1)}, bf16[24,2432]{1,0:T(8,128)(2,1)S(1)}, u32[]{:S(2)}, u32[]{:S(2)}) %collective-permute-start) | collective-permute-done | bytes 116768 | tf_op jit(solution)/shard_map/ppermute | solution.py:35
  6.6 6.1 %all-to-all-start = ((bf16[4,24,2432]{2,1,0:T(8,128)(2,1)}), bf16[4,24,2432]{2,1,0:T(8,128)(2,1)S(1)}, u32[]{:S(2)}, u32[]{:S(2)}) async-start(bf16[4,24,2432]{2,1,0:T(8,128)(2,1)} %bitcast.20), calls=%async_computation | async-start | bytes 933888 | tf_op jit(solution)/shard_map/all_to_all | solution.py:304
  15.2 4.6 %collective-permute-done.1.refs_1_ = bf16[48,2432]{1,0:T(8,128)(2,1)S(1)} collective-permute-done((bf16[48,2432]{1,0:T(8,128)(2,1)S(1)}, bf16[48,2432]{1,0:T(8,128)(2,1)S(1)}, u32[]{:S(2)}, u32[]{:S(2)}) %collective-permute-start.1) | collective-permute-done | bytes 233504 | tf_op jit(solution)/shard_map/ppermute | solution.py:35
  19.8 6.7 %all-to-all-done = bf16[4,24,2432]{2,1,0:T(8,128)(2,1)S(1)} async-done(((bf16[4,24,2432]{2,1,0:T(8,128)(2,1)}), bf16[4,24,2432]{2,1,0:T(8,128)(2,1)S(1)}, u32[]{:S(2)}, u32[]{:S(2)}) %all-to-all-start) | async-done | bytes 466976 | tf_op jit(solution)/shard_map/all_to_all | solution.py:304
  26.7 3.5 %all-to-all-start.1 = ((bf16[4,24,2432]{2,1,0:T(8,128)(2,1)}), bf16[4,24,2432]{2,1,0:T(8,128)(2,1)S(1)}, u32[]{:S(2)}, u32[]{:S(2)}) async-start(bf16[4,24,2432]{2,1,0:T(8,128)(2,1)} %bitcast.7), calls=%async_computation.1 | async-start | bytes 933888 | tf_op jit(solution)/shard_map/all_to_all | solution.py:304
  33.2 8.0 %collective-permute-done.2.refs_1_ = bf16[72,2432]{1,0:T(8,128)(2,1)S(1)} collective-permute-done((bf16[72,2432]{1,0:T(8,128)(2,1)S(1)}, bf16[72,2432]{1,0:T(8,128)(2,1)S(1)}, u32[]{:S(2)}, u32[]{:S(2)}) %collective-permute-start.2) | collective-permute-done | bytes 350240 | tf_op jit(solution)/shard_map/ppermute | solution.py:35
  41.3 1.7 %all-to-all-done.1 = bf16[4,24,2432]{2,1,0:T(8,128)(2,1)S(1)} async-done(((bf16[4,24,2432]{2,1,0:T(8,128)(2,1)}), bf16[4,24,2432]{2,1,0:T(8,128)(2,1)S(1)}, u32[]{:S(2)}, u32[]{:S(2)}) %all-to-all-start.1) | async-done | bytes 466976 | tf_op jit(solution)/shard_map/all_to_all | solution.py:304
  44.8 4.0 %collective-permute-done.4.refs_3_ = bf16[72,2432]{1,0:T(8,128)(2,1)S(1)} collective-permute-done((bf16[72,2432]{1,0:T(8,128)(2,1)S(1)}, bf16[72,2432]{1,0:T(8,128)(2,1)S(1)}, u32[]{:S(2)}, u32[]{:S(2)}) %collective-permute-start.4) | collective-permute-done | bytes 350240 | tf_op jit(solution)/shard_map/ppermute | solution.py:35
  48.8 2.5 %collective-permute-start.12 = (bf16[72,2432]{1,0:T(8,128)(2,1)S(1)}, bf16[72,2432]{1,0:T(8,128)(2,1)S(1)}, u32[]{:S(2)}, u32[]{:S(2)}) collective-permute-start(bf16[72,2432]{1,0:T(8,128)(2,1)S(1)} %fusion.refs_0_), channel_id=1, source_target_pairs={{0,8},{1,9},{2,10},{3,11},{4,20},{5,21},{6,22},{7,23},{8,0},{9,1},... | collective-permute-start | bytes 1050632 | tf_op jit(solution)/shard_map/ppermute | solution.py:35
  51.3 2.0 %collective-permute-start.13 = (bf16[72,2432]{1,0:T(8,128)(2,1)S(1)}, bf16[72,2432]{1,0:T(8,128)(2,1)S(1)}, u32[]{:S(2)}, u32[]{:S(2)}) collective-permute-start(bf16[72,2432]{1,0:T(8,128)(2,1)S(1)} %fusion.refs_0_), channel_id=1, source_target_pairs={{0,16},{1,17},{2,18},{3,19},{4,12},{5,13},{6,14},{7,15},{8,24},{9,... | collective-permute-start | bytes 1050632 | tf_op jit(solution)/shard_map/ppermute | solution.py:35
  54.2 15.1 %ffn.3 = (bf16[72,2304]{1,0:T(8,128)(2,1)S(1)}, bf16[72,2304]{1,0:T(8,128)(2,1)S(1)}, bf16[72,2304]{1,0:T(8,128)(2,1)S(1)}, bf16[72,2304]{1,0:T(8,128)(2,1)S(1)}, f32[8,2432]{1,0:T(8,128)S(1)}) custom-call(f32[8,2432]{1,0:T(8,128)S(1)} %copy-done.1, bf16[72,2432]{1,0:T(8,128)(2,1)S(1)} %fusion.1.refs_0_, ...), custom_call_target="tpu_custom_call" | custom-call | flops 8493465600 | bytes 26542080 | tf_op jit(solution)/shard_map/ffn/pallas_call | solution.py:206
  70.9 2.0 %collective-permute-start.10 = (bf16[72,2304]{1,0:T(8,128)(2,1)S(1)}, bf16[72,2304]{1,0:T(8,128)(2,1)S(1)}, u32[]{:S(2)}, u32[]{:S(2)}) collective-permute-start(bf16[72,2304]{1,0:T(8,128)(2,1)S(1)} %get-tuple-element.58), channel_id=1, source_target_pairs={{0,16},{1,17},{2,18},{3,19},{4,12},{5,13},{6,14},{7,15},{8,24},{9,... | collective-permute-start | bytes 995336 | tf_op jit(solution)/shard_map/ppermute | solution.py:35
  73.3 15.1 %ffn.4 = (bf16[72,2304]{1,0:T(8,128)(2,1)S(1)}, bf16[72,2304]{1,0:T(8,128)(2,1)S(1)}, bf16[72,2304]{1,0:T(8,128)(2,1)S(1)}, bf16[72,2304]{1,0:T(8,128)(2,1)S(1)}, f32[8,2432]{1,0:T(8,128)S(1)}) custom-call(f32[8,2432]{1,0:T(8,128)S(1)} %get-tuple-element.60.pool_in, bf16[72,2432]{1,0:T(8,128)(2,1)S(1)} %fusion.refs_0_, ...), custom_call_target="tpu_custom_call" | custom-call | flops 8493465600 | bytes 26542080 | tf_op jit(solution)/shard_map/ffn/pallas_call | solution.py:206
  89.9 2.2 %settle.1 = bf16[4,24,2304]{2,1,0:T(8,128)(2,1)} custom-call(bf16[72,2304]{1,0:T(8,128)(2,1)} %copy-done, bf16[72,2304]{1,0:T(8,128)(2,1)} %copy-done.4, bf16[72,2304]{1,0:T(8,128)(2,1)} %copy-done.5, bf16[72,2304]{1,0:T(8,128)(2,1)} %copy-done.6), custom_call_target="tpu_custom_call" | custom-call | tf_op jit(solution)/shard_map/settle/pallas_call | solution.py:243
  92.1 5.2 %all-to-all-start.2 = ((bf16[4,24,2304]{2,1,0:T(8,128)(2,1)}), bf16[4,24,2304]{2,1,0:T(8,128)(2,1)}, u32[]{:S(2)}, u32[]{:S(2)}) async-start(bf16[4,24,2304]{2,1,0:T(8,128)(2,1)} %settle.1), calls=%async_computation.2 | async-start | bytes 884736 | tf_op jit(solution)/shard_map/all_to_all | solution.py:304
  98.5 2.0 %collective-permute-start.16 = (bf16[72,2304]{1,0:T(8,128)(2,1)S(1)}, bf16[72,2304]{1,0:T(8,128)(2,1)S(1)}, u32[]{:S(2)}, u32[]{:S(2)}) collective-permute-start(bf16[72,2304]{1,0:T(8,128)(2,1)S(1)} %get-tuple-element.72), channel_id=1, source_target_pairs={{0,16},{1,17},{2,18},{3,19},{4,12},{5,13},{6,14},{7,15},{8,24},{9,... | collective-permute-start | bytes 995336 | tf_op jit(solution)/shard_map/ppermute | solution.py:35
  100.8 12.7 %ffn.5 = (bf16[48,2304]{1,0:T(8,128)(2,1)S(1)}, bf16[48,2304]{1,0:T(8,128)(2,1)S(1)}, bf16[48,2304]{1,0:T(8,128)(2,1)S(1)}, bf16[48,2304]{1,0:T(8,128)(2,1)S(1)}, f32[8,2432]{1,0:T(8,128)S(1)}) custom-call(f32[8,2432]{1,0:T(8,128)S(1)} %get-tuple-element.62.pool_in, bf16[48,2432]{1,0:T(8,128)(2,1)S(1)} %constant_dynamic-update-slice_fusion.refs_0_, ...), custom_call_target="tpu_custom_call" | custom-call | flops 5096079360 | bytes 26542080 | tf_op jit(solution)/shard_map/ffn/pallas_call | solution.py:206
  115.0 3.8 %collective-permute-start.32 = (f32[8,2432]{1,0:T(8,128)S(1)}, f32[8,2432]{1,0:T(8,128)S(1)}, u32[]{:S(2)}, u32[]{:S(2)}) collective-permute-start(f32[8,2432]{1,0:T(8,128)S(1)} %get-tuple-element.89), channel_id=1, source_target_pairs={{0,3},{1,2},{2,1},{3,0},{4,7},{5,6},{6,5},{7,4},{8,11},{9,10},{10,... | collective-permute-start | bytes 233480 | tf_op jit(solution)/shard_map/ppermute | solution.py:35
  119.5 2.6 %collective-permute-start.22 = (bf16[48,2304]{1,0:T(8,128)(2,1)S(1)}, bf16[48,2304]{1,0:T(8,128)(2,1)S(1)}, u32[]{:S(2)}, u32[]{:S(2)}) collective-permute-start(bf16[48,2304]{1,0:T(8,128)(2,1)S(1)} %get-tuple-element.84), channel_id=1, source_target_pairs={{0,24},{1,25},{2,26},{3,27},{4,28},{5,29},{6,30},{7,31},{8,16},{9,... | collective-permute-start | bytes 663560 | tf_op jit(solution)/shard_map/ppermute | solution.py:35
  126.0 2.9 %collective-permute-start.26 = (bf16[24,2304]{1,0:T(8,128)(2,1)S(1)}, bf16[24,2304]{1,0:T(8,128)(2,1)S(1)}, u32[]{:S(2)}, u32[]{:S(2)}) collective-permute-start(bf16[24,2304]{1,0:T(8,128)(2,1)S(1)} %get-tuple-element.91), channel_id=1, source_target_pairs={{0,2},{1,3},{2,0},{3,1},{4,6},{5,7},{6,4},{7,5},{8,10},{9,11},{10,... | collective-permute-start | bytes 331784 | tf_op jit(solution)/shard_map/ppermute | solution.py:307
  130.2 2.6 %collective-permute-start.36 = (f32[8,2432]{1,0:T(8,128)S(1)}, f32[8,2432]{1,0:T(8,128)S(1)}, u32[]{:S(2)}, u32[]{:S(2)}) collective-permute-start(f32[8,2432]{1,0:T(8,128)S(1)} %add.58), channel_id=1, source_target_pairs={{0,24},{1,25},{2,26},{3,27},{4,28},{5,29},{6,30},{7,31},{8,16},{9,... | collective-permute-start | bytes 233480 | tf_op jit(solution)/shard_map/ppermute | solution.py:35
  134.5 2.3 %collective-permute-done.26 = bf16[24,2304]{1,0:T(8,128)(2,1)S(1)} collective-permute-done((bf16[24,2304]{1,0:T(8,128)(2,1)S(1)}, bf16[24,2304]{1,0:T(8,128)(2,1)S(1)}, u32[]{:S(2)}, u32[]{:S(2)}) %collective-permute-start.26) | collective-permute-done | bytes 110624 | tf_op jit(solution)/shard_map/ppermute | solution.py:307
  139.5 3.2 %combine.1 = bf16[64,2304]{1,0:T(8,128)(2,1)} custom-call(bf16[64,2304]{1,0:T(8,128)(2,1)} %tokens.3, f32[240,64]{1,0:T(8,128)} %get-tuple-element.46.weights, bf16[96,2304]{1,0:T(8,128)(2,1)} %bitcast.9.early, bf16[24,2304]{1,0:T(8,128)(2,1)} %get-tuple-element.94.home, bf16[24,2304]{1,0:T(8,128)(2,1)} %copy-done.10, bf16[24,2304]{1,0:T(8,128)(2,1)} %copy-done.7, ...), custom_call_target="tpu_custom_call" | custom-call | tf_op jit(solution)/shard_map/combine/pallas_call | solution.py:272
  (97 shorter events, 26.5 us)
Async XLA Ops:
  5.8 43.0 %collective-permute-start.6 = (bf16[2,960,2304]{2,1,0:T(8,128)(2,1)}, bf16[2,960,2304]{2,1,0:T(8,128)(2,1)}, u32[]{:S(2)}, u32[]{:S(2)}) collective-permute-start(bf16[2,960,2304]{2,1,0:T(8,128)(2,1)} %bitcast.10), channel_id=1, source_target_pairs={{0,4},{1,5},{2,6},{3,7},{4,0},{5,1},{6,2},{7,3},{8,12},{9,13},{10,... | collective-permute-start | bytes 26542088 | tf_op jit(solution)/shard_map/ppermute | solution.py:35
  6.1 45.1 %collective-permute-start.7 = (bf16[2,960,2304]{2,1,0:T(8,128)(2,1)}, bf16[2,960,2304]{2,1,0:T(8,128)(2,1)}, u32[]{:S(2)}, u32[]{:S(2)}) collective-permute-start(bf16[2,960,2304]{2,1,0:T(8,128)(2,1)} %bitcast.14), channel_id=1, source_target_pairs={{0,4},{1,5},{2,6},{3,7},{4,0},{5,1},{6,2},{7,3},{8,12},{9,13},{10,... | collective-permute-start | bytes 26542088 | tf_op jit(solution)/shard_map/ppermute | solution.py:35
  6.3 47.0 %collective-permute-start.8 = (bf16[2,960,2304]{2,1,0:T(8,128)(2,1)}, bf16[2,960,2304]{2,1,0:T(8,128)(2,1)}, u32[]{:S(2)}, u32[]{:S(2)}) collective-permute-start(bf16[2,960,2304]{2,1,0:T(8,128)(2,1)} %refs_6_.5), channel_id=1, source_target_pairs={{0,4},{1,5},{2,6},{3,7},{4,0},{5,1},{6,2},{7,3},{8,12},{9,13},{10,... | collective-permute-start | bytes 26542088 | tf_op jit(solution)/shard_map/ppermute | solution.py:35
  6.6 19.9 %all-to-all-start = ((bf16[4,24,2432]{2,1,0:T(8,128)(2,1)}), bf16[4,24,2432]{2,1,0:T(8,128)(2,1)S(1)}, u32[]{:S(2)}, u32[]{:S(2)}) async-start(bf16[4,24,2432]{2,1,0:T(8,128)(2,1)} %bitcast.20), calls=%async_computation | async-start | bytes 933888 | tf_op jit(solution)/shard_map/all_to_all | solution.py:304
  26.7 16.4 %all-to-all-start.1 = ((bf16[4,24,2432]{2,1,0:T(8,128)(2,1)}), bf16[4,24,2432]{2,1,0:T(8,128)(2,1)S(1)}, u32[]{:S(2)}, u32[]{:S(2)}) async-start(bf16[4,24,2432]{2,1,0:T(8,128)(2,1)} %bitcast.7), calls=%async_computation.1 | async-start | bytes 933888 | tf_op jit(solution)/shard_map/all_to_all | solution.py:304
  30.1 11.1 %collective-permute-start.2 = (bf16[72,2432]{1,0:T(8,128)(2,1)S(1)}, bf16[72,2432]{1,0:T(8,128)(2,1)S(1)}, u32[]{:S(2)}, u32[]{:S(2)}) collective-permute-start(bf16[72,2432]{1,0:T(8,128)(2,1)S(1)} %fusion.1.refs_0_), channel_id=1, source_target_pairs={{0,8},{1,9},{2,10},{3,11},{4,20},{5,21},{6,22},{7,23},{8,0},{9,1},... | collective-permute-start | bytes 1050632 | tf_op jit(solution)/shard_map/ppermute | solution.py:35
  31.7 11.5 %collective-permute-start.3 = (bf16[72,2432]{1,0:T(8,128)(2,1)S(1)}, bf16[72,2432]{1,0:T(8,128)(2,1)S(1)}, u32[]{:S(2)}, u32[]{:S(2)}) collective-permute-start(bf16[72,2432]{1,0:T(8,128)(2,1)S(1)} %fusion.1.refs_0_), channel_id=1, source_target_pairs={{0,16},{1,17},{2,18},{3,19},{4,12},{5,13},{6,14},{7,15},{8,24},{9,... | collective-permute-start | bytes 1050632 | tf_op jit(solution)/shard_map/ppermute | solution.py:35
  43.2 57.6 %collective-permute-start.18 = (bf16[48,2432]{1,0:T(8,128)(2,1)S(1)}, bf16[48,2432]{1,0:T(8,128)(2,1)S(1)}, u32[]{:S(2)}, u32[]{:S(2)}) collective-permute-start(bf16[48,2432]{1,0:T(8,128)(2,1)S(1)} %constant_dynamic-update-slice_fusion.refs_0_), channel_id=1, source_target_pairs={{0,16},{1,17},{2,18},{3,19},{4,12},{5,13},{6,14},{7,15},{8,24},{9,... | collective-permute-start | bytes 700424 | tf_op jit(solution)/shard_map/ppermute | solution.py:35
  48.8 52.0 %collective-permute-start.19 = (bf16[48,2432]{1,0:T(8,128)(2,1)S(1)}, bf16[48,2432]{1,0:T(8,128)(2,1)S(1)}, u32[]{:S(2)}, u32[]{:S(2)}) collective-permute-start(bf16[48,2432]{1,0:T(8,128)(2,1)S(1)} %collective-permute-done.1.refs_1_), channel_id=1, source_target_pairs={{0,16},{1,17},{2,18},{3,19},{4,12},{5,13},{6,14},{7,15},{8,24},{9,... | collective-permute-start | bytes 700424 | tf_op jit(solution)/shard_map/ppermute | solution.py:35
  48.8 20.5 %collective-permute-start.12 = (bf16[72,2432]{1,0:T(8,128)(2,1)S(1)}, bf16[72,2432]{1,0:T(8,128)(2,1)S(1)}, u32[]{:S(2)}, u32[]{:S(2)}) collective-permute-start(bf16[72,2432]{1,0:T(8,128)(2,1)S(1)} %fusion.refs_0_), channel_id=1, source_target_pairs={{0,8},{1,9},{2,10},{3,11},{4,20},{5,21},{6,22},{7,23},{8,0},{9,1},... | collective-permute-start | bytes 1050632 | tf_op jit(solution)/shard_map/ppermute | solution.py:35
  51.3 19.6 %collective-permute-start.13 = (bf16[72,2432]{1,0:T(8,128)(2,1)S(1)}, bf16[72,2432]{1,0:T(8,128)(2,1)S(1)}, u32[]{:S(2)}, u32[]{:S(2)}) collective-permute-start(bf16[72,2432]{1,0:T(8,128)(2,1)S(1)} %fusion.refs_0_), channel_id=1, source_target_pairs={{0,16},{1,17},{2,18},{3,19},{4,12},{5,13},{6,14},{7,15},{8,24},{9,... | collective-permute-start | bytes 1050632 | tf_op jit(solution)/shard_map/ppermute | solution.py:35
  53.3 19.6 %collective-permute-start.14 = (bf16[72,2432]{1,0:T(8,128)(2,1)S(1)}, bf16[72,2432]{1,0:T(8,128)(2,1)S(1)}, u32[]{:S(2)}, u32[]{:S(2)}) collective-permute-start(bf16[72,2432]{1,0:T(8,128)(2,1)S(1)} %fusion.refs_0_), channel_id=1, source_target_pairs={{0,24},{1,25},{2,26},{3,27},{4,28},{5,29},{6,30},{7,31},{8,16},{9,... | collective-permute-start | bytes 1050632 | tf_op jit(solution)/shard_map/ppermute | solution.py:35
  69.3 19.1 %collective-permute-start.9 = (bf16[72,2304]{1,0:T(8,128)(2,1)S(1)}, bf16[72,2304]{1,0:T(8,128)(2,1)S(1)}, u32[]{:S(2)}, u32[]{:S(2)}) collective-permute-start(bf16[72,2304]{1,0:T(8,128)(2,1)S(1)} %get-tuple-element.57), channel_id=1, source_target_pairs={{0,8},{1,9},{2,10},{3,11},{4,20},{5,21},{6,22},{7,23},{8,0},{9,1},... | collective-permute-start | bytes 995336 | tf_op jit(solution)/shard_map/ppermute | solution.py:35
  70.9 17.5 %collective-permute-start.10 = (bf16[72,2304]{1,0:T(8,128)(2,1)S(1)}, bf16[72,2304]{1,0:T(8,128)(2,1)S(1)}, u32[]{:S(2)}, u32[]{:S(2)}) collective-permute-start(bf16[72,2304]{1,0:T(8,128)(2,1)S(1)} %get-tuple-element.58), channel_id=1, source_target_pairs={{0,16},{1,17},{2,18},{3,19},{4,12},{5,13},{6,14},{7,15},{8,24},{9,... | collective-permute-start | bytes 995336 | tf_op jit(solution)/shard_map/ppermute | solution.py:35
  72.8 15.6 %collective-permute-start.11 = (bf16[72,2304]{1,0:T(8,128)(2,1)S(1)}, bf16[72,2304]{1,0:T(8,128)(2,1)S(1)}, u32[]{:S(2)}, u32[]{:S(2)}) collective-permute-start(bf16[72,2304]{1,0:T(8,128)(2,1)S(1)} %get-tuple-element.59), channel_id=1, source_target_pairs={{0,24},{1,25},{2,26},{3,27},{4,28},{5,29},{6,30},{7,31},{8,16},{9,... | collective-permute-start | bytes 995336 | tf_op jit(solution)/shard_map/ppermute | solution.py:35
  92.1 22.9 %all-to-all-start.2 = ((bf16[4,24,2304]{2,1,0:T(8,128)(2,1)}), bf16[4,24,2304]{2,1,0:T(8,128)(2,1)}, u32[]{:S(2)}, u32[]{:S(2)}) async-start(bf16[4,24,2304]{2,1,0:T(8,128)(2,1)} %settle.1), calls=%async_computation.2 | async-start | bytes 884736 | tf_op jit(solution)/shard_map/all_to_all | solution.py:304
  97.3 16.2 %collective-permute-start.15 = (bf16[72,2304]{1,0:T(8,128)(2,1)S(1)}, bf16[72,2304]{1,0:T(8,128)(2,1)S(1)}, u32[]{:S(2)}, u32[]{:S(2)}) collective-permute-start(bf16[72,2304]{1,0:T(8,128)(2,1)S(1)} %get-tuple-element.71), channel_id=1, source_target_pairs={{0,8},{1,9},{2,10},{3,11},{4,20},{5,21},{6,22},{7,23},{8,0},{9,1},... | collective-permute-start | bytes 995336 | tf_op jit(solution)/shard_map/ppermute | solution.py:35
  98.5 15.0 %collective-permute-start.16 = (bf16[72,2304]{1,0:T(8,128)(2,1)S(1)}, bf16[72,2304]{1,0:T(8,128)(2,1)S(1)}, u32[]{:S(2)}, u32[]{:S(2)}) collective-permute-start(bf16[72,2304]{1,0:T(8,128)(2,1)S(1)} %get-tuple-element.72), channel_id=1, source_target_pairs={{0,16},{1,17},{2,18},{3,19},{4,12},{5,13},{6,14},{7,15},{8,24},{9,... | collective-permute-start | bytes 995336 | tf_op jit(solution)/shard_map/ppermute | solution.py:35
  100.5 14.5 %collective-permute-start.17 = (bf16[72,2304]{1,0:T(8,128)(2,1)S(1)}, bf16[72,2304]{1,0:T(8,128)(2,1)}, u32[]{:S(2)}, u32[]{:S(2)}) collective-permute-start(bf16[72,2304]{1,0:T(8,128)(2,1)S(1)} %get-tuple-element.73), channel_id=1, source_target_pairs={{0,24},{1,25},{2,26},{3,27},{4,28},{5,29},{6,30},{7,31},{8,16},{9,... | collective-permute-start | bytes 995336 | tf_op jit(solution)/shard_map/ppermute | solution.py:35
  115.0 8.5 %collective-permute-start.32 = (f32[8,2432]{1,0:T(8,128)S(1)}, f32[8,2432]{1,0:T(8,128)S(1)}, u32[]{:S(2)}, u32[]{:S(2)}) collective-permute-start(f32[8,2432]{1,0:T(8,128)S(1)} %get-tuple-element.89), channel_id=1, source_target_pairs={{0,3},{1,2},{2,1},{3,0},{4,7},{5,6},{6,5},{7,4},{8,11},{9,10},{10,... | collective-permute-start | bytes 233480 | tf_op jit(solution)/shard_map/ppermute | solution.py:35
  119.5 9.4 %collective-permute-start.22 = (bf16[48,2304]{1,0:T(8,128)(2,1)S(1)}, bf16[48,2304]{1,0:T(8,128)(2,1)S(1)}, u32[]{:S(2)}, u32[]{:S(2)}) collective-permute-start(bf16[48,2304]{1,0:T(8,128)(2,1)S(1)} %get-tuple-element.84), channel_id=1, source_target_pairs={{0,24},{1,25},{2,26},{3,27},{4,28},{5,29},{6,30},{7,31},{8,16},{9,... | collective-permute-start | bytes 663560 | tf_op jit(solution)/shard_map/ppermute | solution.py:35
  123.5 9.3 %collective-permute-start.20 = (bf16[48,2304]{1,0:T(8,128)(2,1)S(1)}, bf16[48,2304]{1,0:T(8,128)(2,1)S(1)}, u32[]{:S(2)}, u32[]{:S(2)}) collective-permute-start(bf16[48,2304]{1,0:T(8,128)(2,1)S(1)} %get-tuple-element.82), channel_id=1, source_target_pairs={{0,8},{1,9},{2,10},{3,11},{4,20},{5,21},{6,22},{7,23},{8,0},{9,1},... | collective-permute-start | bytes 663560 | tf_op jit(solution)/shard_map/ppermute | solution.py:35
  124.5 8.5 %collective-permute-start.24 = (bf16[24,2304]{1,0:T(8,128)(2,1)S(1)}, bf16[24,2304]{1,0:T(8,128)(2,1)S(1)}, u32[]{:S(2)}, u32[]{:S(2)}) collective-permute-start(bf16[24,2304]{1,0:T(8,128)(2,1)S(1)} %get-tuple-element.92), channel_id=1, source_target_pairs={{0,1},{1,2},{2,3},{3,0},{4,5},{5,6},{6,7},{7,4},{8,9},{9,10},{10,1... | collective-permute-start | bytes 331784 | tf_op jit(solution)/shard_map/ppermute | solution.py:307
  126.0 10.8 %collective-permute-start.26 = (bf16[24,2304]{1,0:T(8,128)(2,1)S(1)}, bf16[24,2304]{1,0:T(8,128)(2,1)S(1)}, u32[]{:S(2)}, u32[]{:S(2)}) collective-permute-start(bf16[24,2304]{1,0:T(8,128)(2,1)S(1)} %get-tuple-element.91), channel_id=1, source_target_pairs={{0,2},{1,3},{2,0},{3,1},{4,6},{5,7},{6,4},{7,5},{8,10},{9,11},{10,... | collective-permute-start | bytes 331784 | tf_op jit(solution)/shard_map/ppermute | solution.py:307
  (27 other events, 97.0 us)

commit v5 on v4

--- a/solution.py
+++ b/solution.py
@@ -11,7 +11,7 @@
 TOP = 2
 CAP = 24
 LANES = 128
-VMEM_LIMIT = 48 << 20
+VMEM_LIMIT = 50 << 20
 AXES = ("dp", "tensor", "expert")
 
 

time: 143 us -> 143 us (level)
  no operation moved by 1% of the time
where the time goes in v5:
time: 143 us
  starting transfers between devices  52.7 us (37%)
  Pallas kernels  51 us (36%)
  waiting for transfers between devices  29.3 us (20%)
  local copies, waits for them, and re-layouts  6.2 us (4%)
  other arithmetic  2.52 us (2%)
    pallas_call x3, Pallas kernels, ffn(): pl.pallas_call(functools.partial(ffn_kernel, pieces, tile, cols, depth, p...  42.9 us
    ppermute x34, starting transfers between devices, swap(): return lax.ppermute(x, AXES, pairs)  32.4 us
    ppermute x34, waiting for transfers between devices, swap(): return lax.ppermute(x, AXES, pairs)  18.5 us
    all_to_all x3, starting transfers between devices, exchange(): lax.all_to_all(rows, 'expert', split_axis=0, concat_axis=0, tiled=True)  14.8 us
    all_to_all x3, waiting for transfers between devices, exchange(): lax.all_to_all(rows, 'expert', split_axis=0, concat_axis=0, tiled=True)  8.45 us
    ppermute x3, starting transfers between devices, turn(): lax.ppermute(block, 'expert', [(i, (i + step) % planes) for i in range(pl...  5.58 us
    unnamed x23, local copies, waits for them, and re-layouts  5.38 us
    pallas_call x1, Pallas kernels, combine(): pl.pallas_call(functools.partial(combine_kernel, len(late) + 1), out_shap...  3.2 us
  transfers between devices with their start and end apart: 40, of which 9 were waited for; matrix products, arithmetic and copies ran while one was open for 3% of the time, Pallas kernels for 32%

profile of v5, /device:TPU:0, one launch (start us, length us, event | category | flops | bytes accessed | tf_op | source)
XLA Modules:
  0.0 142.7 jit_solution(13711680551463295977)
XLA Ops:
  0.6 2.8 %prep.1 = (bf16[96,2432]{1,0:T(8,128)(2,1)}, bf16[24,2432]{1,0:T(8,128)(2,1)}, bf16[96,2432]{1,0:T(8,128)(2,1)}, bf16[24,2432]{1,0:T(8,128)(2,1)}, f32[240,64]{1,0:T(8,128)}, /*index=5*/f32[8,2432]{1,0:T(8,128)}) custom-call(bf16[64,2304]{1,0:T(8,128)(2,1)} %tokens.3, s32[2,64]{1,0:T(2,128)} %bitcast.21, f32[2,64]{1,0:T(2,128)} %bitcast.22, s32[1,64]{1,0:T(1,128)} %bitcast.23), custom_call_target="tpu_custom_call" | custom-call | tf_op jit(solution)/shard_map/prep/pallas_call | solution.py:100
  3.9 1.8 %collective-permute-done = bf16[24,2432]{1,0:T(8,128)(2,1)S(1)} collective-permute-done((bf16[24,2432]{1,0:T(8,128)(2,1)}, bf16[24,2432]{1,0:T(8,128)(2,1)S(1)}, u32[]{:S(2)}, u32[]{:S(2)}) %collective-permute-start) | collective-permute-done | bytes 116768 | tf_op jit(solution)/shard_map/ppermute | solution.py:35
  6.6 6.1 %all-to-all-start = ((bf16[4,24,2432]{2,1,0:T(8,128)(2,1)}), bf16[4,24,2432]{2,1,0:T(8,128)(2,1)S(1)}, u32[]{:S(2)}, u32[]{:S(2)}) async-start(bf16[4,24,2432]{2,1,0:T(8,128)(2,1)} %bitcast.20), calls=%async_computation | async-start | bytes 933888 | tf_op jit(solution)/shard_map/all_to_all | solution.py:304
  15.2 4.6 %collective-permute-done.1.refs_1_ = bf16[48,2432]{1,0:T(8,128)(2,1)S(1)} collective-permute-done((bf16[48,2432]{1,0:T(8,128)(2,1)S(1)}, bf16[48,2432]{1,0:T(8,128)(2,1)S(1)}, u32[]{:S(2)}, u32[]{:S(2)}) %collective-permute-start.1) | collective-permute-done | bytes 233504 | tf_op jit(solution)/shard_map/ppermute | solution.py:35
  19.8 6.7 %all-to-all-done = bf16[4,24,2432]{2,1,0:T(8,128)(2,1)S(1)} async-done(((bf16[4,24,2432]{2,1,0:T(8,128)(2,1)}), bf16[4,24,2432]{2,1,0:T(8,128)(2,1)S(1)}, u32[]{:S(2)}, u32[]{:S(2)}) %all-to-all-start) | async-done | bytes 466976 | tf_op jit(solution)/shard_map/all_to_all | solution.py:304
  26.7 3.5 %all-to-all-start.1 = ((bf16[4,24,2432]{2,1,0:T(8,128)(2,1)}), bf16[4,24,2432]{2,1,0:T(8,128)(2,1)S(1)}, u32[]{:S(2)}, u32[]{:S(2)}) async-start(bf16[4,24,2432]{2,1,0:T(8,128)(2,1)} %bitcast.7), calls=%async_computation.1 | async-start | bytes 933888 | tf_op jit(solution)/shard_map/all_to_all | solution.py:304
  33.2 8.0 %collective-permute-done.2.refs_1_ = bf16[72,2432]{1,0:T(8,128)(2,1)S(1)} collective-permute-done((bf16[72,2432]{1,0:T(8,128)(2,1)S(1)}, bf16[72,2432]{1,0:T(8,128)(2,1)S(1)}, u32[]{:S(2)}, u32[]{:S(2)}) %collective-permute-start.2) | collective-permute-done | bytes 350240 | tf_op jit(solution)/shard_map/ppermute | solution.py:35
  41.3 1.7 %all-to-all-done.1 = bf16[4,24,2432]{2,1,0:T(8,128)(2,1)S(1)} async-done(((bf16[4,24,2432]{2,1,0:T(8,128)(2,1)}), bf16[4,24,2432]{2,1,0:T(8,128)(2,1)S(1)}, u32[]{:S(2)}, u32[]{:S(2)}) %all-to-all-start.1) | async-done | bytes 466976 | tf_op jit(solution)/shard_map/all_to_all | solution.py:304
  44.8 4.0 %collective-permute-done.4.refs_3_ = bf16[72,2432]{1,0:T(8,128)(2,1)S(1)} collective-permute-done((bf16[72,2432]{1,0:T(8,128)(2,1)S(1)}, bf16[72,2432]{1,0:T(8,128)(2,1)S(1)}, u32[]{:S(2)}, u32[]{:S(2)}) %collective-permute-start.4) | collective-permute-done | bytes 350240 | tf_op jit(solution)/shard_map/ppermute | solution.py:35
  48.8 2.5 %collective-permute-start.12 = (bf16[72,2432]{1,0:T(8,128)(2,1)S(1)}, bf16[72,2432]{1,0:T(8,128)(2,1)S(1)}, u32[]{:S(2)}, u32[]{:S(2)}) collective-permute-start(bf16[72,2432]{1,0:T(8,128)(2,1)S(1)} %fusion.refs_0_), channel_id=1, source_target_pairs={{0,8},{1,9},{2,10},{3,11},{4,20},{5,21},{6,22},{7,23},{8,0},{9,1},... | collective-permute-start | bytes 1050632 | tf_op jit(solution)/shard_map/ppermute | solution.py:35
  51.3 2.0 %collective-permute-start.13 = (bf16[72,2432]{1,0:T(8,128)(2,1)S(1)}, bf16[72,2432]{1,0:T(8,128)(2,1)S(1)}, u32[]{:S(2)}, u32[]{:S(2)}) collective-permute-start(bf16[72,2432]{1,0:T(8,128)(2,1)S(1)} %fusion.refs_0_), channel_id=1, source_target_pairs={{0,16},{1,17},{2,18},{3,19},{4,12},{5,13},{6,14},{7,15},{8,24},{9,... | collective-permute-start | bytes 1050632 | tf_op jit(solution)/shard_map/ppermute | solution.py:35
  54.2 15.1 %ffn.3 = (bf16[72,2304]{1,0:T(8,128)(2,1)S(1)}, bf16[72,2304]{1,0:T(8,128)(2,1)S(1)}, bf16[72,2304]{1,0:T(8,128)(2,1)S(1)}, bf16[72,2304]{1,0:T(8,128)(2,1)S(1)}, f32[8,2432]{1,0:T(8,128)S(1)}) custom-call(f32[8,2432]{1,0:T(8,128)S(1)} %copy-done.1, bf16[72,2432]{1,0:T(8,128)(2,1)S(1)} %fusion.1.refs_0_, ...), custom_call_target="tpu_custom_call" | custom-call | flops 8493465600 | bytes 26542080 | tf_op jit(solution)/shard_map/ffn/pallas_call | solution.py:206
  70.9 2.0 %collective-permute-start.10 = (bf16[72,2304]{1,0:T(8,128)(2,1)S(1)}, bf16[72,2304]{1,0:T(8,128)(2,1)S(1)}, u32[]{:S(2)}, u32[]{:S(2)}) collective-permute-start(bf16[72,2304]{1,0:T(8,128)(2,1)S(1)} %get-tuple-element.58), channel_id=1, source_target_pairs={{0,16},{1,17},{2,18},{3,19},{4,12},{5,13},{6,14},{7,15},{8,24},{9,... | collective-permute-start | bytes 995336 | tf_op jit(solution)/shard_map/ppermute | solution.py:35
  73.3 15.1 %ffn.4 = (bf16[72,2304]{1,0:T(8,128)(2,1)S(1)}, bf16[72,2304]{1,0:T(8,128)(2,1)S(1)}, bf16[72,2304]{1,0:T(8,128)(2,1)S(1)}, bf16[72,2304]{1,0:T(8,128)(2,1)S(1)}, f32[8,2432]{1,0:T(8,128)S(1)}) custom-call(f32[8,2432]{1,0:T(8,128)S(1)} %get-tuple-element.60.pool_in, bf16[72,2432]{1,0:T(8,128)(2,1)S(1)} %fusion.refs_0_, ...), custom_call_target="tpu_custom_call" | custom-call | flops 8493465600 | bytes 26542080 | tf_op jit(solution)/shard_map/ffn/pallas_call | solution.py:206
  89.9 2.2 %settle.1 = bf16[4,24,2304]{2,1,0:T(8,128)(2,1)} custom-call(bf16[72,2304]{1,0:T(8,128)(2,1)} %copy-done, bf16[72,2304]{1,0:T(8,128)(2,1)} %copy-done.4, bf16[72,2304]{1,0:T(8,128)(2,1)} %copy-done.5, bf16[72,2304]{1,0:T(8,128)(2,1)} %copy-done.6), custom_call_target="tpu_custom_call" | custom-call | tf_op jit(solution)/shard_map/settle/pallas_call | solution.py:243
  92.1 5.2 %all-to-all-start.2 = ((bf16[4,24,2304]{2,1,0:T(8,128)(2,1)}), bf16[4,24,2304]{2,1,0:T(8,128)(2,1)}, u32[]{:S(2)}, u32[]{:S(2)}) async-start(bf16[4,24,2304]{2,1,0:T(8,128)(2,1)} %settle.1), calls=%async_computation.2 | async-start | bytes 884736 | tf_op jit(solution)/shard_map/all_to_all | solution.py:304
  98.5 2.0 %collective-permute-start.16 = (bf16[72,2304]{1,0:T(8,128)(2,1)S(1)}, bf16[72,2304]{1,0:T(8,128)(2,1)S(1)}, u32[]{:S(2)}, u32[]{:S(2)}) collective-permute-start(bf16[72,2304]{1,0:T(8,128)(2,1)S(1)} %get-tuple-element.72), channel_id=1, source_target_pairs={{0,16},{1,17},{2,18},{3,19},{4,12},{5,13},{6,14},{7,15},{8,24},{9,... | collective-permute-start | bytes 995336 | tf_op jit(solution)/shard_map/ppermute | solution.py:35
  100.8 12.7 %ffn.5 = (bf16[48,2304]{1,0:T(8,128)(2,1)S(1)}, bf16[48,2304]{1,0:T(8,128)(2,1)S(1)}, bf16[48,2304]{1,0:T(8,128)(2,1)S(1)}, bf16[48,2304]{1,0:T(8,128)(2,1)S(1)}, f32[8,2432]{1,0:T(8,128)S(1)}) custom-call(f32[8,2432]{1,0:T(8,128)S(1)} %get-tuple-element.62.pool_in, bf16[48,2432]{1,0:T(8,128)(2,1)S(1)} %constant_dynamic-update-slice_fusion.refs_0_, ...), custom_call_target="tpu_custom_call" | custom-call | flops 5096079360 | bytes 26542080 | tf_op jit(solution)/shard_map/ffn/pallas_call | solution.py:206
  115.0 3.8 %collective-permute-start.32 = (f32[8,2432]{1,0:T(8,128)S(1)}, f32[8,2432]{1,0:T(8,128)S(1)}, u32[]{:S(2)}, u32[]{:S(2)}) collective-permute-start(f32[8,2432]{1,0:T(8,128)S(1)} %get-tuple-element.89), channel_id=1, source_target_pairs={{0,3},{1,2},{2,1},{3,0},{4,7},{5,6},{6,5},{7,4},{8,11},{9,10},{10,... | collective-permute-start | bytes 233480 | tf_op jit(solution)/shard_map/ppermute | solution.py:35
  119.5 2.6 %collective-permute-start.22 = (bf16[48,2304]{1,0:T(8,128)(2,1)S(1)}, bf16[48,2304]{1,0:T(8,128)(2,1)S(1)}, u32[]{:S(2)}, u32[]{:S(2)}) collective-permute-start(bf16[48,2304]{1,0:T(8,128)(2,1)S(1)} %get-tuple-element.84), channel_id=1, source_target_pairs={{0,24},{1,25},{2,26},{3,27},{4,28},{5,29},{6,30},{7,31},{8,16},{9,... | collective-permute-start | bytes 663560 | tf_op jit(solution)/shard_map/ppermute | solution.py:35
  126.0 2.9 %collective-permute-start.26 = (bf16[24,2304]{1,0:T(8,128)(2,1)S(1)}, bf16[24,2304]{1,0:T(8,128)(2,1)S(1)}, u32[]{:S(2)}, u32[]{:S(2)}) collective-permute-start(bf16[24,2304]{1,0:T(8,128)(2,1)S(1)} %get-tuple-element.91), channel_id=1, source_target_pairs={{0,2},{1,3},{2,0},{3,1},{4,6},{5,7},{6,4},{7,5},{8,10},{9,11},{10,... | collective-permute-start | bytes 331784 | tf_op jit(solution)/shard_map/ppermute | solution.py:307
  130.2 2.6 %collective-permute-start.36 = (f32[8,2432]{1,0:T(8,128)S(1)}, f32[8,2432]{1,0:T(8,128)S(1)}, u32[]{:S(2)}, u32[]{:S(2)}) collective-permute-start(f32[8,2432]{1,0:T(8,128)S(1)} %add.58), channel_id=1, source_target_pairs={{0,24},{1,25},{2,26},{3,27},{4,28},{5,29},{6,30},{7,31},{8,16},{9,... | collective-permute-start | bytes 233480 | tf_op jit(solution)/shard_map/ppermute | solution.py:35
  134.5 2.3 %collective-permute-done.26 = bf16[24,2304]{1,0:T(8,128)(2,1)S(1)} collective-permute-done((bf16[24,2304]{1,0:T(8,128)(2,1)S(1)}, bf16[24,2304]{1,0:T(8,128)(2,1)S(1)}, u32[]{:S(2)}, u32[]{:S(2)}) %collective-permute-start.26) | collective-permute-done | bytes 110624 | tf_op jit(solution)/shard_map/ppermute | solution.py:307
  139.5 3.2 %combine.1 = bf16[64,2304]{1,0:T(8,128)(2,1)} custom-call(bf16[64,2304]{1,0:T(8,128)(2,1)} %tokens.3, f32[240,64]{1,0:T(8,128)} %get-tuple-element.46.weights, bf16[96,2304]{1,0:T(8,128)(2,1)} %bitcast.9.early, bf16[24,2304]{1,0:T(8,128)(2,1)} %get-tuple-element.94.home, bf16[24,2304]{1,0:T(8,128)(2,1)} %copy-done.10, bf16[24,2304]{1,0:T(8,128)(2,1)} %copy-done.7, ...), custom_call_target="tpu_custom_call" | custom-call | tf_op jit(solution)/shard_map/combine/pallas_call | solution.py:272
  (97 shorter events, 26.5 us)
Async XLA Ops:
  5.8 43.0 %collective-permute-start.6 = (bf16[2,960,2304]{2,1,0:T(8,128)(2,1)}, bf16[2,960,2304]{2,1,0:T(8,128)(2,1)}, u32[]{:S(2)}, u32[]{:S(2)}) collective-permute-start(bf16[2,960,2304]{2,1,0:T(8,128)(2,1)} %bitcast.10), channel_id=1, source_target_pairs={{0,4},{1,5},{2,6},{3,7},{4,0},{5,1},{6,2},{7,3},{8,12},{9,13},{10,... | collective-permute-start | bytes 26542088 | tf_op jit(solution)/shard_map/ppermute | solution.py:35
  6.1 45.1 %collective-permute-start.7 = (bf16[2,960,2304]{2,1,0:T(8,128)(2,1)}, bf16[2,960,2304]{2,1,0:T(8,128)(2,1)}, u32[]{:S(2)}, u32[]{:S(2)}) collective-permute-start(bf16[2,960,2304]{2,1,0:T(8,128)(2,1)} %bitcast.14), channel_id=1, source_target_pairs={{0,4},{1,5},{2,6},{3,7},{4,0},{5,1},{6,2},{7,3},{8,12},{9,13},{10,... | collective-permute-start | bytes 26542088 | tf_op jit(solution)/shard_map/ppermute | solution.py:35
  6.3 47.0 %collective-permute-start.8 = (bf16[2,960,2304]{2,1,0:T(8,128)(2,1)}, bf16[2,960,2304]{2,1,0:T(8,128)(2,1)}, u32[]{:S(2)}, u32[]{:S(2)}) collective-permute-start(bf16[2,960,2304]{2,1,0:T(8,128)(2,1)} %refs_6_.5), channel_id=1, source_target_pairs={{0,4},{1,5},{2,6},{3,7},{4,0},{5,1},{6,2},{7,3},{8,12},{9,13},{10,... | collective-permute-start | bytes 26542088 | tf_op jit(solution)/shard_map/ppermute | solution.py:35
  6.6 19.9 %all-to-all-start = ((bf16[4,24,2432]{2,1,0:T(8,128)(2,1)}), bf16[4,24,2432]{2,1,0:T(8,128)(2,1)S(1)}, u32[]{:S(2)}, u32[]{:S(2)}) async-start(bf16[4,24,2432]{2,1,0:T(8,128)(2,1)} %bitcast.20), calls=%async_computation | async-start | bytes 933888 | tf_op jit(solution)/shard_map/all_to_all | solution.py:304
  26.7 16.4 %all-to-all-start.1 = ((bf16[4,24,2432]{2,1,0:T(8,128)(2,1)}), bf16[4,24,2432]{2,1,0:T(8,128)(2,1)S(1)}, u32[]{:S(2)}, u32[]{:S(2)}) async-start(bf16[4,24,2432]{2,1,0:T(8,128)(2,1)} %bitcast.7), calls=%async_computation.1 | async-start | bytes 933888 | tf_op jit(solution)/shard_map/all_to_all | solution.py:304
  30.1 11.1 %collective-permute-start.2 = (bf16[72,2432]{1,0:T(8,128)(2,1)S(1)}, bf16[72,2432]{1,0:T(8,128)(2,1)S(1)}, u32[]{:S(2)}, u32[]{:S(2)}) collective-permute-start(bf16[72,2432]{1,0:T(8,128)(2,1)S(1)} %fusion.1.refs_0_), channel_id=1, source_target_pairs={{0,8},{1,9},{2,10},{3,11},{4,20},{5,21},{6,22},{7,23},{8,0},{9,1},... | collective-permute-start | bytes 1050632 | tf_op jit(solution)/shard_map/ppermute | solution.py:35
  31.7 11.5 %collective-permute-start.3 = (bf16[72,2432]{1,0:T(8,128)(2,1)S(1)}, bf16[72,2432]{1,0:T(8,128)(2,1)S(1)}, u32[]{:S(2)}, u32[]{:S(2)}) collective-permute-start(bf16[72,2432]{1,0:T(8,128)(2,1)S(1)} %fusion.1.refs_0_), channel_id=1, source_target_pairs={{0,16},{1,17},{2,18},{3,19},{4,12},{5,13},{6,14},{7,15},{8,24},{9,... | collective-permute-start | bytes 1050632 | tf_op jit(solution)/shard_map/ppermute | solution.py:35
  43.2 57.6 %collective-permute-start.18 = (bf16[48,2432]{1,0:T(8,128)(2,1)S(1)}, bf16[48,2432]{1,0:T(8,128)(2,1)S(1)}, u32[]{:S(2)}, u32[]{:S(2)}) collective-permute-start(bf16[48,2432]{1,0:T(8,128)(2,1)S(1)} %constant_dynamic-update-slice_fusion.refs_0_), channel_id=1, source_target_pairs={{0,16},{1,17},{2,18},{3,19},{4,12},{5,13},{6,14},{7,15},{8,24},{9,... | collective-permute-start | bytes 700424 | tf_op jit(solution)/shard_map/ppermute | solution.py:35
  48.8 52.0 %collective-permute-start.19 = (bf16[48,2432]{1,0:T(8,128)(2,1)S(1)}, bf16[48,2432]{1,0:T(8,128)(2,1)S(1)}, u32[]{:S(2)}, u32[]{:S(2)}) collective-permute-start(bf16[48,2432]{1,0:T(8,128)(2,1)S(1)} %collective-permute-done.1.refs_1_), channel_id=1, source_target_pairs={{0,16},{1,17},{2,18},{3,19},{4,12},{5,13},{6,14},{7,15},{8,24},{9,... | collective-permute-start | bytes 700424 | tf_op jit(solution)/shard_map/ppermute | solution.py:35
  48.8 20.5 %collective-permute-start.12 = (bf16[72,2432]{1,0:T(8,128)(2,1)S(1)}, bf16[72,2432]{1,0:T(8,128)(2,1)S(1)}, u32[]{:S(2)}, u32[]{:S(2)}) collective-permute-start(bf16[72,2432]{1,0:T(8,128)(2,1)S(1)} %fusion.refs_0_), channel_id=1, source_target_pairs={{0,8},{1,9},{2,10},{3,11},{4,20},{5,21},{6,22},{7,23},{8,0},{9,1},... | collective-permute-start | bytes 1050632 | tf_op jit(solution)/shard_map/ppermute | solution.py:35
  51.3 19.6 %collective-permute-start.13 = (bf16[72,2432]{1,0:T(8,128)(2,1)S(1)}, bf16[72,2432]{1,0:T(8,128)(2,1)S(1)}, u32[]{:S(2)}, u32[]{:S(2)}) collective-permute-start(bf16[72,2432]{1,0:T(8,128)(2,1)S(1)} %fusion.refs_0_), channel_id=1, source_target_pairs={{0,16},{1,17},{2,18},{3,19},{4,12},{5,13},{6,14},{7,15},{8,24},{9,... | collective-permute-start | bytes 1050632 | tf_op jit(solution)/shard_map/ppermute | solution.py:35
  53.3 19.6 %collective-permute-start.14 = (bf16[72,2432]{1,0:T(8,128)(2,1)S(1)}, bf16[72,2432]{1,0:T(8,128)(2,1)S(1)}, u32[]{:S(2)}, u32[]{:S(2)}) collective-permute-start(bf16[72,2432]{1,0:T(8,128)(2,1)S(1)} %fusion.refs_0_), channel_id=1, source_target_pairs={{0,24},{1,25},{2,26},{3,27},{4,28},{5,29},{6,30},{7,31},{8,16},{9,... | collective-permute-start | bytes 1050632 | tf_op jit(solution)/shard_map/ppermute | solution.py:35
  69.3 19.1 %collective-permute-start.9 = (bf16[72,2304]{1,0:T(8,128)(2,1)S(1)}, bf16[72,2304]{1,0:T(8,128)(2,1)S(1)}, u32[]{:S(2)}, u32[]{:S(2)}) collective-permute-start(bf16[72,2304]{1,0:T(8,128)(2,1)S(1)} %get-tuple-element.57), channel_id=1, source_target_pairs={{0,8},{1,9},{2,10},{3,11},{4,20},{5,21},{6,22},{7,23},{8,0},{9,1},... | collective-permute-start | bytes 995336 | tf_op jit(solution)/shard_map/ppermute | solution.py:35
  70.9 17.5 %collective-permute-start.10 = (bf16[72,2304]{1,0:T(8,128)(2,1)S(1)}, bf16[72,2304]{1,0:T(8,128)(2,1)S(1)}, u32[]{:S(2)}, u32[]{:S(2)}) collective-permute-start(bf16[72,2304]{1,0:T(8,128)(2,1)S(1)} %get-tuple-element.58), channel_id=1, source_target_pairs={{0,16},{1,17},{2,18},{3,19},{4,12},{5,13},{6,14},{7,15},{8,24},{9,... | collective-permute-start | bytes 995336 | tf_op jit(solution)/shard_map/ppermute | solution.py:35
  72.8 15.6 %collective-permute-start.11 = (bf16[72,2304]{1,0:T(8,128)(2,1)S(1)}, bf16[72,2304]{1,0:T(8,128)(2,1)S(1)}, u32[]{:S(2)}, u32[]{:S(2)}) collective-permute-start(bf16[72,2304]{1,0:T(8,128)(2,1)S(1)} %get-tuple-element.59), channel_id=1, source_target_pairs={{0,24},{1,25},{2,26},{3,27},{4,28},{5,29},{6,30},{7,31},{8,16},{9,... | collective-permute-start | bytes 995336 | tf_op jit(solution)/shard_map/ppermute | solution.py:35
  92.1 22.9 %all-to-all-start.2 = ((bf16[4,24,2304]{2,1,0:T(8,128)(2,1)}), bf16[4,24,2304]{2,1,0:T(8,128)(2,1)}, u32[]{:S(2)}, u32[]{:S(2)}) async-start(bf16[4,24,2304]{2,1,0:T(8,128)(2,1)} %settle.1), calls=%async_computation.2 | async-start | bytes 884736 | tf_op jit(solution)/shard_map/all_to_all | solution.py:304
  97.3 16.2 %collective-permute-start.15 = (bf16[72,2304]{1,0:T(8,128)(2,1)S(1)}, bf16[72,2304]{1,0:T(8,128)(2,1)S(1)}, u32[]{:S(2)}, u32[]{:S(2)}) collective-permute-start(bf16[72,2304]{1,0:T(8,128)(2,1)S(1)} %get-tuple-element.71), channel_id=1, source_target_pairs={{0,8},{1,9},{2,10},{3,11},{4,20},{5,21},{6,22},{7,23},{8,0},{9,1},... | collective-permute-start | bytes 995336 | tf_op jit(solution)/shard_map/ppermute | solution.py:35
  98.5 15.0 %collective-permute-start.16 = (bf16[72,2304]{1,0:T(8,128)(2,1)S(1)}, bf16[72,2304]{1,0:T(8,128)(2,1)S(1)}, u32[]{:S(2)}, u32[]{:S(2)}) collective-permute-start(bf16[72,2304]{1,0:T(8,128)(2,1)S(1)} %get-tuple-element.72), channel_id=1, source_target_pairs={{0,16},{1,17},{2,18},{3,19},{4,12},{5,13},{6,14},{7,15},{8,24},{9,... | collective-permute-start | bytes 995336 | tf_op jit(solution)/shard_map/ppermute | solution.py:35
  100.5 14.5 %collective-permute-start.17 = (bf16[72,2304]{1,0:T(8,128)(2,1)S(1)}, bf16[72,2304]{1,0:T(8,128)(2,1)}, u32[]{:S(2)}, u32[]{:S(2)}) collective-permute-start(bf16[72,2304]{1,0:T(8,128)(2,1)S(1)} %get-tuple-element.73), channel_id=1, source_target_pairs={{0,24},{1,25},{2,26},{3,27},{4,28},{5,29},{6,30},{7,31},{8,16},{9,... | collective-permute-start | bytes 995336 | tf_op jit(solution)/shard_map/ppermute | solution.py:35
  115.0 8.5 %collective-permute-start.32 = (f32[8,2432]{1,0:T(8,128)S(1)}, f32[8,2432]{1,0:T(8,128)S(1)}, u32[]{:S(2)}, u32[]{:S(2)}) collective-permute-start(f32[8,2432]{1,0:T(8,128)S(1)} %get-tuple-element.89), channel_id=1, source_target_pairs={{0,3},{1,2},{2,1},{3,0},{4,7},{5,6},{6,5},{7,4},{8,11},{9,10},{10,... | collective-permute-start | bytes 233480 | tf_op jit(solution)/shard_map/ppermute | solution.py:35
  119.5 9.4 %collective-permute-start.22 = (bf16[48,2304]{1,0:T(8,128)(2,1)S(1)}, bf16[48,2304]{1,0:T(8,128)(2,1)S(1)}, u32[]{:S(2)}, u32[]{:S(2)}) collective-permute-start(bf16[48,2304]{1,0:T(8,128)(2,1)S(1)} %get-tuple-element.84), channel_id=1, source_target_pairs={{0,24},{1,25},{2,26},{3,27},{4,28},{5,29},{6,30},{7,31},{8,16},{9,... | collective-permute-start | bytes 663560 | tf_op jit(solution)/shard_map/ppermute | solution.py:35
  123.5 9.3 %collective-permute-start.20 = (bf16[48,2304]{1,0:T(8,128)(2,1)S(1)}, bf16[48,2304]{1,0:T(8,128)(2,1)S(1)}, u32[]{:S(2)}, u32[]{:S(2)}) collective-permute-start(bf16[48,2304]{1,0:T(8,128)(2,1)S(1)} %get-tuple-element.82), channel_id=1, source_target_pairs={{0,8},{1,9},{2,10},{3,11},{4,20},{5,21},{6,22},{7,23},{8,0},{9,1},... | collective-permute-start | bytes 663560 | tf_op jit(solution)/shard_map/ppermute | solution.py:35
  124.5 8.5 %collective-permute-start.24 = (bf16[24,2304]{1,0:T(8,128)(2,1)S(1)}, bf16[24,2304]{1,0:T(8,128)(2,1)S(1)}, u32[]{:S(2)}, u32[]{:S(2)}) collective-permute-start(bf16[24,2304]{1,0:T(8,128)(2,1)S(1)} %get-tuple-element.92), channel_id=1, source_target_pairs={{0,1},{1,2},{2,3},{3,0},{4,5},{5,6},{6,7},{7,4},{8,9},{9,10},{10,1... | collective-permute-start | bytes 331784 | tf_op jit(solution)/shard_map/ppermute | solution.py:307
  126.0 10.8 %collective-permute-start.26 = (bf16[24,2304]{1,0:T(8,128)(2,1)S(1)}, bf16[24,2304]{1,0:T(8,128)(2,1)S(1)}, u32[]{:S(2)}, u32[]{:S(2)}) collective-permute-start(bf16[24,2304]{1,0:T(8,128)(2,1)S(1)} %get-tuple-element.91), channel_id=1, source_target_pairs={{0,2},{1,3},{2,0},{3,1},{4,6},{5,7},{6,4},{7,5},{8,10},{9,11},{10,... | collective-permute-start | bytes 331784 | tf_op jit(solution)/shard_map/ppermute | solution.py:307
  (27 other events, 97.0 us)
